TPU v7x, 256 devices: a whole 4x4x8 slice. The times are simulated.
256 devices in a mesh: ctx: 64 (over y, z, core), head: 4 (over x).
Axes of the slice: x: 4, y: 4, z: 8, core: 2. Of those that a mesh axis runs over, the one named last changes fastest.
Arguments:
- tokens: bfloat16 [8192, 2048], P('ctx'), may hold values from -6 to 6
- grad_out: bfloat16 [8192, 2048], P('ctx'), may hold values from -6 to 6
- expert_ids: int32 [8192, 8], P('ctx'), may hold values from 0 to 127, all different within a row; in each aligned block of 128 rows (0 to 127, 128 to 255, ...) at most 10 rows name the same one
- gate_probs: bfloat16 [8192, 8], P('ctx'), may hold values from 0.029907227 to 0.3984375
- w_gate: bfloat16 [128, 768, 2048], P('ctx', 'head'), may hold values from -0.125 to 0.125
- w_up: bfloat16 [128, 768, 2048], P('ctx', 'head'), may hold values from -0.125 to 0.125
- w_down: bfloat16 [128, 768, 2048], P('ctx', 'head'), may hold values from -0.21875 to 0.21875
- query_rows: bfloat16 [8192, 4096], P('ctx', 'head'), may hold values from -4.5 to 4.5, as said below
- key_rows: bfloat16 [8192, 512], P('ctx', 'head'), may hold values from -4.5 to 4.5, as said below
- value_rows: bfloat16 [8192, 512], P('ctx', 'head'), may hold values from -6 to 6
- attn_out: bfloat16 [8192, 4096], P('ctx', 'head'), may hold values from -6 to 6
- grad_attn: bfloat16 [8192, 4096], P('ctx', 'head'), may hold values from -6 to 6
- segment_ids: int32 [8192], replicated, may hold values from 0 to 63, never falling along the last dimension, each value on 1 to 384 neighbouring positions
Outputs:
- grad_tokens: bfloat16 [8192, 2048], P('ctx')
- grad_gate: bfloat16 [128, 768, 2048], P('ctx', 'head')
- grad_up: bfloat16 [128, 768, 2048], P('ctx', 'head')
- grad_down: bfloat16 [128, 768, 2048], P('ctx', 'head')
- grad_query: bfloat16 [8192, 4096], P('ctx', 'head')
- grad_key: bfloat16 [8192, 512], P('ctx', 'head')
- grad_value: bfloat16 [8192, 512], P('ctx', 'head')
Inputs may be any that keep to these rules, and one draw needn't show every extreme that they name: `expert_ids`: each row names different experts; among the 128 tokens of one index of ctx no expert is named more than 10 times, a bound that some block reaches. `segment_ids`: ids never fall; a document has at most 384 positions, and one has exactly that many. `query_rows`: entries stay within the range. `key_rows`: entries stay within the range.
All inputs are finite; a program needn't handle non-finite values.
Results may differ from a plain program's by a relative error of at most 0.0057.
Values may be sent and summed in bfloat16 or wider, within the bound.
No kernel may reach another device: no remote copies, remote signals or barrier semaphores. Data moves between devices by JAX's collectives and lax.ppermute only.
A program may use at most 128 MiB of HBM per device.

v0:
```python
import jax
import jax.numpy as jnp
from jax import lax
from jax.sharding import PartitionSpec as P

HQ = 32
KVH = 4
HD = 128
REACH = 3


def passed_along(block, axis, distance):
    devices = range(lax.axis_size(axis))
    route = [(i - distance, i) for i in devices if i - distance in devices]
    return lax.ppermute(block, axis, route)


def expert_backward(recv_rows, recv_grads, w_gate, w_up, w_down):
    gate_pre = jnp.einsum("secd,efd->secf", recv_rows, w_gate, preferred_element_type=jnp.float32)
    up_pre = jnp.einsum("secd,efd->secf", recv_rows, w_up, preferred_element_type=jnp.float32)
    sigmoid_gate = jax.nn.sigmoid(gate_pre)
    active = gate_pre * sigmoid_gate
    hidden = (active * up_pre).astype(jnp.bfloat16)
    hidden_grad = jnp.einsum(
        "secd,efd->secf", recv_grads, w_down, preferred_element_type=jnp.float32
    )
    gate_grad = (
        hidden_grad * up_pre * sigmoid_gate * (1.0 + gate_pre * (1.0 - sigmoid_gate))
    ).astype(jnp.bfloat16)
    up_grad = (hidden_grad * active).astype(jnp.bfloat16)
    back_rows = jnp.einsum(
        "secf,efd->secd", gate_grad, w_gate, preferred_element_type=jnp.float32
    ) + jnp.einsum("secf,efd->secd", up_grad, w_up, preferred_element_type=jnp.float32)
    grad_gate = jnp.einsum(
        "secf,secd->efd", gate_grad, recv_rows, preferred_element_type=jnp.float32
    ).astype(jnp.bfloat16)
    grad_up = jnp.einsum(
        "secf,secd->efd", up_grad, recv_rows, preferred_element_type=jnp.float32
    ).astype(jnp.bfloat16)
    grad_down = jnp.einsum(
        "secf,secd->efd", hidden, recv_grads, preferred_element_type=jnp.float32
    ).astype(jnp.bfloat16)
    return (back_rows, grad_gate, grad_up, grad_down)


def pair_total(returned, slot_index, tok_count, top_count):
    flat_rows = returned.reshape(-1, returned.shape[3])
    picked = flat_rows[slot_index]
    return jnp.sum(picked.reshape(tok_count, top_count, returned.shape[3]), axis=1)


def body(
    tokens,
    grad_out,
    expert_ids,
    gate_probs,
    w_gate,
    w_up,
    w_down,
    query_rows,
    key_rows,
    value_rows,
    attn_out,
    grad_attn,
    segment_ids,
):
    tok_count, width = tokens.shape
    top_count = expert_ids.shape[1]
    ctx_count = lax.axis_size("ctx")
    local_experts = w_gate.shape[0]
    total_experts = local_experts * ctx_count
    capacity = (5 * tok_count * top_count + 4 * total_experts - 1) // (4 * total_experts)
    pair_count = tok_count * top_count
    flat_expert = expert_ids.reshape(pair_count)
    onehot = (flat_expert[:, None] == jnp.arange(total_experts, dtype=jnp.int32)[None, :]).astype(
        jnp.int32
    )
    earlier = jnp.cumsum(onehot, axis=0) - onehot
    slot_rank = jnp.sum(earlier * onehot, axis=1)
    slot_index = flat_expert * capacity + slot_rank
    slot_pair = (
        jnp.full((total_experts * capacity,), pair_count, jnp.int32)
        .at[slot_index]
        .set(jnp.arange(pair_count, dtype=jnp.int32))
    )
    slot_token = slot_pair // top_count
    padded_tokens = jnp.concatenate([tokens, jnp.zeros((1, width), tokens.dtype)], axis=0)
    padded_grad = jnp.concatenate([grad_out, jnp.zeros((1, width), grad_out.dtype)], axis=0)
    padded_probs = jnp.concatenate(
        [gate_probs.reshape(pair_count).astype(jnp.float32), jnp.zeros((1,), jnp.float32)]
    )
    buffer_shape = (ctx_count, local_experts, capacity, width)
    send_rows = padded_tokens[slot_token].reshape(buffer_shape)
    send_grads = (
        (padded_probs[slot_pair][:, None] * padded_grad[slot_token].astype(jnp.float32))
        .astype(jnp.bfloat16)
        .reshape(buffer_shape)
    )
    recv_rows, recv_grads = (
        lax.all_to_all(send_rows, "ctx", split_axis=0, concat_axis=0, tiled=True),
        lax.all_to_all(send_grads, "ctx", split_axis=0, concat_axis=0, tiled=True),
    )
    back_rows, grad_gate, grad_up, grad_down = expert_backward(
        recv_rows, recv_grads, w_gate, w_up, w_down
    )
    returned = lax.all_to_all(back_rows, "ctx", split_axis=0, concat_axis=0, tiled=True)
    summed = pair_total(returned, slot_index, tok_count, top_count)
    grad_tokens = lax.psum(summed, "head").astype(jnp.bfloat16)
    att_rows = query_rows.shape[0]
    kv_width = key_rows.shape[1]
    kv_local = kv_width // HD
    group_size = HQ // KVH
    window = (REACH + 1) * att_rows
    score_scale = HD ** (-0.5)
    ctx_index = lax.axis_index("ctx")
    key_blocks = []
    value_blocks = []
    for distance in range(REACH, 0, -1):
        far_key, far_value = passed_along((key_rows, value_rows), "ctx", distance)
        key_blocks.append(far_key)
        value_blocks.append(far_value)
    window_key = jnp.concatenate(key_blocks + [key_rows], axis=0).reshape(window, kv_local, HD)
    window_value = jnp.concatenate(value_blocks + [value_rows], axis=0).reshape(
        window, kv_local, HD
    )
    query_pos = ctx_index * att_rows + jnp.arange(att_rows, dtype=jnp.int32)
    key_pos = (ctx_index - REACH) * att_rows + jnp.arange(window, dtype=jnp.int32)
    padded_segment = jnp.concatenate([jnp.full((REACH * att_rows,), -1, jnp.int32), segment_ids])
    key_seg = lax.dynamic_slice_in_dim(padded_segment, ctx_index * att_rows, window, 0)
    query_seg = lax.dynamic_slice_in_dim(segment_ids, ctx_index * att_rows, att_rows, 0)
    visible = (key_pos[None, :] <= query_pos[:, None]) & (key_seg[None, :] == query_seg[:, None])
    query_heads = query_rows.reshape(att_rows, kv_local, group_size, HD)
    out_heads = attn_out.reshape(att_rows, kv_local, group_size, HD)
    grad_heads = grad_attn.reshape(att_rows, kv_local, group_size, HD)
    scores = (
        jnp.einsum("ajgd,tjd->jgat", query_heads, window_key, preferred_element_type=jnp.float32)
        * score_scale
    )
    row_peak = jnp.max(jnp.where(visible, scores, -jnp.inf), axis=-1, keepdims=True)
    weights_exp = jnp.exp(jnp.where(visible, scores - row_peak, -jnp.inf))
    probs = weights_exp / jnp.sum(weights_exp, axis=-1, keepdims=True)
    row_delta = jnp.einsum(
        "ajgd,ajgd->jga", grad_heads, out_heads, preferred_element_type=jnp.float32
    )
    prob_grad = jnp.einsum(
        "ajgd,tjd->jgat", grad_heads, window_value, preferred_element_type=jnp.float32
    )
    score_grad = (probs * (prob_grad - row_delta[..., None])).astype(jnp.bfloat16)
    probs_low = probs.astype(jnp.bfloat16)
    grad_query = (
        (
            score_scale
            * jnp.einsum(
                "jgat,tjd->ajgd", score_grad, window_key, preferred_element_type=jnp.float32
            )
        )
        .astype(jnp.bfloat16)
        .reshape(att_rows, -1)
    )
    key_terms = (
        score_scale
        * jnp.einsum("jgat,ajgd->tjd", score_grad, query_heads, preferred_element_type=jnp.float32)
    ).reshape(window, kv_width)
    value_terms = jnp.einsum(
        "jgat,ajgd->tjd", probs_low, grad_heads, preferred_element_type=jnp.float32
    ).reshape(window, kv_width)
    key_total = key_terms[REACH * att_rows :]
    value_total = value_terms[REACH * att_rows :]
    for distance in range(1, REACH + 1):
        offset = (REACH - distance) * att_rows
        got_key, got_value = passed_along(
            (key_terms[offset : offset + att_rows], value_terms[offset : offset + att_rows]),
            "ctx",
            -distance,
        )
        key_total = key_total + got_key
        value_total = value_total + got_value
    return (
        grad_tokens,
        grad_gate,
        grad_up,
        grad_down,
        grad_query,
        key_total.astype(jnp.bfloat16),
        value_total.astype(jnp.bfloat16),
    )


def solution(mesh):
    placed = (
        P("ctx", None),
        P("ctx", None),
        P("ctx", None),
        P("ctx", None),
        P("ctx", "head", None),
        P("ctx", "head", None),
        P("ctx", "head", None),
        P("ctx", "head"),
        P("ctx", "head"),
        P("ctx", "head"),
        P("ctx", "head"),
        P("ctx", "head"),
        P(),
    )
    return jax.shard_map(
        body,
        mesh=mesh,
        in_specs=placed,
        out_specs=(
            P("ctx", None),
            P("ctx", "head", None),
            P("ctx", "head", None),
            P("ctx", "head", None),
            P("ctx", "head"),
            P("ctx", "head"),
            P("ctx", "head"),
        ),
        check_vma=False,
    )
```

profile of v0, /device:TPU:48, one launch (start us, length us, event | category | flops | bytes accessed | tf_op | source)
XLA Modules:
  0.0 697.2 jit_solution(9661549551551122157)
XLA Ops:
  8.0 6.2 gather_fusion.2
  14.2 9.6 %reshape.169 = bf16[64,2,10,2048]{3,2,1,0:T(8,128)(2,1)} reshape(bf16[1280,2048]{1,0:T(8,128)(2,1)} %gather_fusion.2) | data formatting | bytes 10485760 | tf_op jit(solution)/shard_map/reshape | solution.py:93
  23.8 11.3 %copy.72 = bf16[64,2,10,2048]{3,1,2,0:T(2,128)(2,1)} copy(bf16[64,2,10,2048]{3,2,1,0:T(8,128)(2,1)} %reshape.169) | data formatting | bytes 10485760 | tf_op jit(solution)/shard_map/reshape | solution.py:93
  35.1 11.9 %all-to-all-start.1 = ((bf16[64,2,10,2048]{3,1,2,0:T(2,128)(2,1)}), bf16[64,2,10,2048]{3,1,2,0:T(2,128)(2,1)}, u32[]{:S(2)}, u32[]{:S(2)}) async-start(bf16[64,2,10,2048]{3,1,2,0:T(2,128)(2,1)} %copy.72), calls=%async_computation.1 | async-start | bytes 10485760 | tf_op jit(solution)/shard_map/all_to_all | solution.py:100
  47.3 7.1 %gather_fusion = f32[1280]{0:T(1024)S(1)} fusion(f32[1025]{0:T(1024)S(1)} %maximum_convert_fusion, s32[2048]{0:T(1024)S(1)} %get-tuple-element.48), kind=kCustom, calls=%fused_computation | custom fusion | bytes 15360 | tf_op jit(solution)/shard_map/gather | solution.py:95
  60.8 10.3 %reshape.178 = f32[64,2,10,2048]{3,2,1,0:T(8,128)} reshape(bf16[1280,2048]{1,0:T(8,128)(2,1)} %gather_fusion.1) | data formatting | bytes 15728640 | tf_op jit(solution)/shard_map/convert_element_type | solution.py:95
  71.1 6.5 multiply_convert_fusion
  77.6 12.7 %copy.70 = bf16[64,2,10,2048]{3,1,2,0:T(2,128)(2,1)} copy(bf16[64,2,10,2048]{3,2,1,0:T(8,128)(2,1)S(1)} %multiply_convert_fusion) | data formatting | bytes 10485760 | tf_op jit(solution)/shard_map/convert_element_type | solution.py:96
  90.4 73.3 %all-to-all-done.1 = bf16[64,2,10,2048]{3,1,2,0:T(2,128)(2,1)} async-done(((bf16[64,2,10,2048]{3,1,2,0:T(2,128)(2,1)}), bf16[64,2,10,2048]{3,1,2,0:T(2,128)(2,1)}, u32[]{:S(2)}, u32[]{:S(2)}) %all-to-all-start.1) | async-done | bytes 5242912 | tf_op jit(solution)/shard_map/all_to_all | solution.py:100
  163.6 7.9 %all-to-all-start = ((bf16[64,2,10,2048]{3,1,2,0:T(2,128)(2,1)}), bf16[64,2,10,2048]{3,1,2,0:T(2,128)(2,1)}, u32[]{:S(2)}, u32[]{:S(2)}) async-start(bf16[64,2,10,2048]{3,1,2,0:T(2,128)(2,1)} %copy.70), calls=%async_computation | async-start | bytes 10485760 | tf_op jit(solution)/shard_map/all_to_all | solution.py:101
  171.6 6.7 fusion.36
  178.3 6.6 fusion.31
  184.9 103.0 %all-to-all-done = bf16[64,2,10,2048]{3,1,2,0:T(2,128)(2,1)} async-done(((bf16[64,2,10,2048]{3,1,2,0:T(2,128)(2,1)}), bf16[64,2,10,2048]{3,1,2,0:T(2,128)(2,1)}, u32[]{:S(2)}, u32[]{:S(2)}) %all-to-all-start) | async-done | bytes 5242912 | tf_op jit(solution)/shard_map/all_to_all | solution.py:101
  288.0 7.2 %multiply_convert_fusion.2 = (bf16[64,2,10,192]{3,0,2,1:T(8,128)(2,1)S(1)}, bf16[64,2,10,192]{3,0,2,1:T(8,128)(2,1)S(1)}) fusion(f32[64,2,10,192]{3,0,2,1:T(8,128)} %fusion.36, f32[64,2,10,192]{3,0,2,1:T(8,128)} %fusion.31, bf16[2,192,2048]{2,1,0:T(8,128)(2,1)} %param.19, bf16[64,2,10,2048]{3,1,2,0:T(2,128)(2,1)} %all-to-all-done), kind=kOutput, calls=%fused_computation.44 | convolution fusion | flops 1009827840 | bytes 9764864 | tf_op jit(solution)/shard_map/secd,efd->secf/dot_general | solution.py:24
  298.7 13.0 %copy.75 = f32[64,2,10,2048]{3,1,2,0:T(2,128)} copy(f32[64,2,10,2048]{3,0,2,1:T(8,128)S(1)} %add_bitcast_fusion) | data formatting | bytes 20971520 | tf_op jit(solution)/shard_map/add | solution.py:31
  311.7 7.8 %all-to-all-start.2 = ((f32[64,2,10,2048]{3,1,2,0:T(2,128)}), f32[64,2,10,2048]{3,1,2,0:T(2,128)}, u32[]{:S(2)}, u32[]{:S(2)}) async-start(f32[64,2,10,2048]{3,1,2,0:T(2,128)} %copy.75), calls=%async_computation.2 | async-start | bytes 20971520 | tf_op jit(solution)/shard_map/all_to_all | solution.py:106
  335.7 213.0 %collective-permute-done.1 = bf16[128,128]{1,0:T(8,128)(2,1)S(1)} collective-permute-done((bf16[128,128]{1,0:T(8,128)(2,1)S(1)}, bf16[128,128]{1,0:T(8,128)(2,1)S(1)}, u32[]{:S(2)}, u32[]{:S(2)}) %collective-permute-start.1) | collective-permute-done | bytes 32800 | tf_op jit(solution)/shard_map/ppermute | solution.py:15
  580.5 9.9 %bitcast_convert_fusion.1 = bf16[2,192,2048]{2,1,0:T(8,128)(2,1)} fusion(bf16[64,2,10,192]{3,0,2,1:T(8,128)(2,1)S(1)} %copy-done.6, bf16[64,2,10,2048]{3,1,2,0:T(2,128)(2,1)} %all-to-all-done.1), kind=kOutput, calls=%fused_computation.21 | convolution fusion | flops 1007419392 | bytes 7307264 | tf_op jit(solution)/shard_map/secf,secd->efd/dot_general | solution.py:37
  590.4 10.2 %bitcast_convert_fusion.2 = bf16[2,192,2048]{2,1,0:T(8,128)(2,1)} fusion(bf16[64,2,10,192]{3,0,2,1:T(8,128)(2,1)S(1)} %copy-done.4, bf16[64,2,10,2048]{3,1,2,0:T(2,128)(2,1)} %all-to-all-done.1), kind=kOutput, calls=%fused_computation.22 | convolution fusion | flops 1007419392 | bytes 7307264 | tf_op jit(solution)/shard_map/secf,secd->efd/dot_general | solution.py:34
  600.6 10.1 %bitcast_convert_fusion = bf16[2,192,2048]{2,1,0:T(8,128)(2,1)} fusion(bf16[64,2,10,2048]{3,1,2,0:T(2,128)(2,1)} %all-to-all-done, f32[64,2,10,192]{3,0,2,1:T(8,128)S(1)} %copy-done.17, f32[64,2,10,192]{3,0,2,1:T(8,128)S(1)} %copy-done.16), kind=kOutput, calls=%fused_computation.20 | convolution fusion | flops 1008893952 | bytes 8781824 | tf_op jit(solution)/shard_map/secf,secd->efd/dot_general | solution.py:40
  610.7 19.9 %copy.76 = f32[64,2,10,2048]{3,2,1,0:T(8,128)} copy(f32[64,2,10,2048]{3,1,2,0:T(2,128)} %all-to-all-done.2) | data formatting | bytes 20971520 | tf_op jit(solution)/shard_map/all_to_all | solution.py:106
  630.7 13.9 %reshape.170 = f32[1280,2048]{1,0:T(8,128)} reshape(f32[64,2,10,2048]{3,2,1,0:T(8,128)} %copy.76) | data formatting | bytes 20971520 | tf_op jit(solution)/shard_map/reshape | solution.py:47
  644.6 13.0 %gather_fusion.3 = f32[1024,2048]{1,0:T(8,128)} fusion(f32[1280,2048]{1,0:T(8,128)} %reshape.170, s32[1024]{0:T(1024)S(1)} %broadcast_clamp_fusion), kind=kCustom, calls=%fused_computation.3 | custom fusion | bytes 16781312 | tf_op jit(solution)/shard_map/gather | solution.py:48
  663.1 33.7 %all-reduce.4 = bf16[128,2048]{1,0:T(8,128)(2,1)} all-reduce(f32[128,2048]{1,0:T(8,128)S(1)} %bitcast_reduce_fusion), channel_id=1, replica_groups=mesh['ctx'=64,'head'=4] {'head'}, use_global_device_ids=true, to_apply=%region_5.6 | all-reduce | flops 262144 | bytes 1572864 | tf_op jit(solution)/shard_map/psum | solution.py:108
  (109 shorter events, 70.6 us)
Async XLA Ops:
  0.6 170.9 %copy-start = (bf16[2,192,2048]{2,1,0:T(8,128)(2,1)S(1)}, bf16[2,192,2048]{2,1,0:T(8,128)(2,1)}, u32[]{:S(2)}) copy-start(bf16[2,192,2048]{2,1,0:T(8,128)(2,1)} %param.17) | copy-start | bytes 4718596
  35.1 12.0 %copy-start.14 = (bf16[128,8]{0,1:T(8,128)(2,1)S(1)}, bf16[128,8]{0,1:T(8,128)(2,1)}, u32[]{:S(2)}) copy-start(bf16[128,8]{0,1:T(8,128)(2,1)} %param.16) | copy-start | bytes 6148
  35.1 128.6 %all-to-all-start.1 = ((bf16[64,2,10,2048]{3,1,2,0:T(2,128)(2,1)}), bf16[64,2,10,2048]{3,1,2,0:T(2,128)(2,1)}, u32[]{:S(2)}, u32[]{:S(2)}) async-start(bf16[64,2,10,2048]{3,1,2,0:T(2,128)(2,1)} %copy.72), calls=%async_computation.1 | async-start | bytes 10485760 | tf_op jit(solution)/shard_map/all_to_all | solution.py:100
  163.6 124.3 %all-to-all-start = ((bf16[64,2,10,2048]{3,1,2,0:T(2,128)(2,1)}), bf16[64,2,10,2048]{3,1,2,0:T(2,128)(2,1)}, u32[]{:S(2)}, u32[]{:S(2)}) async-start(bf16[64,2,10,2048]{3,1,2,0:T(2,128)(2,1)} %copy.70), calls=%async_computation | async-start | bytes 10485760 | tf_op jit(solution)/shard_map/all_to_all | solution.py:101
  311.7 14.1 %copy-start.12 = (bf16[128,128]{1,0:T(8,128)(2,1)S(1)}, bf16[128,128]{1,0:T(8,128)(2,1)}, u32[]{:S(2)}) copy-start(bf16[128,128]{1,0:T(8,128)(2,1)} %param.21) | copy-start | bytes 98308
  311.7 23.3 %copy-start.9 = (bf16[128,1024]{1,0:T(8,128)(2,1)S(1)}, bf16[128,1024]{1,0:T(8,128)(2,1)}, u32[]{:S(2)}) copy-start(bf16[128,1024]{1,0:T(8,128)(2,1)} %param.23) | copy-start | bytes 786436
  311.7 23.3 %copy-start.10 = (bf16[128,1024]{1,0:T(8,128)(2,1)S(1)}, bf16[128,1024]{1,0:T(8,128)(2,1)}, u32[]{:S(2)}) copy-start(bf16[128,1024]{1,0:T(8,128)(2,1)} %param.24) | copy-start | bytes 786436
  311.7 23.4 %copy-start.13 = (s32[8192]{0:T(1024)S(1)}, s32[8192]{0:T(1024)}, u32[]{:S(2)}) copy-start(s32[8192]{0:T(1024)} %param.25) | copy-start | bytes 98308
  311.7 239.0 %copy-start.11 = (bf16[128,1024]{1,0:T(8,128)(2,1)S(1)}, bf16[128,1024]{1,0:T(8,128)(2,1)}, u32[]{:S(2)}) copy-start(bf16[128,1024]{1,0:T(8,128)(2,1)} %param.20) | copy-start | bytes 786436
  311.7 299.0 %all-to-all-start.2 = ((f32[64,2,10,2048]{3,1,2,0:T(2,128)}), f32[64,2,10,2048]{3,1,2,0:T(2,128)}, u32[]{:S(2)}, u32[]{:S(2)}) async-start(f32[64,2,10,2048]{3,1,2,0:T(2,128)} %copy.75), calls=%async_computation.2 | async-start | bytes 20971520 | tf_op jit(solution)/shard_map/all_to_all | solution.py:106
  319.6 232.1 %collective-permute-start.4 = (bf16[128,128]{1,0:T(8,128)(2,1)S(1)}, bf16[128,128]{1,0:T(8,128)(2,1)S(1)}, u32[]{:S(2)}, u32[]{:S(2)}) collective-permute-start(bf16[128,128]{1,0:T(8,128)(2,1)S(1)} %copy-done.15), channel_id=1, source_target_pairs={{0,8},{4,12},{8,16},{12,20},{16,24},{20,28},{24,32},{28,36},{32,40... | collective-permute-start | bytes 98312 | tf_op jit(solution)/shard_map/ppermute | solution.py:15
  323.0 228.7 %collective-permute-start.3 = (bf16[128,128]{1,0:T(8,128)(2,1)S(1)}, bf16[128,128]{1,0:T(8,128)(2,1)S(1)}, u32[]{:S(2)}, u32[]{:S(2)}) collective-permute-start(bf16[128,128]{1,0:T(8,128)(2,1)S(1)} %copy-done.15), channel_id=1, source_target_pairs={{0,12},{4,16},{8,20},{12,24},{16,28},{20,32},{24,36},{28,40},{32,4... | collective-permute-start | bytes 98312 | tf_op jit(solution)/shard_map/ppermute | solution.py:15
  325.8 223.0 %collective-permute-start.1 = (bf16[128,128]{1,0:T(8,128)(2,1)S(1)}, bf16[128,128]{1,0:T(8,128)(2,1)S(1)}, u32[]{:S(2)}, u32[]{:S(2)}) collective-permute-start(bf16[128,128]{1,0:T(8,128)(2,1)S(1)} %copy-done.12), channel_id=1, source_target_pairs={{0,8},{4,12},{8,16},{12,20},{16,24},{20,28},{24,32},{28,36},{32,40... | collective-permute-start | bytes 98312 | tf_op jit(solution)/shard_map/ppermute | solution.py:15
  330.4 220.3 %collective-permute-start = (bf16[128,128]{1,0:T(8,128)(2,1)S(1)}, bf16[128,128]{1,0:T(8,128)(2,1)S(1)}, u32[]{:S(2)}, u32[]{:S(2)}) collective-permute-start(bf16[128,128]{1,0:T(8,128)(2,1)S(1)} %copy-done.12), channel_id=1, source_target_pairs={{0,12},{4,16},{8,20},{12,24},{16,28},{20,32},{24,36},{28,40},{32,4... | collective-permute-start | bytes 98312 | tf_op jit(solution)/shard_map/ppermute | solution.py:15
  332.9 217.8 %collective-permute-start.2 = (bf16[128,128]{1,0:T(8,128)(2,1)S(1)}, bf16[128,128]{1,0:T(8,128)(2,1)S(1)}, u32[]{:S(2)}, u32[]{:S(2)}) collective-permute-start(bf16[128,128]{1,0:T(8,128)(2,1)S(1)} %copy-done.12), channel_id=1, source_target_pairs={{0,4},{4,8},{8,12},{12,16},{16,20},{20,24},{24,28},{28,32},{32,36}... | collective-permute-start | bytes 98312 | tf_op jit(solution)/shard_map/ppermute | solution.py:15
  548.8 5.2 collective-permute-start.5
  555.3 18.5 %collective-permute-start.6 = (f32[128,128]{1,0:T(8,128)S(1)}, f32[128,128]{1,0:T(8,128)S(1)}, u32[]{:S(2)}, u32[]{:S(2)}) collective-permute-start(f32[128,128]{1,0:T(8,128)S(1)} %get-tuple-element.40), channel_id=1, source_target_pairs={{4,0},{8,4},{12,8},{16,12},{20,16},{24,20},{28,24},{32,28},{36,32}... | collective-permute-start | bytes 196616 | tf_op jit(solution)/shard_map/ppermute | solution.py:15
  557.2 18.7 %collective-permute-start.8 = (f32[128,128]{1,0:T(8,128)S(1)}, f32[128,128]{1,0:T(8,128)S(1)}, u32[]{:S(2)}, u32[]{:S(2)}) collective-permute-start(f32[128,128]{1,0:T(8,128)S(1)} %get-tuple-element.41), channel_id=1, source_target_pairs={{12,0},{16,4},{20,8},{24,12},{28,16},{32,20},{36,24},{40,28},{44,3... | collective-permute-start | bytes 196616 | tf_op jit(solution)/shard_map/ppermute | solution.py:15
  563.3 12.6 %collective-permute-start.7 = (f32[128,128]{1,0:T(8,128)S(1)}, f32[128,128]{1,0:T(8,128)S(1)}, u32[]{:S(2)}, u32[]{:S(2)}) collective-permute-start(f32[128,128]{1,0:T(8,128)S(1)} %get-tuple-element.42), channel_id=1, source_target_pairs={{8,0},{12,4},{16,8},{20,12},{24,16},{28,20},{32,24},{36,28},{40,32... | collective-permute-start | bytes 196616 | tf_op jit(solution)/shard_map/ppermute | solution.py:15
  566.7 13.9 %copy-start.6 = (bf16[64,2,10,192]{3,0,2,1:T(8,128)(2,1)S(1)}, bf16[64,2,10,192]{3,0,2,1:T(8,128)(2,1)}, u32[]{:S(2)}) copy-start(bf16[64,2,10,192]{3,0,2,1:T(8,128)(2,1)} %copy-done.5) | copy-start | bytes 1474564
  568.2 8.3 %collective-permute-start.9 = (f32[128,128]{1,0:T(8,128)S(1)}, f32[128,128]{1,0:T(8,128)S(1)}, u32[]{:S(2)}, u32[]{:S(2)}) collective-permute-start(f32[128,128]{1,0:T(8,128)S(1)} %get-tuple-element.37), channel_id=1, source_target_pairs={{4,0},{8,4},{12,8},{16,12},{20,16},{24,20},{28,24},{32,28},{36,32}... | collective-permute-start | bytes 196616 | tf_op jit(solution)/shard_map/ppermute | solution.py:15
  570.1 6.4 collective-permute-start.11
  573.7 6.2 collective-permute-start.10
  657.6 39.2 %copy-start.1 = (bf16[2,192,2048]{2,1,0:T(8,128)(2,1)S(1)}, bf16[2,192,2048]{2,1,0:T(8,128)(2,1)}, u32[]{:S(2)}) copy-start(bf16[2,192,2048]{2,1,0:T(8,128)(2,1)} %param.17) | copy-start | bytes 4718596
  (9 other events, 62.6 us)
where the time goes:
time: 706 us; the launch traced here: 697 us
  waiting for transfers between devices  395 us (56%)
  local copies, waits for them, and re-layouts  131 us (19%)
  starting transfers between devices  63.6 us (9%)
  matrix products  56.8 us (8%)
  blocking collectives  33.7 us (5%)
  other arithmetic  15.7 us (2%)
    ppermute x12, waiting for transfers between devices, passed_along(): return lax.ppermute(block, axis, route)  219 us
    all_to_all x1, waiting for transfers between devices, body(): lax.all_to_all(send_grads, 'ctx', split_axis=0, concat_axis=0, tiled=True)  103 us
    all_to_all x1, waiting for transfers between devices, body(): lax.all_to_all(send_rows, 'ctx', split_axis=0, concat_axis=0, tiled=True)  73.3 us
    ppermute x12, starting transfers between devices, passed_along(): return lax.ppermute(block, axis, route)  35.9 us
    psum x1, blocking collectives, body(): grad_tokens = lax.psum(summed, 'head').astype(jnp.bfloat16)  33.7 us
    reshape x2, local copies, waits for them, and re-layouts, body(): send_rows = padded_tokens[slot_token].reshape(buffer_shape)  20.8 us
    all_to_all x1, local copies, waits for them, and re-layouts, body(): lax.all_to_all(back_rows, 'ctx', split_axis=0, concat_axis=0, tiled=True)  19.9 us
  transfers between devices with their start and end apart: 15, of which 5 were waited for; matrix products, arithmetic and copies ran while one was open for 13% of the time, Pallas kernels for 0%

commit v1 on v0

v1 whole, which is shorter than its diff:
```python
import functools

import jax
import jax.numpy as jnp
import numpy as np
from jax import lax
from jax.experimental import pallas as pl
from jax.experimental.pallas import tpu as pltpu
from jax.sharding import PartitionSpec as P

HQ = 32
KVH = 4
HD = 128
REACH = 3
CAP = 10
LOCAL = 2
SLOTS = LOCAL * CAP
GROUP = 2 * SLOTS
BF = jnp.bfloat16
F32 = jnp.float32


def passed_along(block, axis, distance):
    devices = range(lax.axis_size(axis))
    route = [(i - distance, i) for i in devices if i - distance in devices]
    return lax.ppermute(block, axis, route)


def turned(block, distance):
    count = lax.axis_size("head")
    return lax.ppermute(block, "head", [(i, (i + distance) % count) for i in range(count)])


def spec():
    return pl.BlockSpec(memory_space=pltpu.VMEM)


def dot_nt(a, b):
    return lax.dot_general(a, b, (((1,), (1,)), ((), ())), preferred_element_type=F32)


def dot_nn(a, b):
    return lax.dot_general(a, b, (((1,), (0,)), ((), ())), preferred_element_type=F32)


def dot_tn(a, b):
    return lax.dot_general(a, b, (((0,), (0,)), ((), ())), preferred_element_type=F32)


def column_block(shape, offset):
    block = shape[:-1] + (shape[-1] // 4,)
    lead = (0,) * (len(shape) - 1)
    return pl.BlockSpec(block, lambda i, head, lead=lead, offset=offset: lead + ((head[0] + offset) % 4,))


def whole(shape):
    zeros = (0,) * len(shape)
    return pl.BlockSpec(shape, lambda i, head, zeros=zeros: zeros)


def call(kernel, head, ins, outs, scratch=()):
    arrays = [a for a, _ in ins]
    return pl.pallas_call(
        kernel,
        grid_spec=pltpu.PrefetchScalarGridSpec(
            num_scalar_prefetch=1,
            grid=(1,),
            in_specs=[s for _, s in ins],
            out_specs=[s for _, s in outs],
            scratch_shapes=list(scratch),
        ),
        out_shape=[o for o, _ in outs],
        compiler_params=pltpu.CompilerParams(vmem_limit_bytes=56 << 20),
    )(head, *arrays)


def full(a):
    return (a, whole(a.shape))


def out(shape, dtype):
    return (jax.ShapeDtypeStruct(shape, dtype), whole(shape))


def route_kernel(head, ids, probs, pattern, tok, rows_ref, pick_ref, scaled_ref, rank_s, prob_s):
    experts, count = rank_s.shape
    where_e = lax.broadcasted_iota(jnp.int32, (experts, count), 0)
    hits = jnp.zeros((experts, count), F32)
    chance = jnp.zeros((experts, count), F32)
    for k in range(ids.shape[0]):
        hit = ids[k : k + 1, :] == where_e
        hits = jnp.where(hit, 1.0, hits)
        chance = jnp.where(hit, probs[k : k + 1, :], chance)
    first = lax.broadcasted_iota(jnp.int32, (count, count), 0)
    second = lax.broadcasted_iota(jnp.int32, (count, count), 1)
    before = jnp.where(first < second, 1.0, 0.0).astype(BF)
    rank = dot_nn(hits.astype(BF), before)
    rank_s[...] = jnp.where(hits > 0.0, rank, -1.0)
    prob_s[...] = chance
    which = pattern[0]
    place = pattern[1]
    lower = pattern[2]

    def step(i, carry):
        base = i * (2 * LOCAL)
        value = rank_s[pl.ds(base, 1), :]
        weight = prob_s[pl.ds(base, 1), :]
        for j in range(1, 2 * LOCAL):
            mine = which == j
            value = jnp.where(mine, rank_s[pl.ds(base + j, 1), :], value)
            weight = jnp.where(mine, prob_s[pl.ds(base + j, 1), :], weight)
        match = jnp.where(value == place, 1.0, 0.0)
        weight = match * weight
        at = pl.multiple_of(i * 2 * GROUP, 2 * GROUP)
        zero = jnp.zeros_like(match)
        in_low = lower > 0.0
        pick_ref[pl.ds(at, 2 * GROUP), 0:count] = jnp.where(in_low, match, zero).astype(BF)
        pick_ref[pl.ds(at, 2 * GROUP), count : 2 * count] = jnp.where(in_low, zero, match).astype(BF)
        scaled_ref[pl.ds(at, 2 * GROUP), 0:count] = jnp.where(in_low, weight, zero).astype(BF)
        scaled_ref[pl.ds(at, 2 * GROUP), count : 2 * count] = jnp.where(in_low, zero, weight).astype(BF)
        return carry

    lax.fori_loop(0, experts // (2 * LOCAL), step, 0)
    half = tok.shape[1] // 2
    stacked = jnp.concatenate([tok[:, :half], tok[:, half:]], axis=0)
    rows_ref[...] = dot_nn(pick_ref[...], stacked).astype(BF)


def select_kernel(head, scaled, tok, rows_ref):
    half = tok.shape[1] // 2
    stacked = jnp.concatenate([tok[:, :half], tok[:, half:]], axis=0)
    rows_ref[...] = dot_nn(scaled[...], stacked).astype(BF)


def pattern_table(count):
    r = np.arange(2 * GROUP)
    which = (r // GROUP) * LOCAL + (r % SLOTS) // CAP
    place = r % CAP
    lower = (r % GROUP) < SLOTS
    table = np.stack([which, place, lower]).astype(np.float32)
    return jnp.asarray(np.repeat(table[:, :, None], count, axis=2))


def untangle_kernel(head, recv, low_ref, high_ref, wide):
    sources = recv.shape[0] // GROUP
    half = recv.shape[1]
    lanes = wide[0].shape[1]
    for p in range(half // lanes):
        wide[p][...] = recv[:, p * lanes : (p + 1) * lanes].astype(F32)
    for e, ref in ((0, low_ref), (1, high_ref)):
        for c in range(CAP):
            for part in range(2):
                for p in range(half // lanes):
                    rows = wide[p][pl.ds(part * SLOTS + e * CAP + c, sources, stride=GROUP), :]
                    col = part * half + p * lanes
                    ref[c * sources : (c + 1) * sources, col : col + lanes] = rows.astype(BF)


def tangle_kernel(head, own, left_a, left_b, right_a, right_b, send_ref, wide):
    rows = own.shape[0] // 2
    sources = rows // CAP
    half = own.shape[1] // 2
    lanes = wide[0].shape[1]
    for e, (a, b) in ((0, (left_b, right_a)), (1, (left_a, right_b))):
        for c in range(CAP):
            for part in range(2):
                for p in range(half // lanes):
                    col = part * half + p * lanes
                    at = c * sources
                    total = (
                        own[e * rows + at : e * rows + at + sources, col : col + lanes]
                        + a[at : at + sources, col : col + lanes].astype(F32)
                        + b[at : at + sources, col : col + lanes].astype(F32)
                    )
                    wide[p][pl.ds(part * SLOTS + e * CAP + c, sources, stride=GROUP), :] = total
    for p in range(half // lanes):
        send_ref[:, p * lanes : (p + 1) * lanes] = wide[p][...].astype(BF)


def pre_kernel(head, *refs):
    blocks, gates, ups = refs[0:8], refs[8:12], refs[12:16]
    act_ref, slope_ref, hidden_ref = refs[16:]
    for e in range(LOCAL):
        rows = blocks[e].shape[0]
        gate = dot_nt(blocks[e][...], gates[0][e])
        up = dot_nt(blocks[e][...], ups[0][e])
        for q in range(1, 4):
            gate = gate + dot_nt(blocks[2 * q + e][...], gates[q][e])
            up = up + dot_nt(blocks[2 * q + e][...], ups[q][e])
        sig = jax.nn.sigmoid(gate)
        active = gate * sig
        at = pl.ds(e * rows, rows)
        act_ref[at, :] = active
        slope_ref[at, :] = up * sig * (1.0 + gate * (1.0 - sig))
        hidden_ref[at, :] = (active * up).astype(BF)


def grad_kernel(head, *refs):
    blocks, downs = refs[0:8], refs[8:12]
    act, slope, gate_far, up_far = refs[12:16]
    gg_ref, ug_ref, far_low, far_high = refs[16:]
    for e, far in ((0, far_low), (1, far_high)):
        rows = blocks[e].shape[0]
        got = dot_nt(blocks[e][...], downs[0][e])
        for q in range(1, 4):
            got = got + dot_nt(blocks[2 * q + e][...], downs[q][e])
        at = pl.ds(e * rows, rows)
        gg = (got * slope[at, :]).astype(BF)
        ug = (got * act[at, :]).astype(BF)
        gg_ref[at, :] = gg
        ug_ref[at, :] = ug
        far[...] = (dot_nn(gg, gate_far[e]) + dot_nn(ug, up_far[e])).astype(BF)


def back_kernel(head, gg, ug, gate_p, up_p, gate_m, up_m, gate_o, up_o, p0, p1, m0, m1, own):
    rows = gg.shape[0] // 2
    low, high = pl.ds(0, rows), pl.ds(rows, rows)
    p1[...] = (dot_nn(gg[high, :], gate_p[1]) + dot_nn(ug[high, :], up_p[1])).astype(BF)
    m0[...] = (dot_nn(gg[low, :], gate_m[0]) + dot_nn(ug[low, :], up_m[0])).astype(BF)
    p0[...] = dot_nn(gg[low, :], gate_p[0]) + dot_nn(ug[low, :], up_p[0])
    m1[...] = dot_nn(gg[high, :], gate_m[1]) + dot_nn(ug[high, :], up_m[1])
    own[low, :] = dot_nn(gg[low, :], gate_o[0]) + dot_nn(ug[low, :], up_o[0])
    own[high, :] = dot_nn(gg[high, :], gate_o[1]) + dot_nn(ug[high, :], up_o[1])


def weight_kernel(head, *refs):
    blocks = refs[0:8]
    sides = len(refs[8:]) // 2
    lefts, results = refs[8 : 8 + sides], refs[8 + sides :]
    width = blocks[0].shape[1]
    offsets = (0, 3, 1, 2)
    for q in range(4):
        col = pl.multiple_of(((head[0] + offsets[q]) % 4) * width, width)
        for e in range(LOCAL):
            rows = blocks[e].shape[0]
            data = blocks[2 * q + e][...]
            for left, result in zip(lefts, results):
                part = dot_tn(left[pl.ds(e * rows, rows), :], data)
                result[e, :, pl.ds(col, width)] = part.astype(BF)


def round_ring(low, high):
    right_low = turned(low, 1)
    left_high = turned(high, -1)
    right_high = turned(high, 1)
    left_low = turned(low, -1)
    far_low = turned(right_low, 1)
    far_high = turned(left_high, -1)
    return [low, high, right_low, right_high, left_low, left_high, far_low, far_high]


def dispatch(send, head, count, lanes):
    half = send.shape[1]
    recv = lax.all_to_all(
        send.reshape(count, GROUP, half), "ctx", split_axis=0, concat_axis=0, tiled=True
    ).reshape(count * GROUP, half)
    low, high = call(
        untangle_kernel,
        head,
        [full(recv)],
        [out((count * CAP, 2 * half), BF), out((count * CAP, 2 * half), BF)],
        [[pltpu.VMEM((count * GROUP, lanes), F32) for _ in range(half // lanes)]],
    )
    return round_ring(low, high)


def attention(query_rows, window_kv, attn_out, grad_attn, segment_ids, kv_width):
    att_rows = query_rows.shape[0]
    kv_local = kv_width // HD
    group_size = HQ // KVH
    window = (REACH + 1) * att_rows
    score_scale = HD ** (-0.5)
    ctx_index = lax.axis_index("ctx")
    window_key = window_kv[:, :kv_width].reshape(window, kv_local, HD)
    window_value = window_kv[:, kv_width:].reshape(window, kv_local, HD)
    query_pos = ctx_index * att_rows + jnp.arange(att_rows, dtype=jnp.int32)
    key_pos = (ctx_index - REACH) * att_rows + jnp.arange(window, dtype=jnp.int32)
    padded_segment = jnp.concatenate([jnp.full((REACH * att_rows,), -1, jnp.int32), segment_ids])
    key_seg = lax.dynamic_slice_in_dim(padded_segment, ctx_index * att_rows, window, 0)
    query_seg = lax.dynamic_slice_in_dim(segment_ids, ctx_index * att_rows, att_rows, 0)
    visible = (key_pos[None, :] <= query_pos[:, None]) & (key_seg[None, :] == query_seg[:, None])
    query_heads = query_rows.reshape(att_rows, kv_local, group_size, HD)
    out_heads = attn_out.reshape(att_rows, kv_local, group_size, HD)
    grad_heads = grad_attn.reshape(att_rows, kv_local, group_size, HD)
    scores = (
        jnp.einsum("ajgd,tjd->jgat", query_heads, window_key, preferred_element_type=F32)
        * score_scale
    )
    row_peak = jnp.max(jnp.where(visible, scores, -jnp.inf), axis=-1, keepdims=True)
    weights_exp = jnp.exp(jnp.where(visible, scores - row_peak, -jnp.inf))
    probs = weights_exp / jnp.sum(weights_exp, axis=-1, keepdims=True)
    row_delta = jnp.einsum("ajgd,ajgd->jga", grad_heads, out_heads, preferred_element_type=F32)
    prob_grad = jnp.einsum("ajgd,tjd->jgat", grad_heads, window_value, preferred_element_type=F32)
    score_grad = (probs * (prob_grad - row_delta[..., None])).astype(BF)
    probs_low = probs.astype(BF)
    grad_query = (
        (score_scale * jnp.einsum("jgat,tjd->ajgd", score_grad, window_key, preferred_element_type=F32))
        .astype(BF)
        .reshape(att_rows, -1)
    )
    key_terms = (
        score_scale
        * jnp.einsum("jgat,ajgd->tjd", score_grad, query_heads, preferred_element_type=F32)
    ).reshape(window, kv_width)
    value_terms = jnp.einsum(
        "jgat,ajgd->tjd", probs_low, grad_heads, preferred_element_type=F32
    ).reshape(window, kv_width)
    return grad_query, jnp.concatenate([key_terms, value_terms], axis=1)


def body(
    tokens,
    grad_out,
    expert_ids,
    gate_probs,
    w_gate,
    w_up,
    w_down,
    query_rows,
    key_rows,
    value_rows,
    attn_out,
    grad_attn,
    segment_ids,
):
    tok_count, width = tokens.shape
    count = lax.axis_size("ctx")
    quarter = width // 4
    half = quarter // 2
    lanes = min(half, 128)
    hidden_local = w_gate.shape[1]
    head = lax.axis_index("head").astype(jnp.int32).reshape(1)
    experts = count * LOCAL
    slots = count * GROUP
    rows = count * CAP
    kv_width = key_rows.shape[1]
    att_rows = query_rows.shape[0]

    kv = jnp.concatenate([key_rows, value_rows], axis=1)
    kv_blocks = [passed_along(kv, "ctx", distance) for distance in range(REACH, 0, -1)]

    send_rows, pick, scaled = call(
        route_kernel,
        head,
        [
            full(expert_ids.T),
            full(gate_probs.T.astype(F32)),
            full(pattern_table(tok_count)),
            (tokens, column_block(tokens.shape, 0)),
        ],
        [out((slots, half), BF), out((slots, 2 * tok_count), BF), out((slots, 2 * tok_count), BF)],
        [pltpu.VMEM((experts, tok_count), F32), pltpu.VMEM((experts, tok_count), F32)],
    )
    send_rows, kv_blocks = lax.optimization_barrier((send_rows, kv_blocks))
    (send_grads,) = call(
        select_kernel,
        head,
        [full(scaled), (grad_out, column_block(grad_out.shape, 0))],
        [out((slots, half), BF)],
    )
    row_blocks = dispatch(send_rows, head, count, lanes)
    grad_blocks = dispatch(send_grads, head, count, lanes)

    gate_at = lambda offset: (w_gate, column_block(w_gate.shape, offset))
    up_at = lambda offset: (w_up, column_block(w_up.shape, offset))
    down_at = lambda offset: (w_down, column_block(w_down.shape, offset))
    order = (0, 3, 1, 2)
    act, slope, hidden = call(
        pre_kernel,
        head,
        [full(b) for b in row_blocks] + [gate_at(o) for o in order] + [up_at(o) for o in order],
        [
            out((2 * rows, hidden_local), F32),
            out((2 * rows, hidden_local), F32),
            out((2 * rows, hidden_local), BF),
        ],
    )
    gg, ug, far_low, far_high = call(
        grad_kernel,
        head,
        [full(b) for b in grad_blocks]
        + [down_at(o) for o in order]
        + [full(act), full(slope), gate_at(2), up_at(2)],
        [
            out((2 * rows, hidden_local), BF),
            out((2 * rows, hidden_local), BF),
            out((rows, quarter), BF),
            out((rows, quarter), BF),
        ],
    )
    near_low = turned(far_low, 1)
    near_high = turned(far_high, -1)
    p0, p1, m0, m1, own = call(
        back_kernel,
        head,
        [full(gg), full(ug), gate_at(1), up_at(1), gate_at(3), up_at(3), gate_at(0), up_at(0)],
        [
            out((rows, quarter), F32),
            out((rows, quarter), BF),
            out((rows, quarter), BF),
            out((rows, quarter), F32),
            out((2 * rows, quarter), F32),
        ],
    )
    left_a = turned(p1, 1)
    right_a = turned(m0, -1)
    left_b = turned((p0 + near_low.astype(F32)).astype(BF), 1)
    right_b = turned((m1 + near_high.astype(F32)).astype(BF), -1)
    (send_back,) = call(
        tangle_kernel,
        head,
        [full(own), full(left_a), full(left_b), full(right_a), full(right_b)],
        [out((slots, half), BF)],
        [[pltpu.VMEM((slots, lanes), F32) for _ in range(half // lanes)]],
    )
    returned = lax.all_to_all(
        send_back.reshape(count, GROUP, half), "ctx", split_axis=0, concat_axis=0, tiled=True
    ).reshape(slots, half)
    summed = dot_tn(pick, returned)
    token_part = jnp.concatenate([summed[:tok_count], summed[tok_count:]], axis=1).astype(BF)
    grad_tokens = lax.all_gather(token_part, "head", axis=1, tiled=True)

    weight_out = out(w_gate.shape, BF)
    grad_gate, grad_up = call(
        weight_kernel,
        head,
        [full(b) for b in row_blocks] + [full(gg), full(ug)],
        [weight_out, weight_out],
    )
    (grad_down,) = call(
        weight_kernel, head, [full(b) for b in grad_blocks] + [full(hidden)], [weight_out]
    )

    grad_query, terms = attention(
        query_rows,
        jnp.concatenate(kv_blocks + [kv], axis=0),
        attn_out,
        grad_attn,
        segment_ids,
        kv_width,
    )
    total = terms[REACH * att_rows :]
    for distance in range(1, REACH + 1):
        offset = (REACH - distance) * att_rows
        total = total + passed_along(terms[offset : offset + att_rows], "ctx", -distance)
    total = total.astype(BF)
    return (
        grad_tokens,
        grad_gate,
        grad_up,
        grad_down,
        grad_query,
        total[:, :kv_width],
        total[:, kv_width:],
    )


def solution(mesh):
    placed = (
        P("ctx", None),
        P("ctx", None),
        P("ctx", None),
        P("ctx", None),
        P("ctx", "head", None),
        P("ctx", "head", None),
        P("ctx", "head", None),
        P("ctx", "head"),
        P("ctx", "head"),
        P("ctx", "head"),
        P("ctx", "head"),
        P("ctx", "head"),
        P(),
    )
    return jax.shard_map(
        body,
        mesh=mesh,
        in_specs=placed,
        out_specs=(
            P("ctx", None),
            P("ctx", "head", None),
            P("ctx", "head", None),
            P("ctx", "head", None),
            P("ctx", "head"),
            P("ctx", "head"),
            P("ctx", "head"),
        ),
        check_vma=False,
    )
```

time: 706 us -> 328 us (0.46); the launches traced: 697 us -> 327 us
  waiting for transfers between devices: 395 us -> 163 us
  local copies, waits for them, and re-layouts: 131 us -> 9.77 us
  matrix products: 56.8 us -> 3.33 us
  Pallas kernels: 0 us -> 52.6 us
  blocking collectives: 33.7 us -> 13.6 us
  starting transfers between devices: 63.6 us -> 78.2 us
  other arithmetic: 15.7 us -> 5.42 us
    ppermute x12 -> x6, waiting for transfers between devices: 219 us -> 49.2 us  [passed_along(): return lax.ppermute(block, axis, route)]
    all_to_all x3, waiting for transfers between devices: 176 us -> 28.3 us  [the longest x2 28.3 us: dispatch(): lax.all_to_all(send.reshape(count, GROUP, half), 'ctx', split_axis=0, con...]
    ppermute x0 -> x18, waiting for transfers between devices: none -> 85.2 us  [turned(): lax.ppermute(block, 'head', [(i, (i + distance) % count) for i in range(c...]
    dot_general x13 -> x6, matrix products: 56.8 us -> 3.33 us  [the longest x1 0.76 us: attention(): jnp.einsum('ajgd,tjd->jgat', grad_heads, window_value, preferred_element_...]
    pallas_call x0 -> x10, Pallas kernels: none -> 52.6 us  [call(): pl.pallas_call(kernel, grid_spec=pltpu.PrefetchScalarGridSpec(num_scalar_...]
    reshape x3 -> x0, local copies, waits for them, and re-layouts: 34.8 us -> none  [the longest x2 20.8 us: body(): send_rows = padded_tokens[slot_token].reshape(buffer_shape)]
    psum x1 -> x0, blocking collectives: 33.7 us -> none  [body(): grad_tokens = lax.psum(summed, 'head').astype(jnp.bfloat16)]
    gather x4 -> x0, local copies, waits for them, and re-layouts: 32.5 us -> none  [the longest x1 13 us: pair_total(): picked = flat_rows[slot_index]]
  transfers between devices with their start and end apart: 15 -> 27, of which waited for: 5 -> 18; matrix products, arithmetic and copies ran while one was open for 13% -> 4% of each run, Pallas kernels for 0% -> 10%
where the time goes in v1:
time: 328 us; the launch traced here: 327 us
  waiting for transfers between devices  163 us (50%)
  starting transfers between devices  78.2 us (24%)
  Pallas kernels  52.6 us (16%)
  blocking collectives  13.6 us (4%)
  local copies, waits for them, and re-layouts  9.77 us (3%)
  other arithmetic  5.42 us (2%)
  matrix products  3.33 us (1%)
    ppermute x18, waiting for transfers between devices, turned(): lax.ppermute(block, 'head', [(i, (i + distance) % count) for i in range(c...  85.2 us
    pallas_call x10, Pallas kernels, call(): pl.pallas_call(kernel, grid_spec=pltpu.PrefetchScalarGridSpec(num_scalar_...  52.6 us
    ppermute x6, waiting for transfers between devices, passed_along(): return lax.ppermute(block, axis, route)  49.2 us
    ppermute x18, starting transfers between devices, turned(): lax.ppermute(block, 'head', [(i, (i + distance) % count) for i in range(c...  29.3 us
    all_to_all x2, waiting for transfers between devices, dispatch(): lax.all_to_all(send.reshape(count, GROUP, half), 'ctx', split_axis=0, con...  28.3 us
    ppermute x6, starting transfers between devices, passed_along(): return lax.ppermute(block, axis, route)  20.7 us
    all_to_all x2, starting transfers between devices, dispatch(): lax.all_to_all(send.reshape(count, GROUP, half), 'ctx', split_axis=0, con...  20.3 us
    all_gather x1, blocking collectives, body(): grad_tokens = lax.all_gather(token_part, 'head', axis=1, tiled=True)  13.6 us
  transfers between devices with their start and end apart: 27, of which 18 were waited for; matrix products, arithmetic and copies ran while one was open for 4% of the time, Pallas kernels for 10%

profile of v1, /device:TPU:48, one launch (start us, length us, event | category | flops | bytes accessed | tf_op | source)
XLA Modules:
  0.0 326.7 jit_solution(10326792373583744654)
XLA Ops:
  9.0 11.8 %all-to-all-start = ((bf16[64,40,256]{2,1,0:T(8,128)(2,1)}), bf16[64,40,256]{2,1,0:T(8,128)(2,1)S(1)}, u32[]{:S(2)}, u32[]{:S(2)}) async-start(bf16[64,40,256]{2,1,0:T(8,128)(2,1)} %bitcast.84), calls=%async_computation | async-start | bytes 2621440 | tf_op jit(solution)/shard_map/all_to_all | solution.py:254
  26.3 5.4 %collective-permute-start.6 = (bf16[128,256]{1,0:T(8,128)(2,1)S(1)}, bf16[128,256]{1,0:T(8,128)(2,1)S(1)}, u32[]{:S(2)}, u32[]{:S(2)}) collective-permute-start(bf16[128,256]{1,0:T(8,128)(2,1)S(1)} %constant_dynamic-update-slice_fusion), channel_id=1, source_target_pairs={{0,12},{4,16},{8,20},{12,24},{16,28},{20,32},{24,36},{28,40},{32,4... | collective-permute-start | bytes 196616 | tf_op jit(solution)/shard_map/ppermute | solution.py:26
  31.7 18.4 %collective-permute-done.8 = bf16[128,256]{1,0:T(8,128)(2,1)S(1)} collective-permute-done((bf16[128,256]{1,0:T(8,128)(2,1)S(1)}, bf16[128,256]{1,0:T(8,128)(2,1)S(1)}, u32[]{:S(2)}, u32[]{:S(2)}) %collective-permute-start.8) | collective-permute-done | bytes 65568 | tf_op jit(solution)/shard_map/ppermute | solution.py:26
  52.0 4.2 %collective-permute-done.6 = bf16[128,256]{1,0:T(8,128)(2,1)S(1)} collective-permute-done((bf16[128,256]{1,0:T(8,128)(2,1)S(1)}, bf16[128,256]{1,0:T(8,128)(2,1)S(1)}, u32[]{:S(2)}, u32[]{:S(2)}) %collective-permute-start.6) | collective-permute-done | bytes 65568 | tf_op jit(solution)/shard_map/ppermute | solution.py:26
  56.8 8.6 %all-to-all-start.1 = ((bf16[64,40,256]{2,1,0:T(8,128)(2,1)}), bf16[64,40,256]{2,1,0:T(8,128)(2,1)S(1)}, u32[]{:S(2)}, u32[]{:S(2)}) async-start(bf16[64,40,256]{2,1,0:T(8,128)(2,1)} %bitcast.92), calls=%async_computation.1 | async-start | bytes 2621440 | tf_op jit(solution)/shard_map/all_to_all | solution.py:254
  70.0 28.3 %all-to-all-done.1 = bf16[64,40,256]{2,1,0:T(8,128)(2,1)S(1)} async-done(((bf16[64,40,256]{2,1,0:T(8,128)(2,1)}), bf16[64,40,256]{2,1,0:T(8,128)(2,1)S(1)}, u32[]{:S(2)}, u32[]{:S(2)}) %all-to-all-start.1) | async-done | bytes 1310752 | tf_op jit(solution)/shard_map/all_to_all | solution.py:254
  109.2 12.2 %collective-permute-done.9.refs_2_ = bf16[640,512]{1,0:T(8,128)(2,1)S(1)} collective-permute-done((bf16[640,512]{1,0:T(8,128)(2,1)}, bf16[640,512]{1,0:T(8,128)(2,1)S(1)}, u32[]{:S(2)}, u32[]{:S(2)}) %collective-permute-start.9) | collective-permute-done | bytes 655392 | tf_op jit(solution)/shard_map/ppermute | solution.py:31
  124.7 11.1 %collective-permute-done.3.refs_5_ = bf16[640,512]{1,0:T(8,128)(2,1)S(1)} collective-permute-done((bf16[640,512]{1,0:T(8,128)(2,1)}, bf16[640,512]{1,0:T(8,128)(2,1)S(1)}, u32[]{:S(2)}, u32[]{:S(2)}) %collective-permute-start.3) | collective-permute-done | bytes 655392 | tf_op jit(solution)/shard_map/ppermute | solution.py:31
  138.7 11.1 %collective-permute-done.11.refs_4_ = bf16[640,512]{1,0:T(8,128)(2,1)S(1)} collective-permute-done((bf16[640,512]{1,0:T(8,128)(2,1)}, bf16[640,512]{1,0:T(8,128)(2,1)S(1)}, u32[]{:S(2)}, u32[]{:S(2)}) %collective-permute-start.11) | collective-permute-done | bytes 655392 | tf_op jit(solution)/shard_map/ppermute | solution.py:31
  154.6 9.3 %collective-permute-done.14.refs_7_ = bf16[640,512]{1,0:T(8,128)(2,1)S(1)} collective-permute-done((bf16[640,512]{1,0:T(8,128)(2,1)S(1)}, bf16[640,512]{1,0:T(8,128)(2,1)S(1)}, u32[]{:S(2)}, u32[]{:S(2)}) %collective-permute-start.14) | collective-permute-done | bytes 655392 | tf_op jit(solution)/shard_map/ppermute | solution.py:31
  164.7 8.0 %shard_map.193 = (f32[1280,192]{1,0:T(8,128)}, f32[1280,192]{1,0:T(8,128)}, bf16[1280,192]{1,0:T(8,128)(2,1)}) custom-call(s32[1]{0:T(128)} %bitcast.2.head, bf16[640,512]{1,0:T(8,128)(2,1)} %get-tuple-element.38.refs_0_, bf16[640,512]{1,0:T(8,128)(2,1)} %get-tuple-element.39.refs_1_, bf16[640,512]{1,0:T(8,128)(2,1)} %copy-done.4, ...), custom_call_target="tpu_custom_call" | custom-call | tf_op jit(solution)/shard_map/pallas_call | solution.py:63
  172.8 5.1 %collective-permute-done.2.refs_4_ = bf16[640,512]{1,0:T(8,128)(2,1)S(1)} collective-permute-done((bf16[640,512]{1,0:T(8,128)(2,1)}, bf16[640,512]{1,0:T(8,128)(2,1)S(1)}, u32[]{:S(2)}, u32[]{:S(2)}) %collective-permute-start.2) | collective-permute-done | bytes 655392 | tf_op jit(solution)/shard_map/ppermute | solution.py:31
  180.4 10.7 %collective-permute-done.5.refs_7_ = bf16[640,512]{1,0:T(8,128)(2,1)S(1)} collective-permute-done((bf16[640,512]{1,0:T(8,128)(2,1)S(1)}, bf16[640,512]{1,0:T(8,128)(2,1)S(1)}, u32[]{:S(2)}, u32[]{:S(2)}) %collective-permute-start.5) | collective-permute-done | bytes 655392 | tf_op jit(solution)/shard_map/ppermute | solution.py:31
  192.0 8.9 %shard_map.194 = (bf16[1280,192]{1,0:T(8,128)(2,1)}, bf16[1280,192]{1,0:T(8,128)(2,1)}, bf16[640,512]{1,0:T(8,128)(2,1)}, bf16[640,512]{1,0:T(8,128)(2,1)}) custom-call(s32[1]{0:T(128)} %bitcast.2.head, bf16[640,512]{1,0:T(8,128)(2,1)} %get-tuple-element.34.refs_0_, bf16[640,512]{1,0:T(8,128)(2,1)} %get-tuple-element.35.refs_1_, bf16[640,512]{1,0:T(8,128)(2,1)} %copy-done.2, ...), custom_call_target="tpu_custom_call" | custom-call | tf_op jit(solution)/shard_map/pallas_call | solution.py:63
  204.1 5.7 %shard_map.195 = (f32[640,512]{1,0:T(8,128)}, bf16[640,512]{1,0:T(8,128)(2,1)}, bf16[640,512]{1,0:T(8,128)(2,1)}, f32[640,512]{1,0:T(8,128)}, f32[1280,512]{1,0:T(8,128)}) custom-call(s32[1]{0:T(128)} %bitcast.2.head, bf16[1280,192]{1,0:T(8,128)(2,1)} %get-tuple-element.42.gg.refs_8_, bf16[1280,192]{1,0:T(8,128)(2,1)} %get-tuple-element.43.ug.refs_9_, ...), custom_call_target="tpu_custom_call" | custom-call | tf_op jit(solution)/shard_map/pallas_call | solution.py:63
  213.0 6.9 %collective-permute-done.16 = bf16[640,512]{1,0:T(8,128)(2,1)S(1)} collective-permute-done((bf16[640,512]{1,0:T(8,128)(2,1)}, bf16[640,512]{1,0:T(8,128)(2,1)S(1)}, u32[]{:S(2)}, u32[]{:S(2)}) %collective-permute-start.16) | collective-permute-done | bytes 655392 | tf_op jit(solution)/shard_map/ppermute | solution.py:31
  234.2 12.2 %collective-permute-done.17.left_b = bf16[640,512]{1,0:T(8,128)(2,1)} collective-permute-done((bf16[640,512]{1,0:T(8,128)(2,1)S(1)}, bf16[640,512]{1,0:T(8,128)(2,1)}, u32[]{:S(2)}, u32[]{:S(2)}) %collective-permute-start.17) | collective-permute-done | bytes 655392 | tf_op jit(solution)/shard_map/ppermute | solution.py:31
  246.4 4.4 %shard_map.196 = bf16[2560,256]{1,0:T(8,128)(2,1)} custom-call(s32[1]{0:T(128)} %bitcast.2.head, f32[1280,512]{1,0:T(8,128)} %get-tuple-element.44.own, bf16[640,512]{1,0:T(8,128)(2,1)} %copy-done.15, bf16[640,512]{1,0:T(8,128)(2,1)} %collective-permute-done.17.left_b, bf16[640,512]{1,0:T(8,128)(2,1)} %copy-done.16, ...), custom_call_target="tpu_custom_call" | custom-call | tf_op jit(solution)/shard_map/pallas_call | solution.py:63
  250.9 7.8 %all-to-all-start.2 = ((bf16[64,40,256]{2,1,0:T(8,128)(2,1)}), bf16[64,40,256]{2,1,0:T(8,128)(2,1)S(1)}, u32[]{:S(2)}, u32[]{:S(2)}) async-start(bf16[64,40,256]{2,1,0:T(8,128)(2,1)} %bitcast.86), calls=%async_computation.2 | async-start | bytes 2621440 | tf_op jit(solution)/shard_map/all_to_all | solution.py:416
  263.9 4.4 %collective-permute-start.23 = (f32[128,256]{0,1:T(8,128)S(1)}, f32[128,256]{0,1:T(8,128)S(1)}, u32[]{:S(2)}, u32[]{:S(2)}) collective-permute-start(f32[128,256]{0,1:T(8,128)S(1)} %get-tuple-element.65), channel_id=1, source_target_pairs={{12,0},{16,4},{20,8},{24,12},{28,16},{32,20},{36,24},{40,28},{44,3... | collective-permute-start | bytes 393224 | tf_op jit(solution)/shard_map/ppermute | solution.py:26
  272.9 17.6 %collective-permute-done.21 = f32[128,256]{0,1:T(8,128)S(1)} collective-permute-done((f32[128,256]{0,1:T(8,128)S(1)}, f32[128,256]{0,1:T(8,128)S(1)}, u32[]{:S(2)}, u32[]{:S(2)}) %collective-permute-start.21) | collective-permute-done | bytes 131104 | tf_op jit(solution)/shard_map/ppermute | solution.py:26
  299.0 7.0 %shard_map.197 = (bf16[2,192,2048]{2,1,0:T(8,128)(2,1)}, bf16[2,192,2048]{2,1,0:T(8,128)(2,1)}) custom-call(s32[1]{0:T(128)} %bitcast.2.head, bf16[640,512]{1,0:T(8,128)(2,1)} %get-tuple-element.38.refs_0_, bf16[640,512]{1,0:T(8,128)(2,1)} %get-tuple-element.39.refs_1_, bf16[640,512]{1,0:T(8,128)(2,1)} %copy-done.4, bf16[640,512]{1,0:T(8,128)(2,1)} %copy-done.7, ...), custom_call_target="tpu_custom_call" | custom-call | tf_op jit(solution)/shard_map/pallas_call | solution.py:63
  306.0 5.3 %shard_map.198 = bf16[2,192,2048]{2,1,0:T(8,128)(2,1)} custom-call(s32[1]{0:T(128)} %bitcast.2.head, bf16[640,512]{1,0:T(8,128)(2,1)} %get-tuple-element.34.refs_0_, bf16[640,512]{1,0:T(8,128)(2,1)} %get-tuple-element.35.refs_1_, bf16[640,512]{1,0:T(8,128)(2,1)} %copy-done.2, bf16[640,512]{1,0:T(8,128)(2,1)} %copy-done.11, bf16[640,512]{1,0:T(8,128)(2,1)} %copy-done.9, ...), custom_call_target="tpu_custom_call" | custom-call | tf_op jit(solution)/shard_map/pallas_call | solution.py:63
  312.1 13.6 %all_gather.3 = bf16[128,2048]{0,1:T(8,128)(2,1)S(1)} all-gather(bf16[128,512]{0,1:T(8,128)(2,1)S(1)} %pad_maximum_fusion.2), channel_id=1, replica_groups=mesh['ctx'=64,'head'=4] {'head'}, dimensions={1}, use_global_device_ids=true | all-gather | bytes 655360 | tf_op jit(solution)/shard_map/all_gather | solution.py:421
  (133 shorter events, 87.5 us)
Async XLA Ops:
  9.0 47.2 %all-to-all-start = ((bf16[64,40,256]{2,1,0:T(8,128)(2,1)}), bf16[64,40,256]{2,1,0:T(8,128)(2,1)S(1)}, u32[]{:S(2)}, u32[]{:S(2)}) async-start(bf16[64,40,256]{2,1,0:T(8,128)(2,1)} %bitcast.84), calls=%async_computation | async-start | bytes 2621440 | tf_op jit(solution)/shard_map/all_to_all | solution.py:254
  20.8 29.2 %collective-permute-start.8 = (bf16[128,256]{1,0:T(8,128)(2,1)S(1)}, bf16[128,256]{1,0:T(8,128)(2,1)S(1)}, u32[]{:S(2)}, u32[]{:S(2)}) collective-permute-start(bf16[128,256]{1,0:T(8,128)(2,1)S(1)} %constant_dynamic-update-slice_fusion), channel_id=1, source_target_pairs={{0,4},{4,8},{8,12},{12,16},{16,20},{20,24},{24,28},{28,32},{32,36}... | collective-permute-start | bytes 196616 | tf_op jit(solution)/shard_map/ppermute | solution.py:26
  22.9 29.1 %collective-permute-start.7 = (bf16[128,256]{1,0:T(8,128)(2,1)S(1)}, bf16[128,256]{1,0:T(8,128)(2,1)S(1)}, u32[]{:S(2)}, u32[]{:S(2)}) collective-permute-start(bf16[128,256]{1,0:T(8,128)(2,1)S(1)} %constant_dynamic-update-slice_fusion), channel_id=1, source_target_pairs={{0,8},{4,12},{8,16},{12,20},{16,24},{20,28},{24,32},{28,36},{32,40... | collective-permute-start | bytes 196616 | tf_op jit(solution)/shard_map/ppermute | solution.py:26
  26.3 30.0 %collective-permute-start.6 = (bf16[128,256]{1,0:T(8,128)(2,1)S(1)}, bf16[128,256]{1,0:T(8,128)(2,1)S(1)}, u32[]{:S(2)}, u32[]{:S(2)}) collective-permute-start(bf16[128,256]{1,0:T(8,128)(2,1)S(1)} %constant_dynamic-update-slice_fusion), channel_id=1, source_target_pairs={{0,12},{4,16},{8,20},{12,24},{16,28},{20,32},{24,36},{28,40},{32,4... | collective-permute-start | bytes 196616 | tf_op jit(solution)/shard_map/ppermute | solution.py:26
  56.8 41.4 %all-to-all-start.1 = ((bf16[64,40,256]{2,1,0:T(8,128)(2,1)}), bf16[64,40,256]{2,1,0:T(8,128)(2,1)S(1)}, u32[]{:S(2)}, u32[]{:S(2)}) async-start(bf16[64,40,256]{2,1,0:T(8,128)(2,1)} %bitcast.92), calls=%async_computation.1 | async-start | bytes 2621440 | tf_op jit(solution)/shard_map/all_to_all | solution.py:254
  68.5 39.5 %collective-permute-start = (bf16[640,512]{1,0:T(8,128)(2,1)}, bf16[640,512]{1,0:T(8,128)(2,1)S(1)}, u32[]{:S(2)}, u32[]{:S(2)}) collective-permute-start(bf16[640,512]{1,0:T(8,128)(2,1)} %get-tuple-element.34.refs_0_), channel_id=1, source_target_pairs={{0,1},{1,2},{2,3},{3,0},{4,5},{5,6},{6,7},{7,4},{8,9},{9,10},{10,1... | collective-permute-start | bytes 1966088 | tf_op jit(solution)/shard_map/ppermute | solution.py:31
  105.6 30.1 %collective-permute-start.3 = (bf16[640,512]{1,0:T(8,128)(2,1)}, bf16[640,512]{1,0:T(8,128)(2,1)S(1)}, u32[]{:S(2)}, u32[]{:S(2)}) collective-permute-start(bf16[640,512]{1,0:T(8,128)(2,1)} %get-tuple-element.35.refs_1_), channel_id=1, source_target_pairs={{0,3},{1,0},{2,1},{3,2},{4,7},{5,4},{6,5},{7,6},{8,11},{9,8},{10,9... | collective-permute-start | bytes 1966088 | tf_op jit(solution)/shard_map/ppermute | solution.py:31
  107.2 42.6 %collective-permute-start.11 = (bf16[640,512]{1,0:T(8,128)(2,1)}, bf16[640,512]{1,0:T(8,128)(2,1)S(1)}, u32[]{:S(2)}, u32[]{:S(2)}) collective-permute-start(bf16[640,512]{1,0:T(8,128)(2,1)} %get-tuple-element.38.refs_0_), channel_id=1, source_target_pairs={{0,3},{1,0},{2,1},{3,2},{4,7},{5,4},{6,5},{7,6},{8,11},{9,8},{10,9... | collective-permute-start | bytes 1966088 | tf_op jit(solution)/shard_map/ppermute | solution.py:31
  108.0 43.3 %collective-permute-start.10 = (bf16[640,512]{1,0:T(8,128)(2,1)}, bf16[640,512]{1,0:T(8,128)(2,1)S(1)}, u32[]{:S(2)}, u32[]{:S(2)}) collective-permute-start(bf16[640,512]{1,0:T(8,128)(2,1)} %get-tuple-element.39.refs_1_), channel_id=1, source_target_pairs={{0,1},{1,2},{2,3},{3,0},{4,5},{5,6},{6,7},{7,4},{8,9},{9,10},{10,1... | collective-permute-start | bytes 1966088 | tf_op jit(solution)/shard_map/ppermute | solution.py:31
  121.4 31.1 %collective-permute-start.13 = (bf16[640,512]{1,0:T(8,128)(2,1)S(1)}, bf16[640,512]{1,0:T(8,128)(2,1)S(1)}, u32[]{:S(2)}, u32[]{:S(2)}) collective-permute-start(bf16[640,512]{1,0:T(8,128)(2,1)S(1)} %collective-permute-done.9.refs_2_), channel_id=1, source_target_pairs={{0,1},{1,2},{2,3},{3,0},{4,5},{5,6},{6,7},{7,4},{8,9},{9,10},{10,1... | collective-permute-start | bytes 1966088 | tf_op jit(solution)/shard_map/ppermute | solution.py:31
  121.7 42.1 %collective-permute-start.14 = (bf16[640,512]{1,0:T(8,128)(2,1)S(1)}, bf16[640,512]{1,0:T(8,128)(2,1)S(1)}, u32[]{:S(2)}, u32[]{:S(2)}) collective-permute-start(bf16[640,512]{1,0:T(8,128)(2,1)S(1)} %collective-permute-done.12.refs_5_), channel_id=1, source_target_pairs={{0,3},{1,0},{2,1},{3,2},{4,7},{5,4},{6,5},{7,6},{8,11},{9,8},{10,9... | collective-permute-start | bytes 1966088 | tf_op jit(solution)/shard_map/ppermute | solution.py:31
  135.8 42.1 %collective-permute-start.2 = (bf16[640,512]{1,0:T(8,128)(2,1)}, bf16[640,512]{1,0:T(8,128)(2,1)S(1)}, u32[]{:S(2)}, u32[]{:S(2)}) collective-permute-start(bf16[640,512]{1,0:T(8,128)(2,1)} %get-tuple-element.34.refs_0_), channel_id=1, source_target_pairs={{0,3},{1,0},{2,1},{3,2},{4,7},{5,4},{6,5},{7,6},{8,11},{9,8},{10,9... | collective-permute-start | bytes 1966088 | tf_op jit(solution)/shard_map/ppermute | solution.py:31
  149.8 28.1 %collective-permute-start.1 = (bf16[640,512]{1,0:T(8,128)(2,1)}, bf16[640,512]{1,0:T(8,128)(2,1)S(1)}, u32[]{:S(2)}, u32[]{:S(2)}) collective-permute-start(bf16[640,512]{1,0:T(8,128)(2,1)} %get-tuple-element.35.refs_1_), channel_id=1, source_target_pairs={{0,1},{1,2},{2,3},{3,0},{4,5},{5,6},{6,7},{7,4},{8,9},{9,10},{10,1... | collective-permute-start | bytes 1966088 | tf_op jit(solution)/shard_map/ppermute | solution.py:31
  151.3 29.1 %collective-permute-start.4 = (bf16[640,512]{1,0:T(8,128)(2,1)S(1)}, bf16[640,512]{1,0:T(8,128)(2,1)S(1)}, u32[]{:S(2)}, u32[]{:S(2)}) collective-permute-start(bf16[640,512]{1,0:T(8,128)(2,1)S(1)} %collective-permute-done.refs_2_), channel_id=1, source_target_pairs={{0,1},{1,2},{2,3},{3,0},{4,5},{5,6},{6,7},{7,4},{8,9},{9,10},{10,1... | collective-permute-start | bytes 1966088 | tf_op jit(solution)/shard_map/ppermute | solution.py:31
  152.5 38.6 %collective-permute-start.5 = (bf16[640,512]{1,0:T(8,128)(2,1)S(1)}, bf16[640,512]{1,0:T(8,128)(2,1)S(1)}, u32[]{:S(2)}, u32[]{:S(2)}) collective-permute-start(bf16[640,512]{1,0:T(8,128)(2,1)S(1)} %collective-permute-done.3.refs_5_), channel_id=1, source_target_pairs={{0,3},{1,0},{2,1},{3,2},{4,7},{5,4},{6,5},{7,6},{8,11},{9,8},{10,9... | collective-permute-start | bytes 1966088 | tf_op jit(solution)/shard_map/ppermute | solution.py:31
  202.4 19.5 %collective-permute-start.19 = (bf16[640,512]{1,0:T(8,128)(2,1)}, bf16[640,512]{1,0:T(8,128)(2,1)S(1)}, u32[]{:S(2)}, u32[]{:S(2)}) collective-permute-start(bf16[640,512]{1,0:T(8,128)(2,1)} %get-tuple-element.50), channel_id=1, source_target_pairs={{0,3},{1,0},{2,1},{3,2},{4,7},{5,4},{6,5},{7,6},{8,11},{9,8},{10,9... | collective-permute-start | bytes 1966088 | tf_op jit(solution)/shard_map/ppermute | solution.py:31
  209.8 24.2 %collective-permute-start.15 = (bf16[640,512]{1,0:T(8,128)(2,1)}, bf16[640,512]{1,0:T(8,128)(2,1)S(1)}, u32[]{:S(2)}, u32[]{:S(2)}) collective-permute-start(bf16[640,512]{1,0:T(8,128)(2,1)} %get-tuple-element.45), channel_id=1, source_target_pairs={{0,1},{1,2},{2,3},{3,0},{4,5},{5,6},{6,7},{7,4},{8,9},{9,10},{10,1... | collective-permute-start | bytes 1966088 | tf_op jit(solution)/shard_map/ppermute | solution.py:31
  210.0 24.2 %collective-permute-start.18 = (bf16[640,512]{1,0:T(8,128)(2,1)}, bf16[640,512]{1,0:T(8,128)(2,1)S(1)}, u32[]{:S(2)}, u32[]{:S(2)}) collective-permute-start(bf16[640,512]{1,0:T(8,128)(2,1)} %get-tuple-element.48), channel_id=1, source_target_pairs={{0,3},{1,0},{2,1},{3,2},{4,7},{5,4},{6,5},{7,6},{8,11},{9,8},{10,9... | collective-permute-start | bytes 1966088 | tf_op jit(solution)/shard_map/ppermute | solution.py:31
  221.5 24.9 %collective-permute-start.17 = (bf16[640,512]{1,0:T(8,128)(2,1)S(1)}, bf16[640,512]{1,0:T(8,128)(2,1)}, u32[]{:S(2)}, u32[]{:S(2)}) collective-permute-start(bf16[640,512]{1,0:T(8,128)(2,1)S(1)} %add_convert_fusion.1), channel_id=1, source_target_pairs={{0,1},{1,2},{2,3},{3,0},{4,5},{5,6},{6,7},{7,4},{8,9},{9,10},{10,1... | collective-permute-start | bytes 1966088 | tf_op jit(solution)/shard_map/ppermute | solution.py:31
  222.1 24.3 %collective-permute-start.20 = (bf16[640,512]{1,0:T(8,128)(2,1)S(1)}, bf16[640,512]{1,0:T(8,128)(2,1)}, u32[]{:S(2)}, u32[]{:S(2)}) collective-permute-start(bf16[640,512]{1,0:T(8,128)(2,1)S(1)} %add_convert_fusion), channel_id=1, source_target_pairs={{0,3},{1,0},{2,1},{3,2},{4,7},{5,4},{6,5},{7,6},{8,11},{9,8},{10,9... | collective-permute-start | bytes 1966088 | tf_op jit(solution)/shard_map/ppermute | solution.py:31
  250.9 60.5 %all-to-all-start.2 = ((bf16[64,40,256]{2,1,0:T(8,128)(2,1)}), bf16[64,40,256]{2,1,0:T(8,128)(2,1)S(1)}, u32[]{:S(2)}, u32[]{:S(2)}) async-start(bf16[64,40,256]{2,1,0:T(8,128)(2,1)} %bitcast.86), calls=%async_computation.2 | async-start | bytes 2621440 | tf_op jit(solution)/shard_map/all_to_all | solution.py:416
  261.7 28.8 %collective-permute-start.21 = (f32[128,256]{0,1:T(8,128)S(1)}, f32[128,256]{0,1:T(8,128)S(1)}, u32[]{:S(2)}, u32[]{:S(2)}) collective-permute-start(f32[128,256]{0,1:T(8,128)S(1)} %get-tuple-element.64), channel_id=1, source_target_pairs={{4,0},{8,4},{12,8},{16,12},{20,16},{24,20},{28,24},{32,28},{36,32}... | collective-permute-start | bytes 393224 | tf_op jit(solution)/shard_map/ppermute | solution.py:26
  263.9 29.6 %collective-permute-start.23 = (f32[128,256]{0,1:T(8,128)S(1)}, f32[128,256]{0,1:T(8,128)S(1)}, u32[]{:S(2)}, u32[]{:S(2)}) collective-permute-start(f32[128,256]{0,1:T(8,128)S(1)} %get-tuple-element.65), channel_id=1, source_target_pairs={{12,0},{16,4},{20,8},{24,12},{28,16},{32,20},{36,24},{40,28},{44,3... | collective-permute-start | bytes 393224 | tf_op jit(solution)/shard_map/ppermute | solution.py:26
  268.3 29.2 %collective-permute-start.22 = (f32[128,256]{0,1:T(8,128)S(1)}, f32[128,256]{0,1:T(8,128)S(1)}, u32[]{:S(2)}, u32[]{:S(2)}) collective-permute-start(f32[128,256]{0,1:T(8,128)S(1)} %get-tuple-element.66), channel_id=1, source_target_pairs={{8,0},{12,4},{16,8},{20,12},{24,16},{28,20},{32,24},{36,28},{40,32... | collective-permute-start | bytes 393224 | tf_op jit(solution)/shard_map/ppermute | solution.py:26
  (33 other events, 448.0 us)

commit v2 on v1

--- a/solution.py
+++ b/solution.py
@@ -1,5 +1,3 @@
-import functools
-
 import jax
 import jax.numpy as jnp
 import numpy as np
@@ -7,6 +5,7 @@
 from jax.experimental import pallas as pl
 from jax.experimental.pallas import tpu as pltpu
 from jax.sharding import PartitionSpec as P
+
 
 HQ = 32
 KVH = 4
@@ -31,10 +30,6 @@
     return lax.ppermute(block, "head", [(i, (i + distance) % count) for i in range(count)])
 
 
-def spec():
-    return pl.BlockSpec(memory_space=pltpu.VMEM)
-
-
 def dot_nt(a, b):
     return lax.dot_general(a, b, (((1,), (1,)), ((), ())), preferred_element_type=F32)
 
@@ -59,6 +54,10 @@
 
 
 def call(kernel, head, ins, outs, scratch=()):
+    return launched(kernel, head, ins, outs, scratch)
+
+
+def launched(kernel, head, ins, outs, scratch):
     arrays = [a for a, _ in ins]
     return pl.pallas_call(
         kernel,
@@ -87,10 +86,11 @@
     where_e = lax.broadcasted_iota(jnp.int32, (experts, count), 0)
     hits = jnp.zeros((experts, count), F32)
     chance = jnp.zeros((experts, count), F32)
+    weights = probs[...].astype(F32)
     for k in range(ids.shape[0]):
         hit = ids[k : k + 1, :] == where_e
         hits = jnp.where(hit, 1.0, hits)
-        chance = jnp.where(hit, probs[k : k + 1, :], chance)
+        chance = jnp.where(hit, weights[k : k + 1, :], chance)
     first = lax.broadcasted_iota(jnp.int32, (count, count), 0)
     second = lax.broadcasted_iota(jnp.int32, (count, count), 1)
     before = jnp.where(first < second, 1.0, 0.0).astype(BF)
@@ -195,16 +195,22 @@
         hidden_ref[at, :] = (active * up).astype(BF)
 
 
-def grad_kernel(head, *refs):
-    blocks, downs = refs[0:8], refs[8:12]
-    act, slope, gate_far, up_far = refs[12:16]
-    gg_ref, ug_ref, far_low, far_high = refs[16:]
-    for e, far in ((0, far_low), (1, far_high)):
+def near_kernel(head, *refs):
+    blocks, downs, got_ref = refs[0:6], refs[6:9], refs[9]
+    for e in range(LOCAL):
         rows = blocks[e].shape[0]
         got = dot_nt(blocks[e][...], downs[0][e])
-        for q in range(1, 4):
+        for q in range(1, 3):
             got = got + dot_nt(blocks[2 * q + e][...], downs[q][e])
+        got_ref[pl.ds(e * rows, rows), :] = got
+
+
+def grad_kernel(head, low, high, down, got_near, act, slope, gate_far, up_far, *outs):
+    gg_ref, ug_ref, far_low, far_high = outs
+    for e, block, far in ((0, low, far_low), (1, high, far_high)):
+        rows = block.shape[0]
         at = pl.ds(e * rows, rows)
+        got = got_near[at, :] + dot_nt(block[...], down[e])
         gg = (got * slope[at, :]).astype(BF)
         ug = (got * act[at, :]).astype(BF)
         gg_ref[at, :] = gg
@@ -249,11 +255,24 @@
     return [low, high, right_low, right_high, left_low, left_high, far_low, far_high]
 
 
+def join_kernel(head, *refs):
+    parts, result = refs[:4], refs[4]
+    width = parts[0].shape[1]
+    for part, offset in zip(parts, (0, 3, 1, 2)):
+        col = pl.multiple_of(((head[0] + offset) % 4) * width, width)
+        result[:, pl.ds(col, width)] = part[...]
+
+
+def exchange(send, count):
+    half = send.shape[1]
+    return lax.all_to_all(
+        send.reshape(count, GROUP, half), "ctx", split_axis=0, concat_axis=0, tiled=True
+    ).reshape(count * GROUP, half)
+
+
 def dispatch(send, head, count, lanes):
     half = send.shape[1]
-    recv = lax.all_to_all(
-        send.reshape(count, GROUP, half), "ctx", split_axis=0, concat_axis=0, tiled=True
-    ).reshape(count * GROUP, half)
+    recv = exchange(send, count)
     low, high = call(
         untangle_kernel,
         head,
@@ -344,14 +363,13 @@
         head,
         [
             full(expert_ids.T),
-            full(gate_probs.T.astype(F32)),
+            full(gate_probs.T),
             full(pattern_table(tok_count)),
             (tokens, column_block(tokens.shape, 0)),
         ],
         [out((slots, half), BF), out((slots, 2 * tok_count), BF), out((slots, 2 * tok_count), BF)],
         [pltpu.VMEM((experts, tok_count), F32), pltpu.VMEM((experts, tok_count), F32)],
     )
-    send_rows, kv_blocks = lax.optimization_barrier((send_rows, kv_blocks))
     (send_grads,) = call(
         select_kernel,
         head,
@@ -375,12 +393,17 @@
             out((2 * rows, hidden_local), BF),
         ],
     )
+    (got_near,) = call(
+        near_kernel,
+        head,
+        [full(b) for b in grad_blocks[:6]] + [down_at(o) for o in order[:3]],
+        [out((2 * rows, hidden_local), F32)],
+    )
     gg, ug, far_low, far_high = call(
         grad_kernel,
         head,
-        [full(b) for b in grad_blocks]
-        + [down_at(o) for o in order]
-        + [full(act), full(slope), gate_at(2), up_at(2)],
+        [full(b) for b in grad_blocks[6:]]
+        + [down_at(2), full(got_near), full(act), full(slope), gate_at(2), up_at(2)],
         [
             out((2 * rows, hidden_local), BF),
             out((2 * rows, hidden_local), BF),
@@ -413,12 +436,11 @@
         [out((slots, half), BF)],
         [[pltpu.VMEM((slots, lanes), F32) for _ in range(half // lanes)]],
     )
-    returned = lax.all_to_all(
-        send_back.reshape(count, GROUP, half), "ctx", split_axis=0, concat_axis=0, tiled=True
-    ).reshape(slots, half)
+    returned = exchange(send_back, count)
     summed = dot_tn(pick, returned)
     token_part = jnp.concatenate([summed[:tok_count], summed[tok_count:]], axis=1).astype(BF)
-    grad_tokens = lax.all_gather(token_part, "head", axis=1, tiled=True)
+    parts = [token_part] + [turned(token_part, distance) for distance in (1, 3, 2)]
+    (grad_tokens,) = call(join_kernel, head, [full(p) for p in parts], [out(tokens.shape, BF)])
 
     weight_out = out(w_gate.shape, BF)
     grad_gate, grad_up = call(

time: 328 us -> 298 us (0.909)
  blocking collectives: 13.6 us -> 0 us
  waiting for transfers between devices: 163 us -> 151 us
  starting transfers between devices: 78.2 us -> 72.4 us
    ppermute x6, waiting for transfers between devices: 49.2 us -> 23.1 us  [passed_along(): return lax.ppermute(block, axis, route)]
    all_to_all x3, waiting for transfers between devices: 28.3 us -> 53.7 us  [exchange(): lax.all_to_all(send.reshape(count, GROUP, half), 'ctx', split_axis=0, con...]
    all_gather x1 -> x0, blocking collectives: 13.6 us -> none  [body(): grad_tokens = lax.all_gather(token_part, 'head', axis=1, tiled=True)]
    ppermute x18 -> x21, waiting for transfers between devices: 85.2 us -> 74 us  [turned(): lax.ppermute(block, 'head', [(i, (i + distance) % count) for i in range(c...]
    ppermute x6, starting transfers between devices: 20.7 us -> 15.9 us  [passed_along(): return lax.ppermute(block, axis, route)]
    pallas_call x10 -> x12, Pallas kernels: 52.6 us -> 55.4 us  [launched(): pl.pallas_call(kernel, grid_spec=pltpu.PrefetchScalarGridSpec(num_scalar_...]
    unnamed x67 -> x64, local copies, waits for them, and re-layouts: 7.83 us -> 8.51 us
    ppermute x18 -> x21, starting transfers between devices: 29.3 us -> 29.5 us  [turned(): lax.ppermute(block, 'head', [(i, (i + distance) % count) for i in range(c...]
  transfers between devices with their start and end apart: 27 -> 30, of which waited for: 18 -> 14; matrix products, arithmetic and copies ran while one was open for 4% -> 3% of each run, Pallas kernels for 10% -> 15%
where the time goes in v2:
time: 298 us; the launch traced here: 296 us
  waiting for transfers between devices  151 us (51%)
  starting transfers between devices  72.4 us (24%)
  Pallas kernels  55.4 us (19%)
  local copies, waits for them, and re-layouts  9.07 us (3%)
  other arithmetic  4.52 us (2%)
  matrix products  3.27 us (1%)
    ppermute x21, waiting for transfers between devices, turned(): lax.ppermute(block, 'head', [(i, (i + distance) % count) for i in range(c...  74 us
    pallas_call x12, Pallas kernels, launched(): pl.pallas_call(kernel, grid_spec=pltpu.PrefetchScalarGridSpec(num_scalar_...  55.4 us
    all_to_all x3, waiting for transfers between devices, exchange(): lax.all_to_all(send.reshape(count, GROUP, half), 'ctx', split_axis=0, con...  53.7 us
    ppermute x21, starting transfers between devices, turned(): lax.ppermute(block, 'head', [(i, (i + distance) % count) for i in range(c...  29.5 us
    all_to_all x3, starting transfers between devices, exchange(): lax.all_to_all(send.reshape(count, GROUP, half), 'ctx', split_axis=0, con...  27 us
    ppermute x6, waiting for transfers between devices, passed_along(): return lax.ppermute(block, axis, route)  23.1 us
    ppermute x6, starting transfers between devices, passed_along(): return lax.ppermute(block, axis, route)  15.9 us
    unnamed x64, local copies, waits for them, and re-layouts  8.51 us
  transfers between devices with their start and end apart: 30, of which 14 were waited for; matrix products, arithmetic and copies ran while one was open for 3% of the time, Pallas kernels for 15%

profile of v2, /device:TPU:48, one launch (start us, length us, event | category | flops | bytes accessed | tf_op | source)
XLA Modules:
  0.0 296.4 jit_solution(4318307806152294191)
XLA Ops:
  0.6 4.2 %shard_map.189 = (bf16[2560,256]{1,0:T(8,128)(2,1)}, bf16[2560,256]{1,0:T(8,128)(2,1)}, bf16[2560,256]{1,0:T(8,128)(2,1)}) custom-call(s32[1]{0:T(128)} %bitcast.2.head, s32[8,128]{1,0:T(8,128)} %bitcast.96, bf16[8,128]{1,0:T(8,128)(2,1)} %bitcast.97, f32[3,80,128]{2,1,0:T(8,128)} %constant.32.clone.pattern, bf16[128,2048]{1,0:T(8,128)(2,1)} %tok.2), custom_call_target="tpu_custom_call" | custom-call | tf_op jit(solution)/shard_map/pallas_call | solution.py:62
  4.8 11.6 %all-to-all-start.1 = ((bf16[64,40,256]{2,1,0:T(8,128)(2,1)}), bf16[64,40,256]{2,1,0:T(8,128)(2,1)S(1)}, u32[]{:S(2)}, u32[]{:S(2)}) async-start(bf16[64,40,256]{2,1,0:T(8,128)(2,1)} %bitcast.91), calls=%async_computation.1 | async-start | bytes 2621440 | tf_op jit(solution)/shard_map/all_to_all | solution.py:268
  19.4 29.9 %all-to-all-done.1 = bf16[64,40,256]{2,1,0:T(8,128)(2,1)S(1)} async-done(((bf16[64,40,256]{2,1,0:T(8,128)(2,1)}), bf16[64,40,256]{2,1,0:T(8,128)(2,1)S(1)}, u32[]{:S(2)}, u32[]{:S(2)}) %all-to-all-start.1) | async-done | bytes 1310752 | tf_op jit(solution)/shard_map/all_to_all | solution.py:268
  49.3 7.5 %all-to-all-start = ((bf16[64,40,256]{2,1,0:T(8,128)(2,1)}), bf16[64,40,256]{2,1,0:T(8,128)(2,1)S(1)}, u32[]{:S(2)}, u32[]{:S(2)}) async-start(bf16[64,40,256]{2,1,0:T(8,128)(2,1)} %bitcast.84), calls=%async_computation | async-start | bytes 2621440 | tf_op jit(solution)/shard_map/all_to_all | solution.py:268
  65.9 23.7 %all-to-all-done = bf16[64,40,256]{2,1,0:T(8,128)(2,1)S(1)} async-done(((bf16[64,40,256]{2,1,0:T(8,128)(2,1)}), bf16[64,40,256]{2,1,0:T(8,128)(2,1)S(1)}, u32[]{:S(2)}, u32[]{:S(2)}) %all-to-all-start) | async-done | bytes 1310752 | tf_op jit(solution)/shard_map/all_to_all | solution.py:268
  99.9 12.1 %collective-permute-done.5.refs_4_ = bf16[640,512]{1,0:T(8,128)(2,1)S(1)} collective-permute-done((bf16[640,512]{1,0:T(8,128)(2,1)}, bf16[640,512]{1,0:T(8,128)(2,1)S(1)}, u32[]{:S(2)}, u32[]{:S(2)}) %collective-permute-start.5) | collective-permute-done | bytes 655392 | tf_op jit(solution)/shard_map/ppermute | solution.py:30
  115.6 13.9 %collective-permute-done.4.refs_3_ = bf16[640,512]{1,0:T(8,128)(2,1)S(1)} collective-permute-done((bf16[640,512]{1,0:T(8,128)(2,1)}, bf16[640,512]{1,0:T(8,128)(2,1)S(1)}, u32[]{:S(2)}, u32[]{:S(2)}) %collective-permute-start.4) | collective-permute-done | bytes 655392 | tf_op jit(solution)/shard_map/ppermute | solution.py:30
  132.8 4.7 %shard_map.192.got_near = f32[1280,192]{1,0:T(8,128)} custom-call(s32[1]{0:T(128)} %bitcast.2.head, bf16[640,512]{1,0:T(8,128)(2,1)} %get-tuple-element.30.refs_0_, bf16[640,512]{1,0:T(8,128)(2,1)} %get-tuple-element.31.refs_1_, bf16[640,512]{1,0:T(8,128)(2,1)} %copy-done.6, bf16[640,512]{1,0:T(8,128)(2,1)} %copy-done.7, bf16[640,512]{1,0:T(8,128)(2,1)} %copy-done.5, ...), custom_call_target="tpu_custom_call" | custom-call | tf_op jit(solution)/shard_map/pallas_call | solution.py:62
  137.5 6.1 %collective-permute-done.7.refs_3_ = bf16[640,512]{1,0:T(8,128)(2,1)S(1)} collective-permute-done((bf16[640,512]{1,0:T(8,128)(2,1)}, bf16[640,512]{1,0:T(8,128)(2,1)S(1)}, u32[]{:S(2)}, u32[]{:S(2)}) %collective-permute-start.7) | collective-permute-done | bytes 655392 | tf_op jit(solution)/shard_map/ppermute | solution.py:30
  143.6 14.0 %collective-permute-done.10.refs_6_ = bf16[640,512]{1,0:T(8,128)(2,1)S(1)} collective-permute-done((bf16[640,512]{1,0:T(8,128)(2,1)S(1)}, bf16[640,512]{1,0:T(8,128)(2,1)S(1)}, u32[]{:S(2)}, u32[]{:S(2)}) %collective-permute-start.10) | collective-permute-done | bytes 655392 | tf_op jit(solution)/shard_map/ppermute | solution.py:30
  159.3 8.1 %shard_map.194 = (f32[1280,192]{1,0:T(8,128)}, f32[1280,192]{1,0:T(8,128)}, bf16[1280,192]{1,0:T(8,128)(2,1)}) custom-call(s32[1]{0:T(128)} %bitcast.2.head, bf16[640,512]{1,0:T(8,128)(2,1)} %get-tuple-element.33.refs_0_, bf16[640,512]{1,0:T(8,128)(2,1)} %get-tuple-element.34.refs_1_, bf16[640,512]{1,0:T(8,128)(2,1)} %copy-done.3, ...), custom_call_target="tpu_custom_call" | custom-call | tf_op jit(solution)/shard_map/pallas_call | solution.py:62
  167.4 3.5 %collective-permute-done.1.low.refs_6_ = bf16[640,512]{1,0:T(8,128)(2,1)S(1)} collective-permute-done((bf16[640,512]{1,0:T(8,128)(2,1)S(1)}, bf16[640,512]{1,0:T(8,128)(2,1)S(1)}, u32[]{:S(2)}, u32[]{:S(2)}) %collective-permute-start.1) | collective-permute-done | bytes 655392 | tf_op jit(solution)/shard_map/ppermute | solution.py:30
  172.0 5.2 %shard_map.195 = (bf16[1280,192]{1,0:T(8,128)(2,1)}, bf16[1280,192]{1,0:T(8,128)(2,1)}, bf16[640,512]{1,0:T(8,128)(2,1)}, bf16[640,512]{1,0:T(8,128)(2,1)}) custom-call(s32[1]{0:T(128)} %bitcast.2.head, bf16[640,512]{1,0:T(8,128)(2,1)} %copy-done.11, bf16[640,512]{1,0:T(8,128)(2,1)} %copy-done.13, bf16[2,192,2048]{2,1,0:T(8,128)(2,1)} %down.1, ...), custom_call_target="tpu_custom_call" | custom-call | tf_op jit(solution)/shard_map/pallas_call | solution.py:62
  180.4 5.7 %shard_map.196 = (f32[640,512]{1,0:T(8,128)}, bf16[640,512]{1,0:T(8,128)(2,1)}, bf16[640,512]{1,0:T(8,128)(2,1)}, f32[640,512]{1,0:T(8,128)}, f32[1280,512]{1,0:T(8,128)}) custom-call(s32[1]{0:T(128)} %bitcast.2.head, bf16[1280,192]{1,0:T(8,128)(2,1)} %get-tuple-element.37.gg.refs_8_, bf16[1280,192]{1,0:T(8,128)(2,1)} %get-tuple-element.38.ug.refs_9_, ...), custom_call_target="tpu_custom_call" | custom-call | tf_op jit(solution)/shard_map/pallas_call | solution.py:62
  189.3 6.9 %collective-permute-done.13 = bf16[640,512]{1,0:T(8,128)(2,1)S(1)} collective-permute-done((bf16[640,512]{1,0:T(8,128)(2,1)}, bf16[640,512]{1,0:T(8,128)(2,1)S(1)}, u32[]{:S(2)}, u32[]{:S(2)}) %collective-permute-start.13) | collective-permute-done | bytes 655392 | tf_op jit(solution)/shard_map/ppermute | solution.py:30
  203.6 6.7 %collective-permute-done.12.left_a = bf16[640,512]{1,0:T(8,128)(2,1)S(1)} collective-permute-done((bf16[640,512]{1,0:T(8,128)(2,1)}, bf16[640,512]{1,0:T(8,128)(2,1)S(1)}, u32[]{:S(2)}, u32[]{:S(2)}) %collective-permute-start.12) | collective-permute-done | bytes 655392 | tf_op jit(solution)/shard_map/ppermute | solution.py:30
  214.4 8.3 %collective-permute-done.14.left_b = bf16[640,512]{1,0:T(8,128)(2,1)S(1)} collective-permute-done((bf16[640,512]{1,0:T(8,128)(2,1)S(1)}, bf16[640,512]{1,0:T(8,128)(2,1)S(1)}, u32[]{:S(2)}, u32[]{:S(2)}) %collective-permute-start.14) | collective-permute-done | bytes 655392 | tf_op jit(solution)/shard_map/ppermute | solution.py:30
  223.5 4.4 %shard_map.197 = bf16[2560,256]{1,0:T(8,128)(2,1)} custom-call(s32[1]{0:T(128)} %bitcast.2.head, f32[1280,512]{1,0:T(8,128)} %get-tuple-element.39.own, bf16[640,512]{1,0:T(8,128)(2,1)} %copy-done.16, bf16[640,512]{1,0:T(8,128)(2,1)} %copy-done.18, bf16[640,512]{1,0:T(8,128)(2,1)} %copy-done.17, bf16[640,512]{1,0:T(8,128)(2,1)} %collective-permute-done.17.right_b), custom_call_target="tpu_custom_call" | custom-call | tf_op jit(solution)/shard_map/pallas_call | solution.py:62
  227.9 7.8 %all-to-all-start.2 = ((bf16[64,40,256]{2,1,0:T(8,128)(2,1)}), bf16[64,40,256]{2,1,0:T(8,128)(2,1)S(1)}, u32[]{:S(2)}, u32[]{:S(2)}) async-start(bf16[64,40,256]{2,1,0:T(8,128)(2,1)} %bitcast.86), calls=%async_computation.2 | async-start | bytes 2621440 | tf_op jit(solution)/shard_map/all_to_all | solution.py:268
  242.6 4.4 %collective-permute-start.26 = (f32[128,256]{0,1:T(8,128)}, f32[128,256]{0,1:T(8,128)}, u32[]{:S(2)}, u32[]{:S(2)}) collective-permute-start(f32[128,256]{0,1:T(8,128)} %get-tuple-element.57), channel_id=1, source_target_pairs={{12,0},{16,4},{20,8},{24,12},{28,16},{32,20},{36,24},{40,28},{44,3... | collective-permute-start | bytes 393224 | tf_op jit(solution)/shard_map/ppermute | solution.py:25
  251.6 16.1 %collective-permute-done.24 = f32[128,256]{0,1:T(8,128)S(1)} collective-permute-done((f32[128,256]{0,1:T(8,128)}, f32[128,256]{0,1:T(8,128)S(1)}, u32[]{:S(2)}, u32[]{:S(2)}) %collective-permute-start.24) | collective-permute-done | bytes 131104 | tf_op jit(solution)/shard_map/ppermute | solution.py:25
  270.6 4.0 %collective-permute-done.25 = f32[128,256]{0,1:T(8,128)} collective-permute-done((f32[128,256]{0,1:T(8,128)}, f32[128,256]{0,1:T(8,128)}, u32[]{:S(2)}, u32[]{:S(2)}) %collective-permute-start.25) | collective-permute-done | bytes 131104 | tf_op jit(solution)/shard_map/ppermute | solution.py:25
  280.9 7.0 %shard_map.199 = (bf16[2,192,2048]{2,1,0:T(8,128)(2,1)}, bf16[2,192,2048]{2,1,0:T(8,128)(2,1)}) custom-call(s32[1]{0:T(128)} %bitcast.2.head, bf16[640,512]{1,0:T(8,128)(2,1)} %get-tuple-element.33.refs_0_, bf16[640,512]{1,0:T(8,128)(2,1)} %get-tuple-element.34.refs_1_, bf16[640,512]{1,0:T(8,128)(2,1)} %copy-done.3, bf16[640,512]{1,0:T(8,128)(2,1)} %copy-done.9, ...), custom_call_target="tpu_custom_call" | custom-call | tf_op jit(solution)/shard_map/pallas_call | solution.py:62
  287.9 5.2 %shard_map.200 = bf16[2,192,2048]{2,1,0:T(8,128)(2,1)} custom-call(s32[1]{0:T(128)} %bitcast.2.head, bf16[640,512]{1,0:T(8,128)(2,1)} %get-tuple-element.30.refs_0_, bf16[640,512]{1,0:T(8,128)(2,1)} %get-tuple-element.31.refs_1_, bf16[640,512]{1,0:T(8,128)(2,1)} %copy-done.6, bf16[640,512]{1,0:T(8,128)(2,1)} %copy-done.7, bf16[640,512]{1,0:T(8,128)(2,1)} %copy-done.5, ...), custom_call_target="tpu_custom_call" | custom-call | tf_op jit(solution)/shard_map/pallas_call | solution.py:62
  (136 shorter events, 74.3 us)
Async XLA Ops:
  4.8 44.5 %all-to-all-start.1 = ((bf16[64,40,256]{2,1,0:T(8,128)(2,1)}), bf16[64,40,256]{2,1,0:T(8,128)(2,1)S(1)}, u32[]{:S(2)}, u32[]{:S(2)}) async-start(bf16[64,40,256]{2,1,0:T(8,128)(2,1)} %bitcast.91), calls=%async_computation.1 | async-start | bytes 2621440 | tf_op jit(solution)/shard_map/all_to_all | solution.py:268
  49.3 40.3 %all-to-all-start = ((bf16[64,40,256]{2,1,0:T(8,128)(2,1)}), bf16[64,40,256]{2,1,0:T(8,128)(2,1)S(1)}, u32[]{:S(2)}, u32[]{:S(2)}) async-start(bf16[64,40,256]{2,1,0:T(8,128)(2,1)} %bitcast.84), calls=%async_computation | async-start | bytes 2621440 | tf_op jit(solution)/shard_map/all_to_all | solution.py:268
  59.9 36.6 %collective-permute-start.8 = (bf16[640,512]{1,0:T(8,128)(2,1)}, bf16[640,512]{1,0:T(8,128)(2,1)S(1)}, u32[]{:S(2)}, u32[]{:S(2)}) collective-permute-start(bf16[640,512]{1,0:T(8,128)(2,1)} %get-tuple-element.33.refs_0_), channel_id=1, source_target_pairs={{0,3},{1,0},{2,1},{3,2},{4,7},{5,4},{6,5},{7,6},{8,11},{9,8},{10,9... | collective-permute-start | bytes 1966088 | tf_op jit(solution)/shard_map/ppermute | solution.py:30
  62.7 34.6 %collective-permute-start.6 = (bf16[640,512]{1,0:T(8,128)(2,1)}, bf16[640,512]{1,0:T(8,128)(2,1)S(1)}, u32[]{:S(2)}, u32[]{:S(2)}) collective-permute-start(bf16[640,512]{1,0:T(8,128)(2,1)} %get-tuple-element.33.refs_0_), channel_id=1, source_target_pairs={{0,1},{1,2},{2,3},{3,0},{4,5},{5,6},{6,7},{7,4},{8,9},{9,10},{10,1... | collective-permute-start | bytes 1966088 | tf_op jit(solution)/shard_map/ppermute | solution.py:30
  62.7 37.2 %collective-permute-start.9 = (bf16[640,512]{1,0:T(8,128)(2,1)}, bf16[640,512]{1,0:T(8,128)(2,1)S(1)}, u32[]{:S(2)}, u32[]{:S(2)}) collective-permute-start(bf16[640,512]{1,0:T(8,128)(2,1)} %get-tuple-element.34.refs_1_), channel_id=1, source_target_pairs={{0,3},{1,0},{2,1},{3,2},{4,7},{5,4},{6,5},{7,6},{8,11},{9,8},{10,9... | collective-permute-start | bytes 1966088 | tf_op jit(solution)/shard_map/ppermute | solution.py:30
  96.5 33.1 %collective-permute-start.4 = (bf16[640,512]{1,0:T(8,128)(2,1)}, bf16[640,512]{1,0:T(8,128)(2,1)S(1)}, u32[]{:S(2)}, u32[]{:S(2)}) collective-permute-start(bf16[640,512]{1,0:T(8,128)(2,1)} %get-tuple-element.31.refs_1_), channel_id=1, source_target_pairs={{0,1},{1,2},{2,3},{3,0},{4,5},{5,6},{6,7},{7,4},{8,9},{9,10},{10,1... | collective-permute-start | bytes 1966088 | tf_op jit(solution)/shard_map/ppermute | solution.py:30
  97.3 32.3 %collective-permute-start.2 = (bf16[640,512]{1,0:T(8,128)(2,1)}, bf16[640,512]{1,0:T(8,128)(2,1)S(1)}, u32[]{:S(2)}, u32[]{:S(2)}) collective-permute-start(bf16[640,512]{1,0:T(8,128)(2,1)} %get-tuple-element.31.refs_1_), channel_id=1, source_target_pairs={{0,3},{1,0},{2,1},{3,2},{4,7},{5,4},{6,5},{7,6},{8,11},{9,8},{10,9... | collective-permute-start | bytes 1966088 | tf_op jit(solution)/shard_map/ppermute | solution.py:30
  99.9 43.8 %collective-permute-start.7 = (bf16[640,512]{1,0:T(8,128)(2,1)}, bf16[640,512]{1,0:T(8,128)(2,1)S(1)}, u32[]{:S(2)}, u32[]{:S(2)}) collective-permute-start(bf16[640,512]{1,0:T(8,128)(2,1)} %get-tuple-element.34.refs_1_), channel_id=1, source_target_pairs={{0,1},{1,2},{2,3},{3,0},{4,5},{5,6},{6,7},{7,4},{8,9},{9,10},{10,1... | collective-permute-start | bytes 1966088 | tf_op jit(solution)/shard_map/ppermute | solution.py:30
  111.9 45.7 %collective-permute-start.10 = (bf16[640,512]{1,0:T(8,128)(2,1)S(1)}, bf16[640,512]{1,0:T(8,128)(2,1)S(1)}, u32[]{:S(2)}, u32[]{:S(2)}) collective-permute-start(bf16[640,512]{1,0:T(8,128)(2,1)S(1)} %collective-permute-done.6.refs_2_), channel_id=1, source_target_pairs={{0,1},{1,2},{2,3},{3,0},{4,5},{5,6},{6,7},{7,4},{8,9},{9,10},{10,1... | collective-permute-start | bytes 1966088 | tf_op jit(solution)/shard_map/ppermute | solution.py:30
  115.5 42.1 %collective-permute-start.11 = (bf16[640,512]{1,0:T(8,128)(2,1)S(1)}, bf16[640,512]{1,0:T(8,128)(2,1)S(1)}, u32[]{:S(2)}, u32[]{:S(2)}) collective-permute-start(bf16[640,512]{1,0:T(8,128)(2,1)S(1)} %collective-permute-done.9.refs_5_), channel_id=1, source_target_pairs={{0,3},{1,0},{2,1},{3,2},{4,7},{5,4},{6,5},{7,6},{8,11},{9,8},{10,9... | collective-permute-start | bytes 1966088 | tf_op jit(solution)/shard_map/ppermute | solution.py:30
  129.6 41.3 %collective-permute-start.1 = (bf16[640,512]{1,0:T(8,128)(2,1)S(1)}, bf16[640,512]{1,0:T(8,128)(2,1)S(1)}, u32[]{:S(2)}, u32[]{:S(2)}) collective-permute-start(bf16[640,512]{1,0:T(8,128)(2,1)S(1)} %collective-permute-done.refs_2_), channel_id=1, source_target_pairs={{0,1},{1,2},{2,3},{3,0},{4,5},{5,6},{6,7},{7,4},{8,9},{9,10},{10,1... | collective-permute-start | bytes 1966088 | tf_op jit(solution)/shard_map/ppermute | solution.py:30
  129.6 41.3 %collective-permute-start.3 = (bf16[640,512]{1,0:T(8,128)(2,1)S(1)}, bf16[640,512]{1,0:T(8,128)(2,1)S(1)}, u32[]{:S(2)}, u32[]{:S(2)}) collective-permute-start(bf16[640,512]{1,0:T(8,128)(2,1)S(1)} %collective-permute-done.2.refs_5_), channel_id=1, source_target_pairs={{0,3},{1,0},{2,1},{3,2},{4,7},{5,4},{6,5},{7,6},{8,11},{9,8},{10,9... | collective-permute-start | bytes 1966088 | tf_op jit(solution)/shard_map/ppermute | solution.py:30
  177.2 20.7 %collective-permute-start.16 = (bf16[640,512]{1,0:T(8,128)(2,1)}, bf16[640,512]{1,0:T(8,128)(2,1)S(1)}, u32[]{:S(2)}, u32[]{:S(2)}) collective-permute-start(bf16[640,512]{1,0:T(8,128)(2,1)} %get-tuple-element.45), channel_id=1, source_target_pairs={{0,3},{1,0},{2,1},{3,2},{4,7},{5,4},{6,5},{7,6},{8,11},{9,8},{10,9... | collective-permute-start | bytes 1966088 | tf_op jit(solution)/shard_map/ppermute | solution.py:30
  186.1 24.2 %collective-permute-start.12 = (bf16[640,512]{1,0:T(8,128)(2,1)}, bf16[640,512]{1,0:T(8,128)(2,1)S(1)}, u32[]{:S(2)}, u32[]{:S(2)}) collective-permute-start(bf16[640,512]{1,0:T(8,128)(2,1)} %get-tuple-element.40), channel_id=1, source_target_pairs={{0,1},{1,2},{2,3},{3,0},{4,5},{5,6},{6,7},{7,4},{8,9},{9,10},{10,1... | collective-permute-start | bytes 1966088 | tf_op jit(solution)/shard_map/ppermute | solution.py:30
  186.1 26.1 %collective-permute-start.15 = (bf16[640,512]{1,0:T(8,128)(2,1)}, bf16[640,512]{1,0:T(8,128)(2,1)S(1)}, u32[]{:S(2)}, u32[]{:S(2)}) collective-permute-start(bf16[640,512]{1,0:T(8,128)(2,1)} %get-tuple-element.43), channel_id=1, source_target_pairs={{0,3},{1,0},{2,1},{3,2},{4,7},{5,4},{6,5},{7,6},{8,11},{9,8},{10,9... | collective-permute-start | bytes 1966088 | tf_op jit(solution)/shard_map/ppermute | solution.py:30
  197.8 24.9 %collective-permute-start.14 = (bf16[640,512]{1,0:T(8,128)(2,1)S(1)}, bf16[640,512]{1,0:T(8,128)(2,1)S(1)}, u32[]{:S(2)}, u32[]{:S(2)}) collective-permute-start(bf16[640,512]{1,0:T(8,128)(2,1)S(1)} %add_convert_fusion.1), channel_id=1, source_target_pairs={{0,1},{1,2},{2,3},{3,0},{4,5},{5,6},{6,7},{7,4},{8,9},{9,10},{10,1... | collective-permute-start | bytes 1966088 | tf_op jit(solution)/shard_map/ppermute | solution.py:30
  198.1 24.5 %collective-permute-start.17 = (bf16[640,512]{1,0:T(8,128)(2,1)S(1)}, bf16[640,512]{1,0:T(8,128)(2,1)}, u32[]{:S(2)}, u32[]{:S(2)}) collective-permute-start(bf16[640,512]{1,0:T(8,128)(2,1)S(1)} %add_convert_fusion), channel_id=1, source_target_pairs={{0,3},{1,0},{2,1},{3,2},{4,7},{5,4},{6,5},{7,6},{8,11},{9,8},{10,9... | collective-permute-start | bytes 1966088 | tf_op jit(solution)/shard_map/ppermute | solution.py:30
  201.5 35.3 %collective-permute-start.23 = (bf16[128,256]{1,0:T(8,128)(2,1)S(1)}, bf16[128,256]{1,0:T(8,128)(2,1)S(1)}, u32[]{:S(2)}, u32[]{:S(2)}) collective-permute-start(bf16[128,256]{1,0:T(8,128)(2,1)S(1)} %constant_dynamic-update-slice_fusion), channel_id=1, source_target_pairs={{0,4},{4,8},{8,12},{12,16},{16,20},{20,24},{24,28},{28,32},{32,36}... | collective-permute-start | bytes 196616 | tf_op jit(solution)/shard_map/ppermute | solution.py:25
  210.3 26.5 %collective-permute-start.22 = (bf16[128,256]{1,0:T(8,128)(2,1)S(1)}, bf16[128,256]{1,0:T(8,128)(2,1)S(1)}, u32[]{:S(2)}, u32[]{:S(2)}) collective-permute-start(bf16[128,256]{1,0:T(8,128)(2,1)S(1)} %constant_dynamic-update-slice_fusion), channel_id=1, source_target_pairs={{0,8},{4,12},{8,16},{12,20},{16,24},{20,28},{24,32},{28,36},{32,40... | collective-permute-start | bytes 196616 | tf_op jit(solution)/shard_map/ppermute | solution.py:25
  212.2 24.6 %collective-permute-start.21 = (bf16[128,256]{1,0:T(8,128)(2,1)S(1)}, bf16[128,256]{1,0:T(8,128)(2,1)S(1)}, u32[]{:S(2)}, u32[]{:S(2)}) collective-permute-start(bf16[128,256]{1,0:T(8,128)(2,1)S(1)} %constant_dynamic-update-slice_fusion), channel_id=1, source_target_pairs={{0,12},{4,16},{8,20},{12,24},{16,28},{20,32},{24,36},{28,40},{32,4... | collective-permute-start | bytes 196616 | tf_op jit(solution)/shard_map/ppermute | solution.py:25
  227.9 47.8 %all-to-all-start.2 = ((bf16[64,40,256]{2,1,0:T(8,128)(2,1)}), bf16[64,40,256]{2,1,0:T(8,128)(2,1)S(1)}, u32[]{:S(2)}, u32[]{:S(2)}) async-start(bf16[64,40,256]{2,1,0:T(8,128)(2,1)} %bitcast.86), calls=%async_computation.2 | async-start | bytes 2621440 | tf_op jit(solution)/shard_map/all_to_all | solution.py:268
  240.4 27.2 %collective-permute-start.24 = (f32[128,256]{0,1:T(8,128)}, f32[128,256]{0,1:T(8,128)S(1)}, u32[]{:S(2)}, u32[]{:S(2)}) collective-permute-start(f32[128,256]{0,1:T(8,128)} %get-tuple-element.56), channel_id=1, source_target_pairs={{4,0},{8,4},{12,8},{16,12},{20,16},{24,20},{28,24},{32,28},{36,32}... | collective-permute-start | bytes 393224 | tf_op jit(solution)/shard_map/ppermute | solution.py:25
  242.6 28.0 %collective-permute-start.26 = (f32[128,256]{0,1:T(8,128)}, f32[128,256]{0,1:T(8,128)}, u32[]{:S(2)}, u32[]{:S(2)}) collective-permute-start(f32[128,256]{0,1:T(8,128)} %get-tuple-element.57), channel_id=1, source_target_pairs={{12,0},{16,4},{20,8},{24,12},{28,16},{32,20},{36,24},{40,28},{44,3... | collective-permute-start | bytes 393224 | tf_op jit(solution)/shard_map/ppermute | solution.py:25
  247.0 27.6 %collective-permute-start.25 = (f32[128,256]{0,1:T(8,128)}, f32[128,256]{0,1:T(8,128)}, u32[]{:S(2)}, u32[]{:S(2)}) collective-permute-start(f32[128,256]{0,1:T(8,128)} %get-tuple-element.58), channel_id=1, source_target_pairs={{8,0},{12,4},{16,8},{20,12},{24,16},{28,20},{32,24},{36,28},{40,32... | collective-permute-start | bytes 393224 | tf_op jit(solution)/shard_map/ppermute | solution.py:25
  (35 other events, 421.0 us)

commit v3 on v2

--- a/solution.py
+++ b/solution.py
@@ -1,14 +1,11 @@
 import jax
 import jax.numpy as jnp
-import numpy as np
 from jax import lax
 from jax.experimental import pallas as pl
 from jax.experimental.pallas import tpu as pltpu
 from jax.sharding import PartitionSpec as P
 
 
-HQ = 32
-KVH = 4
 HD = 128
 REACH = 3
 CAP = 10
@@ -81,7 +78,7 @@
     return (jax.ShapeDtypeStruct(shape, dtype), whole(shape))
 
 
-def route_kernel(head, ids, probs, pattern, tok, rows_ref, pick_ref, scaled_ref, rank_s, prob_s):
+def route_kernel(head, ids, probs, tok, rows_ref, pick_ref, scaled_ref, rank_s, prob_s):
     experts, count = rank_s.shape
     where_e = lax.broadcasted_iota(jnp.int32, (experts, count), 0)
     hits = jnp.zeros((experts, count), F32)
@@ -97,9 +94,13 @@
     rank = dot_nn(hits.astype(BF), before)
     rank_s[...] = jnp.where(hits > 0.0, rank, -1.0)
     prob_s[...] = chance
-    which = pattern[0]
-    place = pattern[1]
-    lower = pattern[2]
+    row = lax.broadcasted_iota(jnp.int32, (2 * GROUP, count), 0)
+    run = jnp.zeros_like(row)
+    for k in range(1, 2 * GROUP // CAP):
+        run = run + jnp.where(row >= k * CAP, 1, 0)
+    place = (row - CAP * run).astype(F32)
+    which = jnp.where(run >= 2 * LOCAL, LOCAL, 0) + (run & 1)
+    in_low = (run & LOCAL) == 0
 
     def step(i, carry):
         base = i * (2 * LOCAL)
@@ -113,7 +114,6 @@
         weight = match * weight
         at = pl.multiple_of(i * 2 * GROUP, 2 * GROUP)
         zero = jnp.zeros_like(match)
-        in_low = lower > 0.0
         pick_ref[pl.ds(at, 2 * GROUP), 0:count] = jnp.where(in_low, match, zero).astype(BF)
         pick_ref[pl.ds(at, 2 * GROUP), count : 2 * count] = jnp.where(in_low, zero, match).astype(BF)
         scaled_ref[pl.ds(at, 2 * GROUP), 0:count] = jnp.where(in_low, weight, zero).astype(BF)
@@ -126,19 +126,11 @@
     rows_ref[...] = dot_nn(pick_ref[...], stacked).astype(BF)
 
 
-def select_kernel(head, scaled, tok, rows_ref):
-    half = tok.shape[1] // 2
-    stacked = jnp.concatenate([tok[:, :half], tok[:, half:]], axis=0)
-    rows_ref[...] = dot_nn(scaled[...], stacked).astype(BF)
-
-
-def pattern_table(count):
-    r = np.arange(2 * GROUP)
-    which = (r // GROUP) * LOCAL + (r % SLOTS) // CAP
-    place = r % CAP
-    lower = (r % GROUP) < SLOTS
-    table = np.stack([which, place, lower]).astype(np.float32)
-    return jnp.asarray(np.repeat(table[:, :, None], count, axis=2))
+def select_kernel(head, scaled, own, far, own_ref, far_ref):
+    for tok, ref in ((own, own_ref), (far, far_ref)):
+        half = tok.shape[1] // 2
+        stacked = jnp.concatenate([tok[:, :half], tok[:, half:]], axis=0)
+        ref[...] = dot_nn(scaled[...], stacked).astype(BF)
 
 
 def untangle_kernel(head, recv, low_ref, high_ref, wide):
@@ -245,14 +237,12 @@
                 result[e, :, pl.ds(col, width)] = part.astype(BF)
 
 
-def round_ring(low, high):
+def near_ring(low, high):
     right_low = turned(low, 1)
     left_high = turned(high, -1)
     right_high = turned(high, 1)
     left_low = turned(low, -1)
-    far_low = turned(right_low, 1)
-    far_high = turned(left_high, -1)
-    return [low, high, right_low, right_high, left_low, left_high, far_low, far_high]
+    return [low, high, right_low, right_high, left_low, left_high]
 
 
 def join_kernel(head, *refs):
@@ -280,51 +270,64 @@
         [out((count * CAP, 2 * half), BF), out((count * CAP, 2 * half), BF)],
         [[pltpu.VMEM((count * GROUP, lanes), F32) for _ in range(half // lanes)]],
     )
-    return round_ring(low, high)
-
-
-def attention(query_rows, window_kv, attn_out, grad_attn, segment_ids, kv_width):
-    att_rows = query_rows.shape[0]
-    kv_local = kv_width // HD
-    group_size = HQ // KVH
-    window = (REACH + 1) * att_rows
-    score_scale = HD ** (-0.5)
-    ctx_index = lax.axis_index("ctx")
-    window_key = window_kv[:, :kv_width].reshape(window, kv_local, HD)
-    window_value = window_kv[:, kv_width:].reshape(window, kv_local, HD)
-    query_pos = ctx_index * att_rows + jnp.arange(att_rows, dtype=jnp.int32)
-    key_pos = (ctx_index - REACH) * att_rows + jnp.arange(window, dtype=jnp.int32)
-    padded_segment = jnp.concatenate([jnp.full((REACH * att_rows,), -1, jnp.int32), segment_ids])
-    key_seg = lax.dynamic_slice_in_dim(padded_segment, ctx_index * att_rows, window, 0)
-    query_seg = lax.dynamic_slice_in_dim(segment_ids, ctx_index * att_rows, att_rows, 0)
-    visible = (key_pos[None, :] <= query_pos[:, None]) & (key_seg[None, :] == query_seg[:, None])
-    query_heads = query_rows.reshape(att_rows, kv_local, group_size, HD)
-    out_heads = attn_out.reshape(att_rows, kv_local, group_size, HD)
-    grad_heads = grad_attn.reshape(att_rows, kv_local, group_size, HD)
-    scores = (
-        jnp.einsum("ajgd,tjd->jgat", query_heads, window_key, preferred_element_type=F32)
-        * score_scale
-    )
-    row_peak = jnp.max(jnp.where(visible, scores, -jnp.inf), axis=-1, keepdims=True)
-    weights_exp = jnp.exp(jnp.where(visible, scores - row_peak, -jnp.inf))
-    probs = weights_exp / jnp.sum(weights_exp, axis=-1, keepdims=True)
-    row_delta = jnp.einsum("ajgd,ajgd->jga", grad_heads, out_heads, preferred_element_type=F32)
-    prob_grad = jnp.einsum("ajgd,tjd->jgat", grad_heads, window_value, preferred_element_type=F32)
-    score_grad = (probs * (prob_grad - row_delta[..., None])).astype(BF)
-    probs_low = probs.astype(BF)
-    grad_query = (
-        (score_scale * jnp.einsum("jgat,tjd->ajgd", score_grad, window_key, preferred_element_type=F32))
-        .astype(BF)
-        .reshape(att_rows, -1)
-    )
-    key_terms = (
-        score_scale
-        * jnp.einsum("jgat,ajgd->tjd", score_grad, query_heads, preferred_element_type=F32)
-    ).reshape(window, kv_width)
-    value_terms = jnp.einsum(
-        "jgat,ajgd->tjd", probs_low, grad_heads, preferred_element_type=F32
-    ).reshape(window, kv_width)
-    return grad_query, jnp.concatenate([key_terms, value_terms], axis=1)
+    return low, high
+
+
+def attention_kernel(head, query, out_ref, grad, kv3, kv2, kv1, kv0, query_seg, key_seg, *refs):
+    grad_query, t3, t2, t1, t0, window, key_sum, value_sum = refs
+    rows = query.shape[0]
+    span = window.shape[0]
+    scale = HD ** (-0.5)
+    for at, block in enumerate((kv3, kv2, kv1, kv0)):
+        window[at * rows : (at + 1) * rows, :] = block[...]
+    key_sum[...] = jnp.zeros_like(key_sum)
+    value_sum[...] = jnp.zeros_like(value_sum)
+    query_at = lax.broadcasted_iota(jnp.int32, (rows, span), 0) + (span - rows)
+    key_at = lax.broadcasted_iota(jnp.int32, (rows, span), 1)
+    visible = (key_at <= query_at) & (query_seg[...] == key_seg[...])
+
+    def one_head(g, carry):
+        lanes = pl.ds(pl.multiple_of(g * HD, HD), HD)
+        keys, values = window[:, :HD], window[:, HD:]
+        q, dout = query[:, lanes], grad[:, lanes]
+        scores = dot_nt(q, keys) * scale
+        peak = jnp.max(jnp.where(visible, scores, -jnp.inf), axis=1, keepdims=True)
+        weights = jnp.exp(jnp.where(visible, scores - peak, -jnp.inf))
+        probs = weights / jnp.sum(weights, axis=1, keepdims=True)
+        delta = jnp.sum(dout.astype(F32) * out_ref[:, lanes].astype(F32), axis=1, keepdims=True)
+        score_grad = (probs * (dot_nt(dout, values) - delta)).astype(BF)
+        grad_query[:, lanes] = (scale * dot_nn(score_grad, keys)).astype(BF)
+        key_sum[...] += dot_tn(score_grad, q)
+        value_sum[...] += dot_tn(probs.astype(BF), dout)
+        return carry
+
+    lax.fori_loop(0, query.shape[1] // HD, one_head, 0)
+    for at, ref in enumerate((t3, t2, t1, t0)):
+        part = pl.ds(at * rows, rows)
+        ref[:, :HD] = scale * key_sum[part, :]
+        ref[:, HD:] = value_sum[part, :]
+
+
+def attention(head, query_rows, kv_blocks, attn_out, grad_attn, segment_ids):
+    rows = query_rows.shape[0]
+    window = (REACH + 1) * rows
+    at = lax.axis_index("ctx") * rows
+    padded = jnp.concatenate([jnp.full((REACH * rows,), -1, jnp.int32), segment_ids])
+    key_seg = lax.dynamic_slice_in_dim(padded, at, window, 0).reshape(1, window)
+    query_seg = lax.dynamic_slice_in_dim(segment_ids, at, rows, 0).reshape(rows, 1)
+    return call(
+        attention_kernel,
+        head,
+        [full(query_rows), full(attn_out), full(grad_attn)]
+        + [full(b) for b in kv_blocks]
+        + [full(query_seg), full(key_seg)],
+        [out(query_rows.shape, BF)] + [out((rows, 2 * HD), F32) for _ in range(REACH + 1)],
+        [
+            pltpu.VMEM((window, 2 * HD), BF),
+            pltpu.VMEM((window, HD), F32),
+            pltpu.VMEM((window, HD), F32),
+        ],
+    )
 
 
 def body(
@@ -353,7 +356,6 @@
     slots = count * GROUP
     rows = count * CAP
     kv_width = key_rows.shape[1]
-    att_rows = query_rows.shape[0]
 
     kv = jnp.concatenate([key_rows, value_rows], axis=1)
     kv_blocks = [passed_along(kv, "ctx", distance) for distance in range(REACH, 0, -1)]
@@ -364,20 +366,25 @@
         [
             full(expert_ids.T),
             full(gate_probs.T),
-            full(pattern_table(tok_count)),
             (tokens, column_block(tokens.shape, 0)),
         ],
         [out((slots, half), BF), out((slots, 2 * tok_count), BF), out((slots, 2 * tok_count), BF)],
         [pltpu.VMEM((experts, tok_count), F32), pltpu.VMEM((experts, tok_count), F32)],
     )
-    (send_grads,) = call(
+    send_grads, send_far = call(
         select_kernel,
         head,
-        [full(scaled), (grad_out, column_block(grad_out.shape, 0))],
-        [out((slots, half), BF)],
-    )
-    row_blocks = dispatch(send_rows, head, count, lanes)
-    grad_blocks = dispatch(send_grads, head, count, lanes)
+        [
+            full(scaled),
+            (grad_out, column_block(grad_out.shape, 0)),
+            (grad_out, column_block(grad_out.shape, 2)),
+        ],
+        [out((slots, half), BF), out((slots, half), BF)],
+    )
+    row_blocks = near_ring(*dispatch(send_rows, head, count, lanes))
+    row_blocks += [turned(row_blocks[2], 1), turned(row_blocks[5], -1)]
+    grad_blocks = near_ring(*dispatch(send_grads, head, count, lanes))
+    grad_blocks += dispatch(send_far, head, count, lanes)
 
     gate_at = lambda offset: (w_gate, column_block(w_gate.shape, offset))
     up_at = lambda offset: (w_up, column_block(w_up.shape, offset))
@@ -453,18 +460,12 @@
         weight_kernel, head, [full(b) for b in grad_blocks] + [full(hidden)], [weight_out]
     )
 
-    grad_query, terms = attention(
-        query_rows,
-        jnp.concatenate(kv_blocks + [kv], axis=0),
-        attn_out,
-        grad_attn,
-        segment_ids,
-        kv_width,
-    )
-    total = terms[REACH * att_rows :]
+    grad_query, *terms = attention(
+        head, query_rows, kv_blocks + [kv], attn_out, grad_attn, segment_ids
+    )
+    total = terms[REACH]
     for distance in range(1, REACH + 1):
-        offset = (REACH - distance) * att_rows
-        total = total + passed_along(terms[offset : offset + att_rows], "ctx", -distance)
+        total = total + passed_along(terms[REACH - distance], "ctx", -distance)
     total = total.astype(BF)
     return (
         grad_tokens,

time: 298 us -> 332 us (1.11)
  blocking collectives: 0 us -> 40.4 us
  waiting for transfers between devices: 151 us -> 131 us
  Pallas kernels: 55.4 us -> 66.3 us
  starting transfers between devices: 72.4 us -> 78.6 us
    all_to_all x0 -> x1, blocking collectives: none -> 40.4 us  [exchange(): lax.all_to_all(send.reshape(count, GROUP, half), 'ctx', split_axis=0, con...]
    all_to_all x3, waiting for transfers between devices: 53.7 us -> 29 us  [exchange(): lax.all_to_all(send.reshape(count, GROUP, half), 'ctx', split_axis=0, con...]
    pallas_call x12 -> x14, Pallas kernels: 55.4 us -> 66.3 us  [launched(): pl.pallas_call(kernel, grid_spec=pltpu.PrefetchScalarGridSpec(num_scalar_...]
    ppermute x6, starting transfers between devices: 15.9 us -> 21.3 us  [passed_along(): return lax.ppermute(block, axis, route)]
    unnamed x64 -> x51, local copies, waits for them, and re-layouts: 8.51 us -> 5.3 us
    ppermute x21 -> x19, waiting for transfers between devices: 74 us -> 77 us  [turned(): lax.ppermute(block, 'head', [(i, (i + distance) % count) for i in range(c...]
    ppermute x21 -> x19, starting transfers between devices: 29.5 us -> 27.7 us  [turned(): lax.ppermute(block, 'head', [(i, (i + distance) % count) for i in range(c...]
  transfers between devices with their start and end apart: 30 -> 28, of which waited for: 14 -> 16; matrix products, arithmetic and copies ran while one was open for 3% -> 2% of each run, Pallas kernels for 15% -> 13%
where the time goes in v3:
time: 332 us; the launch traced here: 328 us
  waiting for transfers between devices  131 us (39%)
  starting transfers between devices  78.6 us (24%)
  Pallas kernels  66.3 us (20%)
  blocking collectives  40.4 us (12%)
  local copies, waits for them, and re-layouts  7.42 us (2%)
    ppermute x19, waiting for transfers between devices, turned(): lax.ppermute(block, 'head', [(i, (i + distance) % count) for i in range(c...  77 us
    pallas_call x14, Pallas kernels, launched(): pl.pallas_call(kernel, grid_spec=pltpu.PrefetchScalarGridSpec(num_scalar_...  66.3 us
    all_to_all x1, blocking collectives, exchange(): lax.all_to_all(send.reshape(count, GROUP, half), 'ctx', split_axis=0, con...  40.4 us
    all_to_all x3, starting transfers between devices, exchange(): lax.all_to_all(send.reshape(count, GROUP, half), 'ctx', split_axis=0, con...  29.6 us
    all_to_all x3, waiting for transfers between devices, exchange(): lax.all_to_all(send.reshape(count, GROUP, half), 'ctx', split_axis=0, con...  29 us
    ppermute x19, starting transfers between devices, turned(): lax.ppermute(block, 'head', [(i, (i + distance) % count) for i in range(c...  27.7 us
    ppermute x6, waiting for transfers between devices, passed_along(): return lax.ppermute(block, axis, route)  24.7 us
    ppermute x6, starting transfers between devices, passed_along(): return lax.ppermute(block, axis, route)  21.3 us
  transfers between devices with their start and end apart: 28, of which 16 were waited for; matrix products, arithmetic and copies ran while one was open for 2% of the time, Pallas kernels for 13%

profile of v3, /device:TPU:48, one launch (start us, length us, event | category | flops | bytes accessed | tf_op | source)
XLA Modules:
  0.0 327.7 jit_solution(16383352601118650194)
XLA Ops:
  0.6 3.8 %shard_map.180 = (bf16[2560,256]{1,0:T(8,128)(2,1)}, bf16[2560,256]{1,0:T(8,128)(2,1)}, bf16[2560,256]{1,0:T(8,128)(2,1)}) custom-call(s32[1]{0:T(128)} %bitcast.head, s32[8,128]{1,0:T(8,128)} %bitcast.24, bf16[8,128]{1,0:T(8,128)(2,1)} %bitcast.25, bf16[128,2048]{1,0:T(8,128)(2,1)} %tok.1), custom_call_target="tpu_custom_call" | custom-call | tf_op jit(solution)/shard_map/pallas_call | solution.py:59
  4.5 11.6 %all-to-all-start.2 = ((bf16[64,40,256]{2,1,0:T(8,128)(2,1)}), bf16[64,40,256]{2,1,0:T(8,128)(2,1)S(1)}, u32[]{:S(2)}, u32[]{:S(2)}) async-start(bf16[64,40,256]{2,1,0:T(8,128)(2,1)} %bitcast.21), calls=%async_computation.2 | async-start | bytes 2621440 | tf_op jit(solution)/shard_map/all_to_all | solution.py:258
  19.9 29.0 %all-to-all-done.2 = bf16[64,40,256]{2,1,0:T(8,128)(2,1)S(1)} async-done(((bf16[64,40,256]{2,1,0:T(8,128)(2,1)}), bf16[64,40,256]{2,1,0:T(8,128)(2,1)S(1)}, u32[]{:S(2)}, u32[]{:S(2)}) %all-to-all-start.2) | async-done | bytes 1310752 | tf_op jit(solution)/shard_map/all_to_all | solution.py:258
  49.0 40.4 %all_to_all.20 = bf16[64,40,256]{2,1,0:T(8,128)(2,1)} all-to-all(bf16[64,40,256]{2,1,0:T(8,128)(2,1)} %bitcast.22), channel_id=1, replica_groups=mesh['ctx'=64,'head'=4] {'ctx'}, dimensions={0} | all-to-all | bytes 2621440 | tf_op jit(solution)/shard_map/all_to_all | solution.py:258
  89.4 7.5 %all-to-all-start = ((bf16[64,40,256]{2,1,0:T(8,128)(2,1)}), bf16[64,40,256]{2,1,0:T(8,128)(2,1)S(1)}, u32[]{:S(2)}, u32[]{:S(2)}) async-start(bf16[64,40,256]{2,1,0:T(8,128)(2,1)} %bitcast.3), calls=%async_computation | async-start | bytes 2621440 | tf_op jit(solution)/shard_map/all_to_all | solution.py:258
  109.8 9.2 %collective-permute-done.4.refs_2_ = bf16[640,512]{1,0:T(8,128)(2,1)S(1)} collective-permute-done((bf16[640,512]{1,0:T(8,128)(2,1)}, bf16[640,512]{1,0:T(8,128)(2,1)S(1)}, u32[]{:S(2)}, u32[]{:S(2)}) %collective-permute-start.4) | collective-permute-done | bytes 655392 | tf_op jit(solution)/shard_map/ppermute | solution.py:27
  122.3 10.7 %collective-permute-done.refs_2_ = bf16[640,512]{1,0:T(8,128)(2,1)S(1)} collective-permute-done((bf16[640,512]{1,0:T(8,128)(2,1)}, bf16[640,512]{1,0:T(8,128)(2,1)S(1)}, u32[]{:S(2)}, u32[]{:S(2)}) %collective-permute-start) | collective-permute-done | bytes 655392 | tf_op jit(solution)/shard_map/ppermute | solution.py:27
  134.6 12.5 %collective-permute-done.1.refs_3_ = bf16[640,512]{1,0:T(8,128)(2,1)S(1)} collective-permute-done((bf16[640,512]{1,0:T(8,128)(2,1)}, bf16[640,512]{1,0:T(8,128)(2,1)S(1)}, u32[]{:S(2)}, u32[]{:S(2)}) %collective-permute-start.1) | collective-permute-done | bytes 655392 | tf_op jit(solution)/shard_map/ppermute | solution.py:27
  155.4 4.7 %shard_map.184.got_near = f32[1280,192]{1,0:T(8,128)} custom-call(s32[1]{0:T(128)} %bitcast.head, bf16[640,512]{1,0:T(8,128)(2,1)} %get-tuple-element.43.refs_0_, bf16[640,512]{1,0:T(8,128)(2,1)} %get-tuple-element.44.refs_1_, bf16[640,512]{1,0:T(8,128)(2,1)} %copy-done.5, bf16[640,512]{1,0:T(8,128)(2,1)} %copy-done.6, bf16[640,512]{1,0:T(8,128)(2,1)} %copy-done.7, ...), custom_call_target="tpu_custom_call" | custom-call | tf_op jit(solution)/shard_map/pallas_call | solution.py:59
  161.5 12.9 %collective-permute-done.8.refs_6_ = bf16[640,512]{1,0:T(8,128)(2,1)} collective-permute-done((bf16[640,512]{1,0:T(8,128)(2,1)S(1)}, bf16[640,512]{1,0:T(8,128)(2,1)}, u32[]{:S(2)}, u32[]{:S(2)}) %collective-permute-start.8) | collective-permute-done | bytes 655392 | tf_op jit(solution)/shard_map/ppermute | solution.py:27
  174.4 8.1 %shard_map.186 = (f32[1280,192]{1,0:T(8,128)}, f32[1280,192]{1,0:T(8,128)}, bf16[1280,192]{1,0:T(8,128)(2,1)}) custom-call(s32[1]{0:T(128)} %bitcast.head, bf16[640,512]{1,0:T(8,128)(2,1)} %get-tuple-element.46.refs_0_, bf16[640,512]{1,0:T(8,128)(2,1)} %get-tuple-element.47.refs_1_, bf16[640,512]{1,0:T(8,128)(2,1)} %copy-done.4, ...), custom_call_target="tpu_custom_call" | custom-call | tf_op jit(solution)/shard_map/pallas_call | solution.py:59
  182.5 5.1 %shard_map.187 = (bf16[1280,192]{1,0:T(8,128)(2,1)}, bf16[1280,192]{1,0:T(8,128)(2,1)}, bf16[640,512]{1,0:T(8,128)(2,1)}, bf16[640,512]{1,0:T(8,128)(2,1)}) custom-call(s32[1]{0:T(128)} %bitcast.head, bf16[640,512]{1,0:T(8,128)(2,1)} %get-tuple-element.40.low.refs_6_, bf16[640,512]{1,0:T(8,128)(2,1)} %get-tuple-element.41.high.refs_7_, ...), custom_call_target="tpu_custom_call" | custom-call | tf_op jit(solution)/shard_map/pallas_call | solution.py:59
  190.6 5.7 %shard_map.188 = (f32[640,512]{1,0:T(8,128)}, bf16[640,512]{1,0:T(8,128)(2,1)}, bf16[640,512]{1,0:T(8,128)(2,1)}, f32[640,512]{1,0:T(8,128)}, f32[1280,512]{1,0:T(8,128)}) custom-call(s32[1]{0:T(128)} %bitcast.head, bf16[1280,192]{1,0:T(8,128)(2,1)} %get-tuple-element.50.gg.refs_8_, bf16[1280,192]{1,0:T(8,128)(2,1)} %get-tuple-element.51.ug.refs_9_, ...), custom_call_target="tpu_custom_call" | custom-call | tf_op jit(solution)/shard_map/pallas_call | solution.py:59
  199.5 6.5 %collective-permute-done.14 = bf16[640,512]{1,0:T(8,128)(2,1)S(1)} collective-permute-done((bf16[640,512]{1,0:T(8,128)(2,1)}, bf16[640,512]{1,0:T(8,128)(2,1)S(1)}, u32[]{:S(2)}, u32[]{:S(2)}) %collective-permute-start.14) | collective-permute-done | bytes 655392 | tf_op jit(solution)/shard_map/ppermute | solution.py:27
  211.9 11.8 %collective-permute-done.10.left_a = bf16[640,512]{1,0:T(8,128)(2,1)S(1)} collective-permute-done((bf16[640,512]{1,0:T(8,128)(2,1)}, bf16[640,512]{1,0:T(8,128)(2,1)S(1)}, u32[]{:S(2)}, u32[]{:S(2)}) %collective-permute-start.10) | collective-permute-done | bytes 655392 | tf_op jit(solution)/shard_map/ppermute | solution.py:27
  223.7 8.4 %collective-permute-done.15.right_b = bf16[640,512]{1,0:T(8,128)(2,1)S(1)} collective-permute-done((bf16[640,512]{1,0:T(8,128)(2,1)S(1)}, bf16[640,512]{1,0:T(8,128)(2,1)S(1)}, u32[]{:S(2)}, u32[]{:S(2)}) %collective-permute-start.15) | collective-permute-done | bytes 655392 | tf_op jit(solution)/shard_map/ppermute | solution.py:27
  236.3 4.4 %shard_map.189 = bf16[2560,256]{1,0:T(8,128)(2,1)} custom-call(s32[1]{0:T(128)} %bitcast.head, f32[1280,512]{1,0:T(8,128)} %get-tuple-element.52.own, bf16[640,512]{1,0:T(8,128)(2,1)} %copy-done.10, bf16[640,512]{1,0:T(8,128)(2,1)} %copy-done.13, bf16[640,512]{1,0:T(8,128)(2,1)} %copy-done.11, bf16[640,512]{1,0:T(8,128)(2,1)} %copy-done.12), custom_call_target="tpu_custom_call" | custom-call | tf_op jit(solution)/shard_map/pallas_call | solution.py:59
  240.7 10.5 %all-to-all-start.3 = ((bf16[64,40,256]{2,1,0:T(8,128)(2,1)}), bf16[64,40,256]{2,1,0:T(8,128)(2,1)S(1)}, u32[]{:S(2)}, u32[]{:S(2)}) async-start(bf16[64,40,256]{2,1,0:T(8,128)(2,1)} %bitcast.20), calls=%async_computation.3 | async-start | bytes 2621440 | tf_op jit(solution)/shard_map/all_to_all | solution.py:258
  257.9 4.1 %collective-permute-start.21 = (bf16[128,256]{1,0:T(8,128)(2,1)S(1)}, bf16[128,256]{1,0:T(8,128)(2,1)S(1)}, u32[]{:S(2)}, u32[]{:S(2)}) collective-permute-start(bf16[128,256]{1,0:T(8,128)(2,1)S(1)} %constant_dynamic-update-slice_fusion.kv0), channel_id=1, source_target_pairs={{0,4},{4,8},{8,12},{12,16},{16,20},{20,24},{24,28},{28,32},{32,36}... | collective-permute-start | bytes 196616 | tf_op jit(solution)/shard_map/ppermute | solution.py:22
  263.5 20.0 %collective-permute-done.19.kv3 = bf16[128,256]{1,0:T(8,128)(2,1)S(1)} collective-permute-done((bf16[128,256]{1,0:T(8,128)(2,1)S(1)}, bf16[128,256]{1,0:T(8,128)(2,1)S(1)}, u32[]{:S(2)}, u32[]{:S(2)}) %collective-permute-start.19) | collective-permute-done | bytes 65568 | tf_op jit(solution)/shard_map/ppermute | solution.py:22
  285.4 7.3 %shard_map.193 = (bf16[128,1024]{1,0:T(8,128)(2,1)}, f32[128,256]{1,0:T(8,128)}, f32[128,256]{1,0:T(8,128)}, f32[128,256]{1,0:T(8,128)}, f32[128,256]{1,0:T(8,128)}) custom-call(s32[1]{0:T(128)} %bitcast.head, bf16[128,1024]{1,0:T(8,128)(2,1)} %query.1, bf16[128,1024]{1,0:T(8,128)(2,1)} %out_ref.1, bf16[128,1024]{1,0:T(8,128)(2,1)} %grad.1, ...), custom_call_target="tpu_custom_call" | custom-call | tf_op jit(solution)/shard_map/pallas_call | solution.py:59
  299.2 4.1 %collective-permute-start.24 = (f32[128,256]{1,0:T(8,128)}, f32[128,256]{1,0:T(8,128)S(1)}, u32[]{:S(2)}, u32[]{:S(2)}) collective-permute-start(f32[128,256]{1,0:T(8,128)} %get-tuple-element.66), channel_id=1, source_target_pairs={{12,0},{16,4},{20,8},{24,12},{28,16},{32,20},{36,24},{40,28},{44,3... | collective-permute-start | bytes 393224 | tf_op jit(solution)/shard_map/ppermute | solution.py:22
  312.2 7.0 %shard_map.191 = (bf16[2,192,2048]{2,1,0:T(8,128)(2,1)}, bf16[2,192,2048]{2,1,0:T(8,128)(2,1)}) custom-call(s32[1]{0:T(128)} %bitcast.head, bf16[640,512]{1,0:T(8,128)(2,1)} %get-tuple-element.46.refs_0_, bf16[640,512]{1,0:T(8,128)(2,1)} %get-tuple-element.47.refs_1_, bf16[640,512]{1,0:T(8,128)(2,1)} %copy-done.4, ...), custom_call_target="tpu_custom_call" | custom-call | tf_op jit(solution)/shard_map/pallas_call | solution.py:59
  319.2 5.2 %shard_map.192 = bf16[2,192,2048]{2,1,0:T(8,128)(2,1)} custom-call(s32[1]{0:T(128)} %bitcast.head, bf16[640,512]{1,0:T(8,128)(2,1)} %get-tuple-element.43.refs_0_, bf16[640,512]{1,0:T(8,128)(2,1)} %get-tuple-element.44.refs_1_, bf16[640,512]{1,0:T(8,128)(2,1)} %copy-done.5, bf16[640,512]{1,0:T(8,128)(2,1)} %copy-done.6, bf16[640,512]{1,0:T(8,128)(2,1)} %copy-done.7, ...), custom_call_target="tpu_custom_call" | custom-call | tf_op jit(solution)/shard_map/pallas_call | solution.py:59
  (109 shorter events, 76.3 us)
Async XLA Ops:
  4.5 44.5 %all-to-all-start.2 = ((bf16[64,40,256]{2,1,0:T(8,128)(2,1)}), bf16[64,40,256]{2,1,0:T(8,128)(2,1)S(1)}, u32[]{:S(2)}, u32[]{:S(2)}) async-start(bf16[64,40,256]{2,1,0:T(8,128)(2,1)} %bitcast.21), calls=%async_computation.2 | async-start | bytes 2621440 | tf_op jit(solution)/shard_map/all_to_all | solution.py:258
  89.4 61.8 %all-to-all-start = ((bf16[64,40,256]{2,1,0:T(8,128)(2,1)}), bf16[64,40,256]{2,1,0:T(8,128)(2,1)S(1)}, u32[]{:S(2)}, u32[]{:S(2)}) async-start(bf16[64,40,256]{2,1,0:T(8,128)(2,1)} %bitcast.3), calls=%async_computation | async-start | bytes 2621440 | tf_op jit(solution)/shard_map/all_to_all | solution.py:258
  100.0 19.0 %collective-permute-start.4 = (bf16[640,512]{1,0:T(8,128)(2,1)}, bf16[640,512]{1,0:T(8,128)(2,1)S(1)}, u32[]{:S(2)}, u32[]{:S(2)}) collective-permute-start(bf16[640,512]{1,0:T(8,128)(2,1)} %get-tuple-element.46.refs_0_), channel_id=1, source_target_pairs={{0,1},{1,2},{2,3},{3,0},{4,5},{5,6},{6,7},{7,4},{8,9},{9,10},{10,1... | collective-permute-start | bytes 1966088 | tf_op jit(solution)/shard_map/ppermute | solution.py:27
  101.5 17.9 %collective-permute-start.7 = (bf16[640,512]{1,0:T(8,128)(2,1)}, bf16[640,512]{1,0:T(8,128)(2,1)}, u32[]{:S(2)}, u32[]{:S(2)}) collective-permute-start(bf16[640,512]{1,0:T(8,128)(2,1)} %get-tuple-element.47.refs_1_), channel_id=1, source_target_pairs={{0,3},{1,0},{2,1},{3,2},{4,7},{5,4},{6,5},{7,6},{8,11},{9,8},{10,9... | collective-permute-start | bytes 1966088 | tf_op jit(solution)/shard_map/ppermute | solution.py:27
  106.2 26.8 %collective-permute-start = (bf16[640,512]{1,0:T(8,128)(2,1)}, bf16[640,512]{1,0:T(8,128)(2,1)S(1)}, u32[]{:S(2)}, u32[]{:S(2)}) collective-permute-start(bf16[640,512]{1,0:T(8,128)(2,1)} %get-tuple-element.43.refs_0_), channel_id=1, source_target_pairs={{0,1},{1,2},{2,3},{3,0},{4,5},{5,6},{6,7},{7,4},{8,9},{9,10},{10,1... | collective-permute-start | bytes 1966088 | tf_op jit(solution)/shard_map/ppermute | solution.py:27
  106.5 40.6 %collective-permute-start.1 = (bf16[640,512]{1,0:T(8,128)(2,1)}, bf16[640,512]{1,0:T(8,128)(2,1)S(1)}, u32[]{:S(2)}, u32[]{:S(2)}) collective-permute-start(bf16[640,512]{1,0:T(8,128)(2,1)} %get-tuple-element.44.refs_1_), channel_id=1, source_target_pairs={{0,1},{1,2},{2,3},{3,0},{4,5},{5,6},{6,7},{7,4},{8,9},{9,10},{10,1... | collective-permute-start | bytes 1966088 | tf_op jit(solution)/shard_map/ppermute | solution.py:27
  108.0 39.3 %collective-permute-start.2 = (bf16[640,512]{1,0:T(8,128)(2,1)}, bf16[640,512]{1,0:T(8,128)(2,1)S(1)}, u32[]{:S(2)}, u32[]{:S(2)}) collective-permute-start(bf16[640,512]{1,0:T(8,128)(2,1)} %get-tuple-element.43.refs_0_), channel_id=1, source_target_pairs={{0,3},{1,0},{2,1},{3,2},{4,7},{5,4},{6,5},{7,6},{8,11},{9,8},{10,9... | collective-permute-start | bytes 1966088 | tf_op jit(solution)/shard_map/ppermute | solution.py:27
  119.0 42.2 %collective-permute-start.5 = (bf16[640,512]{1,0:T(8,128)(2,1)S(1)}, bf16[640,512]{1,0:T(8,128)(2,1)}, u32[]{:S(2)}, u32[]{:S(2)}) collective-permute-start(bf16[640,512]{1,0:T(8,128)(2,1)S(1)} %copy-done.3), channel_id=1, source_target_pairs={{0,1},{1,2},{2,3},{3,0},{4,5},{5,6},{6,7},{7,4},{8,9},{9,10},{10,1... | collective-permute-start | bytes 1966088 | tf_op jit(solution)/shard_map/ppermute | solution.py:27
  119.4 36.0 %collective-permute-start.3 = (bf16[640,512]{1,0:T(8,128)(2,1)}, bf16[640,512]{1,0:T(8,128)(2,1)}, u32[]{:S(2)}, u32[]{:S(2)}) collective-permute-start(bf16[640,512]{1,0:T(8,128)(2,1)} %get-tuple-element.44.refs_1_), channel_id=1, source_target_pairs={{0,3},{1,0},{2,1},{3,2},{4,7},{5,4},{6,5},{7,6},{8,11},{9,8},{10,9... | collective-permute-start | bytes 1966088 | tf_op jit(solution)/shard_map/ppermute | solution.py:27
  133.0 28.5 %collective-permute-start.6 = (bf16[640,512]{1,0:T(8,128)(2,1)S(1)}, bf16[640,512]{1,0:T(8,128)(2,1)}, u32[]{:S(2)}, u32[]{:S(2)}) collective-permute-start(bf16[640,512]{1,0:T(8,128)(2,1)S(1)} %copy-done.2), channel_id=1, source_target_pairs={{0,3},{1,0},{2,1},{3,2},{4,7},{5,4},{6,5},{7,6},{8,11},{9,8},{10,9... | collective-permute-start | bytes 1966088 | tf_op jit(solution)/shard_map/ppermute | solution.py:27
  147.1 27.3 %collective-permute-start.8 = (bf16[640,512]{1,0:T(8,128)(2,1)S(1)}, bf16[640,512]{1,0:T(8,128)(2,1)}, u32[]{:S(2)}, u32[]{:S(2)}) collective-permute-start(bf16[640,512]{1,0:T(8,128)(2,1)S(1)} %collective-permute-done.4.refs_2_), channel_id=1, source_target_pairs={{0,1},{1,2},{2,3},{3,0},{4,5},{5,6},{6,7},{7,4},{8,9},{9,10},{10,1... | collective-permute-start | bytes 1966088 | tf_op jit(solution)/shard_map/ppermute | solution.py:27
  148.8 25.7 %collective-permute-start.9 = (bf16[640,512]{1,0:T(8,128)(2,1)}, bf16[640,512]{1,0:T(8,128)(2,1)}, u32[]{:S(2)}, u32[]{:S(2)}) collective-permute-start(bf16[640,512]{1,0:T(8,128)(2,1)} %collective-permute-done.7.refs_5_), channel_id=1, source_target_pairs={{0,3},{1,0},{2,1},{3,2},{4,7},{5,4},{6,5},{7,6},{8,11},{9,8},{10,9... | collective-permute-start | bytes 1966088 | tf_op jit(solution)/shard_map/ppermute | solution.py:27
  187.6 18.4 %collective-permute-start.14 = (bf16[640,512]{1,0:T(8,128)(2,1)}, bf16[640,512]{1,0:T(8,128)(2,1)S(1)}, u32[]{:S(2)}, u32[]{:S(2)}) collective-permute-start(bf16[640,512]{1,0:T(8,128)(2,1)} %get-tuple-element.58), channel_id=1, source_target_pairs={{0,3},{1,0},{2,1},{3,2},{4,7},{5,4},{6,5},{7,6},{8,11},{9,8},{10,9... | collective-permute-start | bytes 1966088 | tf_op jit(solution)/shard_map/ppermute | solution.py:27
  190.6 20.7 %collective-permute-start.11 = (bf16[640,512]{1,0:T(8,128)(2,1)}, bf16[640,512]{1,0:T(8,128)(2,1)S(1)}, u32[]{:S(2)}, u32[]{:S(2)}) collective-permute-start(bf16[640,512]{1,0:T(8,128)(2,1)} %get-tuple-element.55), channel_id=1, source_target_pairs={{0,1},{1,2},{2,3},{3,0},{4,5},{5,6},{6,7},{7,4},{8,9},{9,10},{10,1... | collective-permute-start | bytes 1966088 | tf_op jit(solution)/shard_map/ppermute | solution.py:27
  196.2 27.4 %collective-permute-start.10 = (bf16[640,512]{1,0:T(8,128)(2,1)}, bf16[640,512]{1,0:T(8,128)(2,1)S(1)}, u32[]{:S(2)}, u32[]{:S(2)}) collective-permute-start(bf16[640,512]{1,0:T(8,128)(2,1)} %get-tuple-element.53), channel_id=1, source_target_pairs={{0,1},{1,2},{2,3},{3,0},{4,5},{5,6},{6,7},{7,4},{8,9},{9,10},{10,1... | collective-permute-start | bytes 1966088 | tf_op jit(solution)/shard_map/ppermute | solution.py:27
  196.8 26.8 %collective-permute-start.13 = (bf16[640,512]{1,0:T(8,128)(2,1)}, bf16[640,512]{1,0:T(8,128)(2,1)S(1)}, u32[]{:S(2)}, u32[]{:S(2)}) collective-permute-start(bf16[640,512]{1,0:T(8,128)(2,1)} %get-tuple-element.56), channel_id=1, source_target_pairs={{0,3},{1,0},{2,1},{3,2},{4,7},{5,4},{6,5},{7,6},{8,11},{9,8},{10,9... | collective-permute-start | bytes 1966088 | tf_op jit(solution)/shard_map/ppermute | solution.py:27
  207.6 24.4 %collective-permute-start.15 = (bf16[640,512]{1,0:T(8,128)(2,1)S(1)}, bf16[640,512]{1,0:T(8,128)(2,1)S(1)}, u32[]{:S(2)}, u32[]{:S(2)}) collective-permute-start(bf16[640,512]{1,0:T(8,128)(2,1)S(1)} %add_convert_fusion), channel_id=1, source_target_pairs={{0,3},{1,0},{2,1},{3,2},{4,7},{5,4},{6,5},{7,6},{8,11},{9,8},{10,9... | collective-permute-start | bytes 1966088 | tf_op jit(solution)/shard_map/ppermute | solution.py:27
  211.6 23.9 %collective-permute-start.12 = (bf16[640,512]{1,0:T(8,128)(2,1)S(1)}, bf16[640,512]{1,0:T(8,128)(2,1)S(1)}, u32[]{:S(2)}, u32[]{:S(2)}) collective-permute-start(bf16[640,512]{1,0:T(8,128)(2,1)S(1)} %add_convert_fusion.1), channel_id=1, source_target_pairs={{0,1},{1,2},{2,3},{3,0},{4,5},{5,6},{6,7},{7,4},{8,9},{9,10},{10,1... | collective-permute-start | bytes 1966088 | tf_op jit(solution)/shard_map/ppermute | solution.py:27
  240.7 66.9 %all-to-all-start.3 = ((bf16[64,40,256]{2,1,0:T(8,128)(2,1)}), bf16[64,40,256]{2,1,0:T(8,128)(2,1)S(1)}, u32[]{:S(2)}, u32[]{:S(2)}) async-start(bf16[64,40,256]{2,1,0:T(8,128)(2,1)} %bitcast.20), calls=%async_computation.3 | async-start | bytes 2621440 | tf_op jit(solution)/shard_map/all_to_all | solution.py:258
  251.2 32.3 %collective-permute-start.19 = (bf16[128,256]{1,0:T(8,128)(2,1)S(1)}, bf16[128,256]{1,0:T(8,128)(2,1)S(1)}, u32[]{:S(2)}, u32[]{:S(2)}) collective-permute-start(bf16[128,256]{1,0:T(8,128)(2,1)S(1)} %constant_dynamic-update-slice_fusion.kv0), channel_id=1, source_target_pairs={{0,12},{4,16},{8,20},{12,24},{16,28},{20,32},{24,36},{28,40},{32,4... | collective-permute-start | bytes 196616 | tf_op jit(solution)/shard_map/ppermute | solution.py:22
  254.5 30.2 %collective-permute-start.20 = (bf16[128,256]{1,0:T(8,128)(2,1)S(1)}, bf16[128,256]{1,0:T(8,128)(2,1)S(1)}, u32[]{:S(2)}, u32[]{:S(2)}) collective-permute-start(bf16[128,256]{1,0:T(8,128)(2,1)S(1)} %constant_dynamic-update-slice_fusion.kv0), channel_id=1, source_target_pairs={{0,8},{4,12},{8,16},{12,20},{16,24},{20,28},{24,32},{28,36},{32,40... | collective-permute-start | bytes 196616 | tf_op jit(solution)/shard_map/ppermute | solution.py:22
  257.9 26.9 %collective-permute-start.21 = (bf16[128,256]{1,0:T(8,128)(2,1)S(1)}, bf16[128,256]{1,0:T(8,128)(2,1)S(1)}, u32[]{:S(2)}, u32[]{:S(2)}) collective-permute-start(bf16[128,256]{1,0:T(8,128)(2,1)S(1)} %constant_dynamic-update-slice_fusion.kv0), channel_id=1, source_target_pairs={{0,4},{4,8},{8,12},{12,16},{16,20},{20,24},{24,28},{28,32},{32,36}... | collective-permute-start | bytes 196616 | tf_op jit(solution)/shard_map/ppermute | solution.py:22
  308.2 16.2 %collective-permute-start.16 = (bf16[128,512]{1,0:T(8,128)(2,1)S(1)}, bf16[128,512]{1,0:T(8,128)(2,1)S(1)}, u32[]{:S(2)}, u32[]{:S(2)}) collective-permute-start(bf16[128,512]{1,0:T(8,128)(2,1)S(1)} %pad_maximum_fusion.refs_0_), channel_id=1, source_target_pairs={{0,1},{1,2},{2,3},{3,0},{4,5},{5,6},{6,7},{7,4},{8,9},{9,10},{10,1... | collective-permute-start | bytes 393224 | tf_op jit(solution)/shard_map/ppermute | solution.py:27
  308.3 16.1 %collective-permute-start.17 = (bf16[128,512]{1,0:T(8,128)(2,1)S(1)}, bf16[128,512]{1,0:T(8,128)(2,1)S(1)}, u32[]{:S(2)}, u32[]{:S(2)}) collective-permute-start(bf16[128,512]{1,0:T(8,128)(2,1)S(1)} %pad_maximum_fusion.refs_0_), channel_id=1, source_target_pairs={{0,3},{1,0},{2,1},{3,2},{4,7},{5,4},{6,5},{7,6},{8,11},{9,8},{10,9... | collective-permute-start | bytes 393224 | tf_op jit(solution)/shard_map/ppermute | solution.py:27
  (29 other events, 370.2 us)

commit v4 on v3

--- a/solution.py
+++ b/solution.py
@@ -126,11 +126,10 @@
     rows_ref[...] = dot_nn(pick_ref[...], stacked).astype(BF)
 
 
-def select_kernel(head, scaled, own, far, own_ref, far_ref):
-    for tok, ref in ((own, own_ref), (far, far_ref)):
-        half = tok.shape[1] // 2
-        stacked = jnp.concatenate([tok[:, :half], tok[:, half:]], axis=0)
-        ref[...] = dot_nn(scaled[...], stacked).astype(BF)
+def select_kernel(head, scaled, tok, rows_ref):
+    half = tok.shape[1] // 2
+    stacked = jnp.concatenate([tok[:, :half], tok[:, half:]], axis=0)
+    rows_ref[...] = dot_nn(scaled[...], stacked).astype(BF)
 
 
 def untangle_kernel(head, recv, low_ref, high_ref, wide):
@@ -148,30 +147,9 @@
                     ref[c * sources : (c + 1) * sources, col : col + lanes] = rows.astype(BF)
 
 
-def tangle_kernel(head, own, left_a, left_b, right_a, right_b, send_ref, wide):
-    rows = own.shape[0] // 2
-    sources = rows // CAP
-    half = own.shape[1] // 2
-    lanes = wide[0].shape[1]
-    for e, (a, b) in ((0, (left_b, right_a)), (1, (left_a, right_b))):
-        for c in range(CAP):
-            for part in range(2):
-                for p in range(half // lanes):
-                    col = part * half + p * lanes
-                    at = c * sources
-                    total = (
-                        own[e * rows + at : e * rows + at + sources, col : col + lanes]
-                        + a[at : at + sources, col : col + lanes].astype(F32)
-                        + b[at : at + sources, col : col + lanes].astype(F32)
-                    )
-                    wide[p][pl.ds(part * SLOTS + e * CAP + c, sources, stride=GROUP), :] = total
-    for p in range(half // lanes):
-        send_ref[:, p * lanes : (p + 1) * lanes] = wide[p][...].astype(BF)
-
-
 def pre_kernel(head, *refs):
     blocks, gates, ups = refs[0:8], refs[8:12], refs[12:16]
-    act_ref, slope_ref, hidden_ref = refs[16:]
+    act_ref, slope_ref, *hidden_refs = refs[16:]
     for e in range(LOCAL):
         rows = blocks[e].shape[0]
         gate = dot_nt(blocks[e][...], gates[0][e])
@@ -184,7 +162,7 @@
         at = pl.ds(e * rows, rows)
         act_ref[at, :] = active
         slope_ref[at, :] = up * sig * (1.0 + gate * (1.0 - sig))
-        hidden_ref[at, :] = (active * up).astype(BF)
+        hidden_refs[e][...] = (active * up).astype(BF)
 
 
 def near_kernel(head, *refs):
@@ -197,52 +175,72 @@
         got_ref[pl.ds(e * rows, rows), :] = got
 
 
-def grad_kernel(head, low, high, down, got_near, act, slope, gate_far, up_far, *outs):
-    gg_ref, ug_ref, far_low, far_high = outs
-    for e, block, far in ((0, low, far_low), (1, high, far_high)):
+def grad_kernel(head, low, high, down, got_near, act, slope, gu_low, gu_high):
+    units = act.shape[1]
+    for e, block, ref in ((0, low, gu_low), (1, high, gu_high)):
         rows = block.shape[0]
         at = pl.ds(e * rows, rows)
         got = got_near[at, :] + dot_nt(block[...], down[e])
-        gg = (got * slope[at, :]).astype(BF)
-        ug = (got * act[at, :]).astype(BF)
-        gg_ref[at, :] = gg
-        ug_ref[at, :] = ug
-        far[...] = (dot_nn(gg, gate_far[e]) + dot_nn(ug, up_far[e])).astype(BF)
-
-
-def back_kernel(head, gg, ug, gate_p, up_p, gate_m, up_m, gate_o, up_o, p0, p1, m0, m1, own):
-    rows = gg.shape[0] // 2
-    low, high = pl.ds(0, rows), pl.ds(rows, rows)
-    p1[...] = (dot_nn(gg[high, :], gate_p[1]) + dot_nn(ug[high, :], up_p[1])).astype(BF)
-    m0[...] = (dot_nn(gg[low, :], gate_m[0]) + dot_nn(ug[low, :], up_m[0])).astype(BF)
-    p0[...] = dot_nn(gg[low, :], gate_p[0]) + dot_nn(ug[low, :], up_p[0])
-    m1[...] = dot_nn(gg[high, :], gate_m[1]) + dot_nn(ug[high, :], up_m[1])
-    own[low, :] = dot_nn(gg[low, :], gate_o[0]) + dot_nn(ug[low, :], up_o[0])
-    own[high, :] = dot_nn(gg[high, :], gate_o[1]) + dot_nn(ug[high, :], up_o[1])
+        ref[:, :units] = (got * slope[at, :]).astype(BF)
+        ref[:, units:] = (got * act[at, :]).astype(BF)
+
+
+def columns_kernel(head, *refs):
+    gates, ups, results = refs[0:4], refs[4:8], refs[8:12]
+    units = gates[0].shape[1]
+    for gate, up, result in zip(gates, ups, results):
+        result[:, :units, :] = gate[...]
+        result[:, units:, :] = up[...]
+
+
+def back_kernel(head, *refs):
+    blocks, mats, own = refs[0:6], refs[6:9], refs[9]
+    for e in range(LOCAL):
+        rows = blocks[e].shape[0]
+        total = dot_nn(blocks[e][...], mats[0][e])
+        for q in range(1, 3):
+            total = total + dot_nn(blocks[2 * q + e][...], mats[q][e])
+        own[pl.ds(e * rows, rows), :] = total
+
+
+def tangle_kernel(head, own, low, high, mat, send_ref, wide, total):
+    rows = own.shape[0] // 2
+    sources = rows // CAP
+    half = own.shape[1] // 2
+    lanes = wide[0].shape[1]
+    for e, block in ((0, low), (1, high)):
+        total[...] = own[pl.ds(e * rows, rows), :] + dot_nn(block[...], mat[e])
+        for c in range(CAP):
+            for part in range(2):
+                for p in range(half // lanes):
+                    col = part * half + p * lanes
+                    at = pl.ds(part * SLOTS + e * CAP + c, sources, stride=GROUP)
+                    wide[p][at, :] = total[c * sources : (c + 1) * sources, col : col + lanes]
+    for p in range(half // lanes):
+        send_ref[:, p * lanes : (p + 1) * lanes] = wide[p][...].astype(BF)
 
 
 def weight_kernel(head, *refs):
-    blocks = refs[0:8]
-    sides = len(refs[8:]) // 2
-    lefts, results = refs[8 : 8 + sides], refs[8 + sides :]
+    blocks, low, high, results = refs[0:8], refs[8], refs[9], refs[10:]
     width = blocks[0].shape[1]
+    units = results[0].shape[1]
     offsets = (0, 3, 1, 2)
     for q in range(4):
         col = pl.multiple_of(((head[0] + offsets[q]) % 4) * width, width)
-        for e in range(LOCAL):
-            rows = blocks[e].shape[0]
-            data = blocks[2 * q + e][...]
-            for left, result in zip(lefts, results):
-                part = dot_tn(left[pl.ds(e * rows, rows), :], data)
-                result[e, :, pl.ds(col, width)] = part.astype(BF)
-
-
-def near_ring(low, high):
+        for e, left in ((0, low), (1, high)):
+            part = dot_tn(left[...], blocks[2 * q + e][...]).astype(BF)
+            for i, result in enumerate(results):
+                result[e, :, pl.ds(col, width)] = part[i * units : (i + 1) * units, :]
+
+
+def round_ring(low, high):
     right_low = turned(low, 1)
     left_high = turned(high, -1)
     right_high = turned(high, 1)
     left_low = turned(low, -1)
-    return [low, high, right_low, right_high, left_low, left_high]
+    far_low = turned(right_low, 1)
+    far_high = turned(left_high, -1)
+    return [low, high, right_low, right_high, left_low, left_high, far_low, far_high]
 
 
 def join_kernel(head, *refs):
@@ -270,7 +268,7 @@
         [out((count * CAP, 2 * half), BF), out((count * CAP, 2 * half), BF)],
         [[pltpu.VMEM((count * GROUP, lanes), F32) for _ in range(half // lanes)]],
     )
-    return low, high
+    return round_ring(low, high)
 
 
 def attention_kernel(head, query, out_ref, grad, kv3, kv2, kv1, kv0, query_seg, key_seg, *refs):
@@ -371,33 +369,36 @@
         [out((slots, half), BF), out((slots, 2 * tok_count), BF), out((slots, 2 * tok_count), BF)],
         [pltpu.VMEM((experts, tok_count), F32), pltpu.VMEM((experts, tok_count), F32)],
     )
-    send_grads, send_far = call(
+    (send_grads,) = call(
         select_kernel,
         head,
-        [
-            full(scaled),
-            (grad_out, column_block(grad_out.shape, 0)),
-            (grad_out, column_block(grad_out.shape, 2)),
-        ],
-        [out((slots, half), BF), out((slots, half), BF)],
-    )
-    row_blocks = near_ring(*dispatch(send_rows, head, count, lanes))
-    row_blocks += [turned(row_blocks[2], 1), turned(row_blocks[5], -1)]
-    grad_blocks = near_ring(*dispatch(send_grads, head, count, lanes))
-    grad_blocks += dispatch(send_far, head, count, lanes)
+        [full(scaled), (grad_out, column_block(grad_out.shape, 0))],
+        [out((slots, half), BF)],
+    )
+    row_blocks = dispatch(send_rows, head, count, lanes)
+    grad_blocks = dispatch(send_grads, head, count, lanes)
 
     gate_at = lambda offset: (w_gate, column_block(w_gate.shape, offset))
     up_at = lambda offset: (w_up, column_block(w_up.shape, offset))
     down_at = lambda offset: (w_down, column_block(w_down.shape, offset))
     order = (0, 3, 1, 2)
-    act, slope, hidden = call(
+    mat_shape = (LOCAL, 2 * hidden_local, quarter)
+    mats = call(
+        columns_kernel,
+        head,
+        [gate_at(o) for o in (0, 1, 3, 2)] + [up_at(o) for o in (0, 1, 3, 2)],
+        [out(mat_shape, BF) for _ in range(4)],
+    )
+    mats = [mats[0]] + [turned(m, distance) for m, distance in zip(mats[1:], (1, 3, 2))]
+    act, slope, hidden_low, hidden_high = call(
         pre_kernel,
         head,
         [full(b) for b in row_blocks] + [gate_at(o) for o in order] + [up_at(o) for o in order],
         [
             out((2 * rows, hidden_local), F32),
             out((2 * rows, hidden_local), F32),
-            out((2 * rows, hidden_local), BF),
+            out((rows, hidden_local), BF),
+            out((rows, hidden_local), BF),
         ],
     )
     (got_near,) = call(
@@ -406,42 +407,29 @@
         [full(b) for b in grad_blocks[:6]] + [down_at(o) for o in order[:3]],
         [out((2 * rows, hidden_local), F32)],
     )
-    gg, ug, far_low, far_high = call(
+    gu_low, gu_high = call(
         grad_kernel,
         head,
         [full(b) for b in grad_blocks[6:]]
-        + [down_at(2), full(got_near), full(act), full(slope), gate_at(2), up_at(2)],
-        [
-            out((2 * rows, hidden_local), BF),
-            out((2 * rows, hidden_local), BF),
-            out((rows, quarter), BF),
-            out((rows, quarter), BF),
-        ],
-    )
-    near_low = turned(far_low, 1)
-    near_high = turned(far_high, -1)
-    p0, p1, m0, m1, own = call(
+        + [down_at(2), full(got_near), full(act), full(slope)],
+        [out((rows, 2 * hidden_local), BF), out((rows, 2 * hidden_local), BF)],
+    )
+    gu_blocks = round_ring(gu_low, gu_high)
+    (own,) = call(
         back_kernel,
         head,
-        [full(gg), full(ug), gate_at(1), up_at(1), gate_at(3), up_at(3), gate_at(0), up_at(0)],
-        [
-            out((rows, quarter), F32),
-            out((rows, quarter), BF),
-            out((rows, quarter), BF),
-            out((rows, quarter), F32),
-            out((2 * rows, quarter), F32),
-        ],
-    )
-    left_a = turned(p1, 1)
-    right_a = turned(m0, -1)
-    left_b = turned((p0 + near_low.astype(F32)).astype(BF), 1)
-    right_b = turned((m1 + near_high.astype(F32)).astype(BF), -1)
+        [full(b) for b in gu_blocks[:6]] + [full(m) for m in mats[:3]],
+        [out((2 * rows, quarter), F32)],
+    )
     (send_back,) = call(
         tangle_kernel,
         head,
-        [full(own), full(left_a), full(left_b), full(right_a), full(right_b)],
+        [full(own), full(gu_blocks[6]), full(gu_blocks[7]), full(mats[3])],
         [out((slots, half), BF)],
-        [[pltpu.VMEM((slots, lanes), F32) for _ in range(half // lanes)]],
+        [
+            [pltpu.VMEM((slots, lanes), F32) for _ in range(half // lanes)],
+            pltpu.VMEM((rows, quarter), F32),
+        ],
     )
     returned = exchange(send_back, count)
     summed = dot_tn(pick, returned)
@@ -453,11 +441,14 @@
     grad_gate, grad_up = call(
         weight_kernel,
         head,
-        [full(b) for b in row_blocks] + [full(gg), full(ug)],
+        [full(b) for b in row_blocks] + [full(gu_low), full(gu_high)],
         [weight_out, weight_out],
     )
     (grad_down,) = call(
-        weight_kernel, head, [full(b) for b in grad_blocks] + [full(hidden)], [weight_out]
+        weight_kernel,
+        head,
+        [full(b) for b in grad_blocks] + [full(hidden_low), full(hidden_high)],
+        [weight_out],
     )
 
     grad_query, *terms = attention(

time: 332 us -> 314 us (0.946)
  blocking collectives: 40.4 us -> 0 us
  starting transfers between devices: 78.6 us -> 96.7 us
  waiting for transfers between devices: 131 us -> 136 us
    all_to_all x1 -> x0, blocking collectives: 40.4 us -> none  [exchange(): lax.all_to_all(send.reshape(count, GROUP, half), 'ctx', split_axis=0, con...]
    all_to_all x3, waiting for transfers between devices: 29 us -> 53.2 us  [exchange(): lax.all_to_all(send.reshape(count, GROUP, half), 'ctx', split_axis=0, con...]
    ppermute x19 -> x24, starting transfers between devices: 27.7 us -> 49.2 us  [turned(): lax.ppermute(block, 'head', [(i, (i + distance) % count) for i in range(c...]
    ppermute x19 -> x24, waiting for transfers between devices: 77 us -> 57.9 us  [turned(): lax.ppermute(block, 'head', [(i, (i + distance) % count) for i in range(c...]
    all_to_all x3, starting transfers between devices: 29.6 us -> 26.2 us  [exchange(): lax.all_to_all(send.reshape(count, GROUP, half), 'ctx', split_axis=0, con...]
    unnamed x51 -> x71, local copies, waits for them, and re-layouts: 5.3 us -> 8.33 us
  transfers between devices with their start and end apart: 28 -> 33, of which waited for: 16 -> 16; matrix products, arithmetic and copies ran while one was open for 2% -> 1% of each run, Pallas kernels for 13% -> 18%
where the time goes in v4:
time: 314 us; the launch traced here: 311 us
  waiting for transfers between devices  136 us (43%)
  starting transfers between devices  96.7 us (31%)
  Pallas kernels  65.5 us (21%)
  local copies, waits for them, and re-layouts  10.4 us (3%)
    pallas_call x14, Pallas kernels, launched(): pl.pallas_call(kernel, grid_spec=pltpu.PrefetchScalarGridSpec(num_scalar_...  65.5 us
    ppermute x24, waiting for transfers between devices, turned(): lax.ppermute(block, 'head', [(i, (i + distance) % count) for i in range(c...  57.9 us
    all_to_all x3, waiting for transfers between devices, exchange(): lax.all_to_all(send.reshape(count, GROUP, half), 'ctx', split_axis=0, con...  53.2 us
    ppermute x24, starting transfers between devices, turned(): lax.ppermute(block, 'head', [(i, (i + distance) % count) for i in range(c...  49.2 us
    all_to_all x3, starting transfers between devices, exchange(): lax.all_to_all(send.reshape(count, GROUP, half), 'ctx', split_axis=0, con...  26.2 us
    ppermute x6, waiting for transfers between devices, passed_along(): return lax.ppermute(block, axis, route)  24.7 us
    ppermute x6, starting transfers between devices, passed_along(): return lax.ppermute(block, axis, route)  21.3 us
    unnamed x71, local copies, waits for them, and re-layouts  8.33 us
  transfers between devices with their start and end apart: 33, of which 16 were waited for; matrix products, arithmetic and copies ran while one was open for 1% of the time, Pallas kernels for 18%

profile of v4, /device:TPU:48, one launch (start us, length us, event | category | flops | bytes accessed | tf_op | source)
XLA Modules:
  0.0 310.9 jit_solution(6184498054340224438)
XLA Ops:
  4.5 11.6 %all-to-all-start.1 = ((bf16[64,40,256]{2,1,0:T(8,128)(2,1)}), bf16[64,40,256]{2,1,0:T(8,128)(2,1)S(1)}, u32[]{:S(2)}, u32[]{:S(2)}) async-start(bf16[64,40,256]{2,1,0:T(8,128)(2,1)} %bitcast.19), calls=%async_computation.1 | async-start | bytes 2621440 | tf_op jit(solution)/shard_map/all_to_all | solution.py:256
  19.1 29.9 %all-to-all-done.1 = bf16[64,40,256]{2,1,0:T(8,128)(2,1)S(1)} async-done(((bf16[64,40,256]{2,1,0:T(8,128)(2,1)}), bf16[64,40,256]{2,1,0:T(8,128)(2,1)S(1)}, u32[]{:S(2)}, u32[]{:S(2)}) %all-to-all-start.1) | async-done | bytes 1310752 | tf_op jit(solution)/shard_map/all_to_all | solution.py:256
  50.0 7.5 %all-to-all-start = ((bf16[64,40,256]{2,1,0:T(8,128)(2,1)}), bf16[64,40,256]{2,1,0:T(8,128)(2,1)S(1)}, u32[]{:S(2)}, u32[]{:S(2)}) async-start(bf16[64,40,256]{2,1,0:T(8,128)(2,1)} %bitcast.16), calls=%async_computation | async-start | bytes 2621440 | tf_op jit(solution)/shard_map/all_to_all | solution.py:256
  67.1 23.3 %all-to-all-done = bf16[64,40,256]{2,1,0:T(8,128)(2,1)S(1)} async-done(((bf16[64,40,256]{2,1,0:T(8,128)(2,1)}), bf16[64,40,256]{2,1,0:T(8,128)(2,1)S(1)}, u32[]{:S(2)}, u32[]{:S(2)}) %all-to-all-start) | async-done | bytes 1310752 | tf_op jit(solution)/shard_map/all_to_all | solution.py:256
  101.0 12.5 %collective-permute-done.refs_2_ = bf16[640,512]{1,0:T(8,128)(2,1)S(1)} collective-permute-done((bf16[640,512]{1,0:T(8,128)(2,1)}, bf16[640,512]{1,0:T(8,128)(2,1)S(1)}, u32[]{:S(2)}, u32[]{:S(2)}) %collective-permute-start) | collective-permute-done | bytes 655392 | tf_op jit(solution)/shard_map/ppermute | solution.py:27
  115.5 12.0 %collective-permute-done.4.refs_3_ = bf16[640,512]{1,0:T(8,128)(2,1)S(1)} collective-permute-done((bf16[640,512]{1,0:T(8,128)(2,1)}, bf16[640,512]{1,0:T(8,128)(2,1)S(1)}, u32[]{:S(2)}, u32[]{:S(2)}) %collective-permute-start.4) | collective-permute-done | bytes 655392 | tf_op jit(solution)/shard_map/ppermute | solution.py:27
  133.3 8.3 %collective-permute-done.10.refs_6_ = bf16[640,512]{1,0:T(8,128)(2,1)S(1)} collective-permute-done((bf16[640,512]{1,0:T(8,128)(2,1)S(1)}, bf16[640,512]{1,0:T(8,128)(2,1)S(1)}, u32[]{:S(2)}, u32[]{:S(2)}) %collective-permute-start.10) | collective-permute-done | bytes 655392 | tf_op jit(solution)/shard_map/ppermute | solution.py:27
  143.1 4.7 %shard_map.183.got_near = f32[1280,192]{1,0:T(8,128)} custom-call(s32[1]{0:T(128)} %bitcast.head, bf16[640,512]{1,0:T(8,128)(2,1)} %get-tuple-element.33.refs_0_, bf16[640,512]{1,0:T(8,128)(2,1)} %get-tuple-element.34.refs_1_, bf16[640,512]{1,0:T(8,128)(2,1)} %copy-done.7, bf16[640,512]{1,0:T(8,128)(2,1)} %copy-done.9, bf16[640,512]{1,0:T(8,128)(2,1)} %copy-done.10, ...), custom_call_target="tpu_custom_call" | custom-call | tf_op jit(solution)/shard_map/pallas_call | solution.py:59
  148.7 8.1 %shard_map.185 = (f32[1280,192]{1,0:T(8,128)}, f32[1280,192]{1,0:T(8,128)}, bf16[640,192]{1,0:T(8,128)(2,1)}, bf16[640,192]{1,0:T(8,128)(2,1)}) custom-call(s32[1]{0:T(128)} %bitcast.head, bf16[640,512]{1,0:T(8,128)(2,1)} %get-tuple-element.36.refs_0_, bf16[640,512]{1,0:T(8,128)(2,1)} %get-tuple-element.37.refs_1_, bf16[640,512]{1,0:T(8,128)(2,1)} %copy-done.2, ...), custom_call_target="tpu_custom_call" | custom-call | tf_op jit(solution)/shard_map/pallas_call | solution.py:59
  157.8 4.3 %shard_map.186 = (bf16[640,384]{1,0:T(8,128)(2,1)}, bf16[640,384]{1,0:T(8,128)(2,1)}) custom-call(s32[1]{0:T(128)} %bitcast.head, bf16[640,512]{1,0:T(8,128)(2,1)} %copy-done.11, bf16[640,512]{1,0:T(8,128)(2,1)} %copy-done.12, bf16[2,192,2048]{2,1,0:T(8,128)(2,1)} %down.1, f32[1280,192]{1,0:T(8,128)} %shard_map.183.got_near, ...), custom_call_target="tpu_custom_call" | custom-call | tf_op jit(solution)/shard_map/pallas_call | solution.py:59
  165.8 6.7 %collective-permute-done.16.refs_7_ = bf16[2,384,512]{2,1,0:T(8,128)(2,1)S(1)} collective-permute-done((bf16[2,384,512]{2,1,0:T(8,128)(2,1)}, bf16[2,384,512]{2,1,0:T(8,128)(2,1)S(1)}, u32[]{:S(2)}, u32[]{:S(2)}) %collective-permute-start.16) | collective-permute-done | bytes 786464 | tf_op jit(solution)/shard_map/ppermute | solution.py:27
  175.7 7.4 %collective-permute-done.12.refs_2_ = bf16[640,384]{1,0:T(8,128)(2,1)S(1)} collective-permute-done((bf16[640,384]{1,0:T(8,128)(2,1)}, bf16[640,384]{1,0:T(8,128)(2,1)S(1)}, u32[]{:S(2)}, u32[]{:S(2)}) %collective-permute-start.12) | collective-permute-done | bytes 491552 | tf_op jit(solution)/shard_map/ppermute | solution.py:27
  183.1 15.6 %collective-permute-start.18 = (bf16[640,384]{1,0:T(8,128)(2,1)S(1)}, bf16[640,384]{1,0:T(8,128)(2,1)S(1)}, u32[]{:S(2)}, u32[]{:S(2)}) collective-permute-start(bf16[640,384]{1,0:T(8,128)(2,1)S(1)} %collective-permute-done.12.refs_2_), channel_id=1, source_target_pairs={{0,1},{1,2},{2,3},{3,0},{4,5},{5,6},{6,7},{7,4},{8,9},{9,10},{10,1... | collective-permute-start | bytes 1474568 | tf_op jit(solution)/shard_map/ppermute | solution.py:27
  199.3 3.9 %collective-permute-start.19 = (bf16[640,384]{1,0:T(8,128)(2,1)S(1)}, bf16[640,384]{1,0:T(8,128)(2,1)S(1)}, u32[]{:S(2)}, u32[]{:S(2)}) collective-permute-start(bf16[640,384]{1,0:T(8,128)(2,1)S(1)} %collective-permute-done.15.refs_5_), channel_id=1, source_target_pairs={{0,3},{1,0},{2,1},{3,2},{4,7},{5,4},{6,5},{7,6},{8,11},{9,8},{10,9... | collective-permute-start | bytes 1474568 | tf_op jit(solution)/shard_map/ppermute | solution.py:27
  203.1 7.3 %collective-permute-done.13.refs_3_ = bf16[640,384]{1,0:T(8,128)(2,1)S(1)} collective-permute-done((bf16[640,384]{1,0:T(8,128)(2,1)}, bf16[640,384]{1,0:T(8,128)(2,1)S(1)}, u32[]{:S(2)}, u32[]{:S(2)}) %collective-permute-start.13) | collective-permute-done | bytes 491552 | tf_op jit(solution)/shard_map/ppermute | solution.py:27
  211.5 6.2 %shard_map.188.own = f32[1280,512]{1,0:T(8,128)} custom-call(s32[1]{0:T(128)} %bitcast.head, bf16[640,384]{1,0:T(8,128)(2,1)} %get-tuple-element.40.refs_0_.refs_8_, bf16[640,384]{1,0:T(8,128)(2,1)} %get-tuple-element.41.refs_1_.refs_9_, bf16[640,384]{1,0:T(8,128)(2,1)} %copy-done.18, bf16[640,384]{1,0:T(8,128)(2,1)} %copy-done.21, ...), custom_call_target="tpu_custom_call" | custom-call | tf_op jit(solution)/shard_map/pallas_call | solution.py:59
  222.0 4.4 %shard_map.189 = bf16[2560,256]{1,0:T(8,128)(2,1)} custom-call(s32[1]{0:T(128)} %bitcast.head, f32[1280,512]{1,0:T(8,128)} %shard_map.188.own, bf16[640,384]{1,0:T(8,128)(2,1)} %copy-done.20, bf16[640,384]{1,0:T(8,128)(2,1)} %copy-done.22, bf16[2,384,512]{2,1,0:T(8,128)(2,1)} %copy-done.14), custom_call_target="tpu_custom_call" | custom-call | tf_op jit(solution)/shard_map/pallas_call | solution.py:59
  226.4 7.1 %all-to-all-start.2 = ((bf16[64,40,256]{2,1,0:T(8,128)(2,1)}), bf16[64,40,256]{2,1,0:T(8,128)(2,1)S(1)}, u32[]{:S(2)}, u32[]{:S(2)}) async-start(bf16[64,40,256]{2,1,0:T(8,128)(2,1)} %bitcast.18), calls=%async_computation.2 | async-start | bytes 2621440 | tf_op jit(solution)/shard_map/all_to_all | solution.py:256
  240.3 4.1 %collective-permute-start.26 = (bf16[128,256]{1,0:T(8,128)(2,1)S(1)}, bf16[128,256]{1,0:T(8,128)(2,1)S(1)}, u32[]{:S(2)}, u32[]{:S(2)}) collective-permute-start(bf16[128,256]{1,0:T(8,128)(2,1)S(1)} %constant_dynamic-update-slice_fusion.kv0), channel_id=1, source_target_pairs={{0,4},{4,8},{8,12},{12,16},{16,20},{20,24},{24,28},{28,32},{32,36}... | collective-permute-start | bytes 196616 | tf_op jit(solution)/shard_map/ppermute | solution.py:22
  245.9 20.0 %collective-permute-done.24.kv3 = bf16[128,256]{1,0:T(8,128)(2,1)S(1)} collective-permute-done((bf16[128,256]{1,0:T(8,128)(2,1)S(1)}, bf16[128,256]{1,0:T(8,128)(2,1)S(1)}, u32[]{:S(2)}, u32[]{:S(2)}) %collective-permute-start.24) | collective-permute-done | bytes 65568 | tf_op jit(solution)/shard_map/ppermute | solution.py:22
  267.8 7.3 %shard_map.193 = (bf16[128,1024]{1,0:T(8,128)(2,1)}, f32[128,256]{1,0:T(8,128)}, f32[128,256]{1,0:T(8,128)}, f32[128,256]{1,0:T(8,128)}, f32[128,256]{1,0:T(8,128)}) custom-call(s32[1]{0:T(128)} %bitcast.head, bf16[128,1024]{1,0:T(8,128)(2,1)} %query.1, bf16[128,1024]{1,0:T(8,128)(2,1)} %out_ref.1, bf16[128,1024]{1,0:T(8,128)(2,1)} %grad.1, ...), custom_call_target="tpu_custom_call" | custom-call | tf_op jit(solution)/shard_map/pallas_call | solution.py:59
  281.6 4.1 %collective-permute-start.29 = (f32[128,256]{1,0:T(8,128)}, f32[128,256]{1,0:T(8,128)S(1)}, u32[]{:S(2)}, u32[]{:S(2)}) collective-permute-start(f32[128,256]{1,0:T(8,128)} %get-tuple-element.54), channel_id=1, source_target_pairs={{12,0},{16,4},{20,8},{24,12},{28,16},{32,20},{36,24},{40,28},{44,3... | collective-permute-start | bytes 393224 | tf_op jit(solution)/shard_map/ppermute | solution.py:22
  295.4 7.0 %shard_map.191 = (bf16[2,192,2048]{2,1,0:T(8,128)(2,1)}, bf16[2,192,2048]{2,1,0:T(8,128)(2,1)}) custom-call(s32[1]{0:T(128)} %bitcast.head, bf16[640,512]{1,0:T(8,128)(2,1)} %get-tuple-element.36.refs_0_, bf16[640,512]{1,0:T(8,128)(2,1)} %get-tuple-element.37.refs_1_, bf16[640,512]{1,0:T(8,128)(2,1)} %copy-done.2, bf16[640,512]{1,0:T(8,128)(2,1)} %copy-done.4, ...), custom_call_target="tpu_custom_call" | custom-call | tf_op jit(solution)/shard_map/pallas_call | solution.py:59
  302.4 5.2 %shard_map.192 = bf16[2,192,2048]{2,1,0:T(8,128)(2,1)} custom-call(s32[1]{0:T(128)} %bitcast.head, bf16[640,512]{1,0:T(8,128)(2,1)} %get-tuple-element.33.refs_0_, bf16[640,512]{1,0:T(8,128)(2,1)} %get-tuple-element.34.refs_1_, bf16[640,512]{1,0:T(8,128)(2,1)} %copy-done.7, bf16[640,512]{1,0:T(8,128)(2,1)} %copy-done.9, bf16[640,512]{1,0:T(8,128)(2,1)} %copy-done.10, ...), custom_call_target="tpu_custom_call" | custom-call | tf_op jit(solution)/shard_map/pallas_call | solution.py:59
  (136 shorter events, 81.4 us)
Async XLA Ops:
  4.5 44.5 %all-to-all-start.1 = ((bf16[64,40,256]{2,1,0:T(8,128)(2,1)}), bf16[64,40,256]{2,1,0:T(8,128)(2,1)S(1)}, u32[]{:S(2)}, u32[]{:S(2)}) async-start(bf16[64,40,256]{2,1,0:T(8,128)(2,1)} %bitcast.19), calls=%async_computation.1 | async-start | bytes 2621440 | tf_op jit(solution)/shard_map/all_to_all | solution.py:256
  50.0 40.3 %all-to-all-start = ((bf16[64,40,256]{2,1,0:T(8,128)(2,1)}), bf16[64,40,256]{2,1,0:T(8,128)(2,1)S(1)}, u32[]{:S(2)}, u32[]{:S(2)}) async-start(bf16[64,40,256]{2,1,0:T(8,128)(2,1)} %bitcast.16), calls=%async_computation | async-start | bytes 2621440 | tf_op jit(solution)/shard_map/all_to_all | solution.py:256
  60.6 35.4 %collective-permute-start.6 = (bf16[640,512]{1,0:T(8,128)(2,1)}, bf16[640,512]{1,0:T(8,128)(2,1)S(1)}, u32[]{:S(2)}, u32[]{:S(2)}) collective-permute-start(bf16[640,512]{1,0:T(8,128)(2,1)} %get-tuple-element.36.refs_0_), channel_id=1, source_target_pairs={{0,1},{1,2},{2,3},{3,0},{4,5},{5,6},{6,7},{7,4},{8,9},{9,10},{10,1... | collective-permute-start | bytes 1966088 | tf_op jit(solution)/shard_map/ppermute | solution.py:27
  62.1 35.6 %collective-permute-start.9 = (bf16[640,512]{1,0:T(8,128)(2,1)}, bf16[640,512]{1,0:T(8,128)(2,1)S(1)}, u32[]{:S(2)}, u32[]{:S(2)}) collective-permute-start(bf16[640,512]{1,0:T(8,128)(2,1)} %get-tuple-element.37.refs_1_), channel_id=1, source_target_pairs={{0,3},{1,0},{2,1},{3,2},{4,7},{5,4},{6,5},{7,6},{8,11},{9,8},{10,9... | collective-permute-start | bytes 1966088 | tf_op jit(solution)/shard_map/ppermute | solution.py:27
  63.8 34.2 %collective-permute-start.7 = (bf16[640,512]{1,0:T(8,128)(2,1)}, bf16[640,512]{1,0:T(8,128)(2,1)S(1)}, u32[]{:S(2)}, u32[]{:S(2)}) collective-permute-start(bf16[640,512]{1,0:T(8,128)(2,1)} %get-tuple-element.37.refs_1_), channel_id=1, source_target_pairs={{0,1},{1,2},{2,3},{3,0},{4,5},{5,6},{6,7},{7,4},{8,9},{9,10},{10,1... | collective-permute-start | bytes 1966088 | tf_op jit(solution)/shard_map/ppermute | solution.py:27
  64.1 36.9 %collective-permute-start.8 = (bf16[640,512]{1,0:T(8,128)(2,1)}, bf16[640,512]{1,0:T(8,128)(2,1)}, u32[]{:S(2)}, u32[]{:S(2)}) collective-permute-start(bf16[640,512]{1,0:T(8,128)(2,1)} %get-tuple-element.36.refs_0_), channel_id=1, source_target_pairs={{0,3},{1,0},{2,1},{3,2},{4,7},{5,4},{6,5},{7,6},{8,11},{9,8},{10,9... | collective-permute-start | bytes 1966088 | tf_op jit(solution)/shard_map/ppermute | solution.py:27
  97.7 29.8 %collective-permute-start.4 = (bf16[640,512]{1,0:T(8,128)(2,1)}, bf16[640,512]{1,0:T(8,128)(2,1)S(1)}, u32[]{:S(2)}, u32[]{:S(2)}) collective-permute-start(bf16[640,512]{1,0:T(8,128)(2,1)} %get-tuple-element.34.refs_1_), channel_id=1, source_target_pairs={{0,1},{1,2},{2,3},{3,0},{4,5},{5,6},{6,7},{7,4},{8,9},{9,10},{10,1... | collective-permute-start | bytes 1966088 | tf_op jit(solution)/shard_map/ppermute | solution.py:27
  98.0 34.7 %collective-permute-start.5 = (bf16[640,512]{1,0:T(8,128)(2,1)}, bf16[640,512]{1,0:T(8,128)(2,1)S(1)}, u32[]{:S(2)}, u32[]{:S(2)}) collective-permute-start(bf16[640,512]{1,0:T(8,128)(2,1)} %get-tuple-element.33.refs_0_), channel_id=1, source_target_pairs={{0,3},{1,0},{2,1},{3,2},{4,7},{5,4},{6,5},{7,6},{8,11},{9,8},{10,9... | collective-permute-start | bytes 1966088 | tf_op jit(solution)/shard_map/ppermute | solution.py:27
  101.0 40.6 %collective-permute-start.10 = (bf16[640,512]{1,0:T(8,128)(2,1)S(1)}, bf16[640,512]{1,0:T(8,128)(2,1)S(1)}, u32[]{:S(2)}, u32[]{:S(2)}) collective-permute-start(bf16[640,512]{1,0:T(8,128)(2,1)S(1)} %collective-permute-done.6.refs_2_), channel_id=1, source_target_pairs={{0,1},{1,2},{2,3},{3,0},{4,5},{5,6},{6,7},{7,4},{8,9},{9,10},{10,1... | collective-permute-start | bytes 1966088 | tf_op jit(solution)/shard_map/ppermute | solution.py:27
  113.5 34.3 %collective-permute-start.11 = (bf16[640,512]{1,0:T(8,128)(2,1)S(1)}, bf16[640,512]{1,0:T(8,128)(2,1)S(1)}, u32[]{:S(2)}, u32[]{:S(2)}) collective-permute-start(bf16[640,512]{1,0:T(8,128)(2,1)S(1)} %collective-permute-done.9.refs_5_), channel_id=1, source_target_pairs={{0,3},{1,0},{2,1},{3,2},{4,7},{5,4},{6,5},{7,6},{8,11},{9,8},{10,9... | collective-permute-start | bytes 1966088 | tf_op jit(solution)/shard_map/ppermute | solution.py:27
  115.1 41.7 %collective-permute-start.1 = (bf16[640,512]{1,0:T(8,128)(2,1)S(1)}, bf16[640,512]{1,0:T(8,128)(2,1)S(1)}, u32[]{:S(2)}, u32[]{:S(2)}) collective-permute-start(bf16[640,512]{1,0:T(8,128)(2,1)S(1)} %collective-permute-done.refs_2_), channel_id=1, source_target_pairs={{0,1},{1,2},{2,3},{3,0},{4,5},{5,6},{6,7},{7,4},{8,9},{9,10},{10,1... | collective-permute-start | bytes 1966088 | tf_op jit(solution)/shard_map/ppermute | solution.py:27
  127.5 29.2 %collective-permute-start.3 = (bf16[640,512]{1,0:T(8,128)(2,1)S(1)}, bf16[640,512]{1,0:T(8,128)(2,1)S(1)}, u32[]{:S(2)}, u32[]{:S(2)}) collective-permute-start(bf16[640,512]{1,0:T(8,128)(2,1)S(1)} %collective-permute-done.2.refs_5_), channel_id=1, source_target_pairs={{0,3},{1,0},{2,1},{3,2},{4,7},{5,4},{6,5},{7,6},{8,11},{9,8},{10,9... | collective-permute-start | bytes 1966088 | tf_op jit(solution)/shard_map/ppermute | solution.py:27
  132.7 39.8 %collective-permute-start.16 = (bf16[2,384,512]{2,1,0:T(8,128)(2,1)}, bf16[2,384,512]{2,1,0:T(8,128)(2,1)S(1)}, u32[]{:S(2)}, u32[]{:S(2)}) collective-permute-start(bf16[2,384,512]{2,1,0:T(8,128)(2,1)} %get-tuple-element.43), channel_id=1, source_target_pairs={{0,1},{1,2},{2,3},{3,0},{4,5},{5,6},{6,7},{7,4},{8,9},{9,10},{10,1... | collective-permute-start | bytes 2359304 | tf_op jit(solution)/shard_map/ppermute | solution.py:27
  141.6 31.2 %collective-permute-start.17 = (bf16[2,384,512]{2,1,0:T(8,128)(2,1)}, bf16[2,384,512]{2,1,0:T(8,128)(2,1)S(1)}, u32[]{:S(2)}, u32[]{:S(2)}) collective-permute-start(bf16[2,384,512]{2,1,0:T(8,128)(2,1)} %get-tuple-element.44), channel_id=1, source_target_pairs={{0,3},{1,0},{2,1},{3,2},{4,7},{5,4},{6,5},{7,6},{8,11},{9,8},{10,9... | collective-permute-start | bytes 2359304 | tf_op jit(solution)/shard_map/ppermute | solution.py:27
  162.5 36.7 %collective-permute-start.15 = (bf16[640,384]{1,0:T(8,128)(2,1)}, bf16[640,384]{1,0:T(8,128)(2,1)S(1)}, u32[]{:S(2)}, u32[]{:S(2)}) collective-permute-start(bf16[640,384]{1,0:T(8,128)(2,1)} %get-tuple-element.41.refs_1_.refs_9_), channel_id=1, source_target_pairs={{0,3},{1,0},{2,1},{3,2},{4,7},{5,4},{6,5},{7,6},{8,11},{9,8},{10,9... | collective-permute-start | bytes 1474568 | tf_op jit(solution)/shard_map/ppermute | solution.py:27
  165.3 52.4 %collective-permute-start.20 = (bf16[2,384,512]{2,1,0:T(8,128)(2,1)S(1)}, bf16[2,384,512]{2,1,0:T(8,128)(2,1)S(1)}, u32[]{:S(2)}, u32[]{:S(2)}) collective-permute-start(bf16[2,384,512]{2,1,0:T(8,128)(2,1)S(1)} %copy-done.34), channel_id=1, source_target_pairs={{0,2},{1,3},{2,0},{3,1},{4,6},{5,7},{6,4},{7,5},{8,10},{9,11},{10,... | collective-permute-start | bytes 2359304 | tf_op jit(solution)/shard_map/ppermute | solution.py:27
  172.5 37.9 %collective-permute-start.13 = (bf16[640,384]{1,0:T(8,128)(2,1)}, bf16[640,384]{1,0:T(8,128)(2,1)S(1)}, u32[]{:S(2)}, u32[]{:S(2)}) collective-permute-start(bf16[640,384]{1,0:T(8,128)(2,1)} %get-tuple-element.41.refs_1_.refs_9_), channel_id=1, source_target_pairs={{0,1},{1,2},{2,3},{3,0},{4,5},{5,6},{6,7},{7,4},{8,9},{9,10},{10,1... | collective-permute-start | bytes 1474568 | tf_op jit(solution)/shard_map/ppermute | solution.py:27
  172.8 38.0 %collective-permute-start.14 = (bf16[640,384]{1,0:T(8,128)(2,1)}, bf16[640,384]{1,0:T(8,128)(2,1)S(1)}, u32[]{:S(2)}, u32[]{:S(2)}) collective-permute-start(bf16[640,384]{1,0:T(8,128)(2,1)} %get-tuple-element.40.refs_0_.refs_8_), channel_id=1, source_target_pairs={{0,3},{1,0},{2,1},{3,2},{4,7},{5,4},{6,5},{7,6},{8,11},{9,8},{10,9... | collective-permute-start | bytes 1474568 | tf_op jit(solution)/shard_map/ppermute | solution.py:27
  183.1 37.2 %collective-permute-start.18 = (bf16[640,384]{1,0:T(8,128)(2,1)S(1)}, bf16[640,384]{1,0:T(8,128)(2,1)S(1)}, u32[]{:S(2)}, u32[]{:S(2)}) collective-permute-start(bf16[640,384]{1,0:T(8,128)(2,1)S(1)} %collective-permute-done.12.refs_2_), channel_id=1, source_target_pairs={{0,1},{1,2},{2,3},{3,0},{4,5},{5,6},{6,7},{7,4},{8,9},{9,10},{10,1... | collective-permute-start | bytes 1474568 | tf_op jit(solution)/shard_map/ppermute | solution.py:27
  199.3 21.2 %collective-permute-start.19 = (bf16[640,384]{1,0:T(8,128)(2,1)S(1)}, bf16[640,384]{1,0:T(8,128)(2,1)S(1)}, u32[]{:S(2)}, u32[]{:S(2)}) collective-permute-start(bf16[640,384]{1,0:T(8,128)(2,1)S(1)} %collective-permute-done.15.refs_5_), channel_id=1, source_target_pairs={{0,3},{1,0},{2,1},{3,2},{4,7},{5,4},{6,5},{7,6},{8,11},{9,8},{10,9... | collective-permute-start | bytes 1474568 | tf_op jit(solution)/shard_map/ppermute | solution.py:27
  226.4 63.5 %all-to-all-start.2 = ((bf16[64,40,256]{2,1,0:T(8,128)(2,1)}), bf16[64,40,256]{2,1,0:T(8,128)(2,1)S(1)}, u32[]{:S(2)}, u32[]{:S(2)}) async-start(bf16[64,40,256]{2,1,0:T(8,128)(2,1)} %bitcast.18), calls=%async_computation.2 | async-start | bytes 2621440 | tf_op jit(solution)/shard_map/all_to_all | solution.py:256
  233.6 32.3 %collective-permute-start.24 = (bf16[128,256]{1,0:T(8,128)(2,1)S(1)}, bf16[128,256]{1,0:T(8,128)(2,1)S(1)}, u32[]{:S(2)}, u32[]{:S(2)}) collective-permute-start(bf16[128,256]{1,0:T(8,128)(2,1)S(1)} %constant_dynamic-update-slice_fusion.kv0), channel_id=1, source_target_pairs={{0,12},{4,16},{8,20},{12,24},{16,28},{20,32},{24,36},{28,40},{32,4... | collective-permute-start | bytes 196616 | tf_op jit(solution)/shard_map/ppermute | solution.py:22
  236.9 30.2 %collective-permute-start.25 = (bf16[128,256]{1,0:T(8,128)(2,1)S(1)}, bf16[128,256]{1,0:T(8,128)(2,1)S(1)}, u32[]{:S(2)}, u32[]{:S(2)}) collective-permute-start(bf16[128,256]{1,0:T(8,128)(2,1)S(1)} %constant_dynamic-update-slice_fusion.kv0), channel_id=1, source_target_pairs={{0,8},{4,12},{8,16},{12,20},{16,24},{20,28},{24,32},{28,36},{32,40... | collective-permute-start | bytes 196616 | tf_op jit(solution)/shard_map/ppermute | solution.py:22
  240.3 26.9 %collective-permute-start.26 = (bf16[128,256]{1,0:T(8,128)(2,1)S(1)}, bf16[128,256]{1,0:T(8,128)(2,1)S(1)}, u32[]{:S(2)}, u32[]{:S(2)}) collective-permute-start(bf16[128,256]{1,0:T(8,128)(2,1)S(1)} %constant_dynamic-update-slice_fusion.kv0), channel_id=1, source_target_pairs={{0,4},{4,8},{8,12},{12,16},{16,20},{20,24},{24,28},{28,32},{32,36}... | collective-permute-start | bytes 196616 | tf_op jit(solution)/shard_map/ppermute | solution.py:22
  (44 other events, 568.9 us)
